TPU v7x, 32 devices: a whole 2x2x4 slice. The times are simulated.
32 devices in a mesh: dp: 16 (over z, y, core), mp: 2 (over x).
Axes of the slice: x: 2, y: 2, z: 4, core: 2. Of those that a mesh axis runs over, the one named last changes fastest.
Arguments:
- tokens: bfloat16 [32768, 1024], P(('dp', 'mp')), may hold values from -6 to 6
- w_qkv: bfloat16 [1024, 3, 1024], P('dp', None, 'mp'), may hold values from -0.1875 to 0.1875
- w_out: bfloat16 [1024, 1024], P(('mp', 'dp')), may hold values from -0.1875 to 0.1875
- w_in: bfloat16 [1024, 4096], P('dp', 'mp'), may hold values from -0.1875 to 0.1875
- w_back: bfloat16 [4096, 1024], P(('mp', 'dp')), may hold values from -0.28125 to 0.28125
- gain_attn: bfloat16 [1024], P('dp'), may hold values from 0.25 to 1.75
- gain_post: bfloat16 [1024], P('dp'), may hold values from 0.25 to 1.75
- gain_ffn: bfloat16 [1024], P('dp'), may hold values from 0.25 to 1.75
- gain_mid: bfloat16 [4096], P(('mp', 'dp')), may hold values from 0.25 to 1.75
- head_scale: bfloat16 [16], P('mp'), may hold values from 0.25 to 1.75
- cotangent: bfloat16 [32768, 1024], P(('dp', 'mp')), may hold values from -6 to 6
Outputs:
- output: bfloat16 [32768, 1024], P(('dp', 'mp'))
- grad_tokens: bfloat16 [32768, 1024], P(('dp', 'mp'))
- grad_w_qkv: float32 [1024, 3, 1024], P('dp', None, 'mp')
- grad_w_out: float32 [1024, 1024], P(('mp', 'dp'))
- grad_w_in: float32 [1024, 4096], P('dp', 'mp')
- grad_w_back: float32 [4096, 1024], P(('mp', 'dp'))
- grad_gain_attn: float32 [1024], P(('dp', 'mp'))
- grad_gain_post: float32 [1024], P(('dp', 'mp'))
- grad_gain_ffn: float32 [1024], P(('dp', 'mp'))
- grad_gain_mid: float32 [4096], P(('mp', 'dp'))
- grad_head_scale: float32 [16], P('mp')
All inputs are finite; a program needn't handle non-finite values.
Results may differ from a plain program's by a relative error of at most 0.02.
Values may be sent and summed in bfloat16 or wider, within the bound.
No kernel may reach another device: no remote copies, remote signals or barrier semaphores. Data moves between devices by JAX's collectives and lax.ppermute only.
A program may use at most 256 MiB of HBM per device.

v0:
```python
import jax
import jax.numpy as jnp
from jax import lax
from jax.sharding import PartitionSpec as P

D = 1024
HD = 64
FF = 4096
BLOCK = 256
QBLOCK = 512


NORM_EPS = 1e-05
NEG_FILL = -1e30


def normalize(row_values):
    row_mean = jnp.mean(row_values, axis=-1, keepdims=True)
    centred = row_values - row_mean
    spread = jnp.mean(centred * centred, axis=-1, keepdims=True)
    inverse = lax.rsqrt(spread + NORM_EPS)
    return (centred * inverse, inverse)


def norm_back(gradient, normed, inverse):
    return inverse * (
        gradient
        - jnp.mean(gradient, axis=-1, keepdims=True)
        - normed * jnp.mean(gradient * normed, axis=-1, keepdims=True)
    )


def block_scores(query_rows, key_rows, offset):
    row_count = query_rows.shape[0]
    total_rows = key_rows.shape[0]
    head_count = query_rows.shape[1] // HD
    query_heads = query_rows.reshape(row_count, head_count, HD)
    key_heads = key_rows.reshape(total_rows, head_count, HD)
    raw_scores = jnp.einsum(
        "qhd,khd->hqk", query_heads, key_heads, preferred_element_type=jnp.float32
    ) * HD ** (-0.5)
    query_pos = offset + jnp.arange(row_count, dtype=jnp.int32)
    key_pos = jnp.arange(total_rows, dtype=jnp.int32)
    allowed = key_pos[None, :] // BLOCK <= query_pos[:, None] // BLOCK
    return jnp.where(allowed[None], raw_scores, NEG_FILL)


def attend(queries, key_rows, value_rows):
    total_rows = queries.shape[0]
    feat_width = queries.shape[1]
    head_count = feat_width // HD
    value_heads = value_rows.reshape(total_rows, head_count, HD)

    def one_block(block_index):
        offset = block_index * QBLOCK
        query_rows = lax.dynamic_slice_in_dim(queries, offset, QBLOCK, 0)
        scores = block_scores(query_rows, key_rows, offset)
        row_top = jnp.max(scores, axis=-1, keepdims=True)
        exp_scores = jnp.exp(scores - row_top)
        row_total = jnp.sum(exp_scores, axis=-1, keepdims=True)
        probabilities = (exp_scores / row_total).astype(jnp.bfloat16)
        block_out = jnp.einsum(
            "hqk,khd->qhd", probabilities, value_heads, preferred_element_type=jnp.float32
        )
        return (block_out.reshape(QBLOCK, feat_width), (row_top + jnp.log(row_total))[..., 0])

    outputs, log_sums = lax.map(one_block, jnp.arange(total_rows // QBLOCK, dtype=jnp.int32))
    return (outputs.reshape(total_rows, feat_width), log_sums)


def attend_back(queries, key_rows, value_rows, log_sums, grad_out):
    total_rows = queries.shape[0]
    feat_width = queries.shape[1]
    head_count = feat_width // HD
    key_heads = key_rows.reshape(total_rows, head_count, HD)
    value_heads = value_rows.reshape(total_rows, head_count, HD)
    factor = HD ** (-0.5)

    def one_block(carried, block_index):
        grad_keys, grad_values = carried
        offset = block_index * QBLOCK
        query_rows = lax.dynamic_slice_in_dim(queries, offset, QBLOCK, 0)
        grad_rows = lax.dynamic_slice_in_dim(grad_out, offset, QBLOCK, 0).reshape(
            QBLOCK, head_count, HD
        )
        scores = block_scores(query_rows, key_rows, offset)
        probabilities = jnp.exp(scores - log_sums[block_index][..., None])
        grad_values = grad_values + jnp.einsum(
            "hqk,qhd->khd",
            probabilities.astype(jnp.bfloat16),
            grad_rows,
            preferred_element_type=jnp.float32,
        ).reshape(total_rows, feat_width)
        grad_probs = jnp.einsum(
            "qhd,khd->hqk", grad_rows, value_heads, preferred_element_type=jnp.float32
        )
        inner_sum = jnp.sum(probabilities * grad_probs, axis=-1, keepdims=True)
        grad_scores = (probabilities * (grad_probs - inner_sum)).astype(jnp.bfloat16)
        query_heads = query_rows.reshape(QBLOCK, head_count, HD)
        grad_query = (
            jnp.einsum("hqk,khd->qhd", grad_scores, key_heads, preferred_element_type=jnp.float32)
            * factor
        )
        grad_keys = (
            grad_keys
            + jnp.einsum(
                "hqk,qhd->khd", grad_scores, query_heads, preferred_element_type=jnp.float32
            ).reshape(total_rows, feat_width)
            * factor
        )
        return ((grad_keys, grad_values), grad_query.reshape(QBLOCK, feat_width))

    empty = jnp.zeros((total_rows, feat_width), jnp.float32)
    (grad_keys, grad_values), grad_queries = lax.scan(
        one_block, (empty, empty), jnp.arange(total_rows // QBLOCK, dtype=jnp.int32)
    )
    return (grad_queries.reshape(total_rows, feat_width), grad_keys, grad_values)


def body(
    tokens,
    w_qkv,
    w_out,
    w_in,
    w_back,
    gain_attn,
    gain_post,
    gain_ffn,
    gain_mid,
    head_scale,
    cotangent,
):
    inputs = tokens.astype(jnp.float32)

    def fetch_weights():
        return (
            lax.all_gather(w_qkv, "dp", axis=0, tiled=True),
            lax.all_gather(w_out, "dp", axis=0, tiled=True),
            lax.all_gather(w_in, "dp", axis=0, tiled=True),
            lax.all_gather(w_back, "dp", axis=0, tiled=True),
            lax.all_gather(gain_attn, "dp", axis=0, tiled=True),
            lax.all_gather(gain_post, "dp", axis=0, tiled=True),
            lax.all_gather(gain_ffn, "dp", axis=0, tiled=True),
            lax.all_gather(gain_mid, "dp", axis=0, tiled=True),
        )

    w_proj, w_mix, w_up, w_down, g_attn, g_post, g_ffn, g_mid = fetch_weights()
    feat_width = w_proj.shape[2]
    head_count = feat_width // HD
    columns = jnp.repeat(head_scale.astype(jnp.float32), HD)
    norm_attn, inv_attn = normalize(inputs)
    entry_attn = (norm_attn * g_attn).astype(jnp.bfloat16)
    gathered = lax.all_gather(entry_attn, "mp", axis=0, tiled=True)
    projected = jnp.dot(
        gathered, w_proj.reshape(D, 3 * feat_width), preferred_element_type=jnp.float32
    ).astype(jnp.bfloat16)
    queries = projected[:, :feat_width]
    key_rows = projected[:, feat_width : 2 * feat_width]
    value_rows = projected[:, 2 * feat_width :]
    attended, log_sums = attend(queries, key_rows, value_rows)
    scaled = (attended * columns).astype(jnp.bfloat16)
    mixed_sum = lax.psum_scatter(
        jnp.dot(scaled, w_mix, preferred_element_type=jnp.float32).astype(jnp.bfloat16),
        "mp",
        scatter_dimension=0,
        tiled=True,
    ).astype(jnp.float32)
    norm_post, inv_post = normalize(mixed_sum)
    middle = inputs + norm_post * g_post
    norm_ffn, inv_ffn = normalize(middle)
    entry_ffn = (norm_ffn * g_ffn).astype(jnp.bfloat16)
    gathered_ffn = lax.all_gather(entry_ffn, "mp", axis=0, tiled=True)
    upper_pre = jnp.dot(gathered_ffn, w_up, preferred_element_type=jnp.float32)
    active = jax.nn.gelu(upper_pre, approximate=False)
    row_sums = lax.psum((jnp.sum(active, axis=-1), jnp.sum(active * active, axis=-1)), "mp")
    row_mean = row_sums[0][:, None] / FF
    inv_mid = lax.rsqrt(row_sums[1][:, None] / FF - row_mean * row_mean + NORM_EPS)
    norm_mid = (active - row_mean) * inv_mid
    fed_down = (norm_mid * g_mid).astype(jnp.bfloat16)
    lowered = lax.psum_scatter(
        jnp.dot(fed_down, w_down, preferred_element_type=jnp.float32).astype(jnp.bfloat16),
        "mp",
        scatter_dimension=0,
        tiled=True,
    ).astype(jnp.float32)
    output = (middle + lowered).astype(jnp.bfloat16)
    w_proj, w_mix, w_up, w_down, g_attn, g_post, g_ffn, g_mid = fetch_weights()
    grad_top = cotangent.astype(jnp.float32)
    grad_full = lax.all_gather(cotangent, "mp", axis=0, tiled=True)
    grad_down = jnp.einsum("sf,sd->fd", fed_down, grad_full, preferred_element_type=jnp.float32)
    grad_fed = jnp.dot(grad_full, w_down.T, preferred_element_type=jnp.float32)
    grad_gmid = jnp.sum(grad_fed * norm_mid, axis=0)
    scaled_mid = grad_fed * g_mid
    moments = lax.psum(
        (jnp.sum(scaled_mid, axis=-1), jnp.sum(scaled_mid * norm_mid, axis=-1)), "mp"
    )
    grad_active = inv_mid * (
        scaled_mid - moments[0][:, None] / FF - norm_mid * moments[1][:, None] / FF
    )
    normal_cdf = 0.5 * (1.0 + lax.erf(upper_pre * 0.7071067811865476))
    density = jnp.exp(-0.5 * upper_pre * upper_pre) * 0.3989422804014327
    grad_upper = (grad_active * (normal_cdf + upper_pre * density)).astype(jnp.bfloat16)
    grad_up = jnp.einsum("sd,sf->df", gathered_ffn, grad_upper, preferred_element_type=jnp.float32)
    grad_entry_ffn = lax.psum_scatter(
        jnp.dot(grad_upper, w_up.T, preferred_element_type=jnp.float32).astype(jnp.bfloat16),
        "mp",
        scatter_dimension=0,
        tiled=True,
    ).astype(jnp.float32)
    grad_gffn = jnp.sum(grad_entry_ffn * norm_ffn, axis=0)
    grad_middle = grad_top + norm_back(grad_entry_ffn * g_ffn, norm_ffn, inv_ffn)
    grad_gpost = jnp.sum(grad_middle * norm_post, axis=0)
    grad_mixed = norm_back(grad_middle * g_post, norm_post, inv_post).astype(jnp.bfloat16)
    grad_mfull = lax.all_gather(grad_mixed, "mp", axis=0, tiled=True)
    grad_mix = jnp.einsum("sw,sd->wd", scaled, grad_mfull, preferred_element_type=jnp.float32)
    grad_scaled = jnp.dot(grad_mfull, w_mix.T, preferred_element_type=jnp.float32)
    grad_head_part = jnp.sum((grad_scaled * attended).reshape(-1, head_count, HD), axis=(0, 2))
    grad_attended = (grad_scaled * columns).astype(jnp.bfloat16)
    grad_queries, grad_keys, grad_values = attend_back(
        queries, key_rows, value_rows, log_sums, grad_attended
    )
    grad_proj = jnp.concatenate(
        [
            grad_queries.astype(jnp.bfloat16),
            grad_keys.astype(jnp.bfloat16),
            grad_values.astype(jnp.bfloat16),
        ],
        axis=1,
    )
    grad_wproj = jnp.einsum(
        "sd,se->de", gathered, grad_proj, preferred_element_type=jnp.float32
    ).reshape(D, 3, feat_width)
    proj_matrix = w_proj.reshape(D, 3 * feat_width)
    grad_entry_attn = lax.psum_scatter(
        jnp.dot(grad_proj, proj_matrix.T, preferred_element_type=jnp.float32).astype(jnp.bfloat16),
        "mp",
        scatter_dimension=0,
        tiled=True,
    ).astype(jnp.float32)
    grad_gattn = jnp.sum(grad_entry_attn * norm_attn, axis=0)
    grad_inputs = grad_middle + norm_back(grad_entry_attn * g_attn, norm_attn, inv_attn)
    shares = (
        lax.psum_scatter(
            grad_wproj.astype(jnp.bfloat16), "dp", scatter_dimension=0, tiled=True
        ).astype(jnp.float32),
        lax.psum_scatter(
            grad_mix.astype(jnp.bfloat16), "dp", scatter_dimension=0, tiled=True
        ).astype(jnp.float32),
        lax.psum_scatter(
            grad_up.astype(jnp.bfloat16), "dp", scatter_dimension=0, tiled=True
        ).astype(jnp.float32),
        lax.psum_scatter(
            grad_down.astype(jnp.bfloat16), "dp", scatter_dimension=0, tiled=True
        ).astype(jnp.float32),
        lax.psum_scatter(
            grad_gmid.astype(jnp.bfloat16), "dp", scatter_dimension=0, tiled=True
        ).astype(jnp.float32),
    )
    gain_shares = (
        lax.psum_scatter(grad_gattn, ("dp", "mp"), scatter_dimension=0, tiled=True),
        lax.psum_scatter(grad_gpost, ("dp", "mp"), scatter_dimension=0, tiled=True),
        lax.psum_scatter(grad_gffn, ("dp", "mp"), scatter_dimension=0, tiled=True),
    )
    grad_heads = lax.psum(grad_head_part, "dp")
    return (
        output,
        grad_inputs.astype(jnp.bfloat16),
        shares[0],
        shares[1],
        shares[2],
        shares[3],
        gain_shares[0],
        gain_shares[1],
        gain_shares[2],
        shares[4],
        grad_heads,
    )


def solution(mesh):
    return jax.shard_map(
        body,
        mesh=mesh,
        in_specs=(
            P(("dp", "mp"), None),
            P("dp", None, "mp"),
            P(("mp", "dp"), None),
            P("dp", "mp"),
            P(("mp", "dp"), None),
            P("dp"),
            P("dp"),
            P("dp"),
            P(("mp", "dp")),
            P("mp"),
            P(("dp", "mp"), None),
        ),
        out_specs=(
            P(("dp", "mp"), None),
            P(("dp", "mp"), None),
            P("dp", None, "mp"),
            P(("mp", "dp"), None),
            P("dp", "mp"),
            P(("mp", "dp"), None),
            P(("dp", "mp")),
            P(("dp", "mp")),
            P(("dp", "mp")),
            P(("mp", "dp")),
            P("mp"),
        ),
        check_vma=False,
    )
```

profile of v0, /device:TPU:0, one launch (start us, length us, event | category | flops | bytes accessed | tf_op | source)
XLA Modules:
  0.0 1646.8 jit_solution(12270819974073319281)
XLA Ops:
  12.5 36.8 %all-reduce.11 = (bf16[1024]{0:T(1024)(128)(2,1)}, bf16[1024]{0:T(1024)(128)(2,1)}, bf16[1024]{0:T(1024)(128)(2,1)S(1)}) all-reduce(bf16[1024]{0:T(1024)(128)(2,1)S(1)} %dynamic-update-slice.2, bf16[1024]{0:T(1024)(128)(2,1)S(1)} %dynamic-update-slice.1, bf16[1024]{0:T(1024)(128)(2,1)S(1)} %dynamic-update-slice), channel_id=1, replica_groups=mesh['dp'=16,'mp'=2] {'dp'}, use_global_device_ids=true, to_apply=%add.2 | all-reduce | flops 3072 | bytes 12288
  61.5 54.2 %all-gather.10.cloned.1.call-done = bf16[2048,1024]{1,0:T(8,128)(2,1)} async-done(((bf16[1024,1024]{1,0:T(8,128)(2,1)}), bf16[2048,1024]{1,0:T(8,128)(2,1)}) %all-gather.10.cloned.1.call-update) | async-done | bytes 4194320 | tf_op jit(solution)/shard_map/all_gather | solution.py:153
  115.7 9.3 convolution_convert_fusion
  128.0 203.2 %while.35 = (s32[]{:T(128)}, f32[4,512,512]{2,1,0:T(8,128)}, f32[4,8,512]{2,1,0:T(8,128)}, s32[4]{0:T(128)S(1)}, bf16[2048,512]{0,1:T(8,128)(2,1)}, /*index=5*/b...) while((s32[]{:T(128)}, f32[4,512,512]{2,1,0:T(8,128)}, ...), condition=%wide.region_5.6_spmd.clone, body=%wide.region_2.5_spmd.sunk.clone | while | flops 2249216000 | bytes 116019368 | solution.py:67
  131.0 13.9 fusion.151
  144.9 15.1 fusion.152
  160.0 15.7 fusion.153
  181.9 13.8 fusion.151
  195.7 15.0 fusion.152
  210.7 15.7 fusion.153
  232.6 13.8 fusion.151
  246.4 15.0 fusion.152
  261.4 15.7 fusion.153
  283.3 13.8 fusion.151
  297.2 15.0 fusion.152
  312.1 15.7 fusion.153
  343.0 53.8 %reduce-scatter.8.cloned.1.call-done = bf16[1024,1024]{1,0:T(8,128)(2,1)} async-done(((bf16[2048,1024]{1,0:T(8,128)(2,1)}), bf16[1024,1024]{1,0:T(8,128)(2,1)}) %reduce-scatter.8.cloned.1.call-update) | async-done | bytes 2097168 | tf_op jit(solution)/shard_map/reduce_scatter | solution.py:162
  410.2 21.4 %all-gather = bf16[16,1,128]{2,1,0:T(2,128)(2,1)S(1)} all-gather(bf16[1,1,128]{2,1,0:T(2,128)(2,1)S(1)} %bitcast.165), channel_id=1, replica_groups=mesh['dp'=16,'mp'=2] {'dp'}, dimensions={0}, use_global_device_ids=true | all-gather | bytes 4352 | tf_op jit(solution)/shard_map/all_gather | solution.py:144
  431.7 17.5 %all-gather.18.cloned.1.call-done = bf16[1024,2048]{1,0:T(8,128)(2,1)} async-done(((bf16[64,2048]{1,0:T(8,128)(2,1)}), bf16[1024,2048]{1,0:T(8,128)(2,1)}) %all-gather.18.cloned.1.call-update) | async-done | bytes 4194320 | tf_op jit(solution)/shard_map/all_gather | solution.py:139
  449.2 57.3 %all-gather.16.cloned.1.call-done = bf16[2048,1024]{1,0:T(8,128)(2,1)} async-done(((bf16[1024,1024]{1,0:T(8,128)(2,1)}), bf16[2048,1024]{1,0:T(8,128)(2,1)}) %all-gather.16.cloned.1.call-update) | async-done | bytes 4194320 | tf_op jit(solution)/shard_map/all_gather | solution.py:172
  506.5 49.7 %fusion.74 = (f32[2048]{0:T(1024)S(1)}, f32[2048]{0:T(1024)S(1)}, f32[2048,2048]{0,1:T(8,128)}, f32[2048,2048]{0,1:T(8,128)}) fusion(bf16[2048,1024]{1,0:T(8,128)(2,1)} %all-gather.16.cloned.1.call-done, bf16[1024,2048]{1,0:T(8,128)(2,1)} %all-gather.18.cloned.1.call-done), kind=kOutput, calls=%fused_computation.173 | convolution fusion | flops 8870948864 | bytes 41959424 | tf_op jit(solution)/shard_map/dot_general | solution.py:173
  565.1 52.6 %all-gather.20.cloned.1.call-done = bf16[2048,1024]{1,0:T(8,128)(2,1)} async-done(((bf16[128,1024]{1,0:T(8,128)(2,1)}), bf16[2048,1024]{1,0:T(8,128)(2,1)}) %all-gather.20.cloned.1.call-update) | async-done | bytes 4194320 | tf_op jit(solution)/shard_map/all_gather | solution.py:140
  617.7 19.2 %multiply_reduce_fusion.1 = (bf16[2048]{0:T(1024)(128)(2,1)}, f32[2048]{0:T(1024)S(1)}, f32[2048]{0:T(1024)S(1)}, f32[2048,2048]{0,1:T(8,128)}) fusion(f32[2048,2048]{0,1:T(8,128)} %get-tuple-element.473, f32[2048]{0:T(1024)S(1)} %get-tuple-element.487, f32[2048]{0:T(1024)S(1)} %get-tuple-element.486, f32[2048]{0:T(1024)S(1)} %bitcast.161, ...), kind=kOutput, calls=%fused_computation.68 | convolution fusion | flops 8623482880 | bytes 41988096 | tf_op jit(solution)/shard_map/dot_general | solution.py:191
  645.0 17.5 %fusion.26 = bf16[2048,2048]{0,1:T(8,128)(2,1)S(1)} fusion(f32[2048,2048]{0,1:T(8,128)} %get-tuple-element.490, f32[2048,2048]{0,1:T(8,128)} %get-tuple-element.491, f32[2048,2048]{0,1:T(8,128)} %get-tuple-element.473, f32[2048]{0:T(1024)S(1)} %get-tuple-element.465, f32[2048]{0:T(1024)S(1)} %broadcast_multiply_fusion, f32[2048]{0:T(1024)S(1)} %bitcast.162, ...), kind=kLoop, calls=%fused_computation.67 | loop fusion | flops 75497472 | bytes 58761216 | tf_op jit(solution)/shard_map/convert_element_type | solution.py:202
  665.7 10.5 convolution_convert_fusion.6
  676.3 16.6 %convolution_convert_fusion.7 = bf16[2048,1024]{1,0:T(8,128)(2,1)} fusion(bf16[2048,1024]{1,0:T(8,128)(2,1)} %all-gather.20.cloned.1.call-done, f32[2048,2048]{0,1:T(8,128)} %get-tuple-element.473, f32[2048]{0:T(1024)S(1)} %bitcast.163, f32[2048]{0:T(1024)S(1)} %get-tuple-element.487, f32[2048]{0:T(1024)S(1)} %get-tuple-element.486), kind=kOutput, calls=%fused_computation.150 | convolution fusion | flops 8608808960 | bytes 25190400 | tf_op jit(solution)/shard_map/dot_general | solution.py:181
  693.0 35.4 %reduce-scatter.12.cloned.1.call-done = bf16[1024,1024]{1,0:T(8,128)(2,1)} async-done(((bf16[2048,1024]{1,0:T(8,128)(2,1)}), bf16[1024,1024]{1,0:T(8,128)(2,1)}) %reduce-scatter.12.cloned.1.call-update) | async-done | bytes 2097168 | tf_op jit(solution)/shard_map/reduce_scatter | solution.py:204
  734.1 50.8 %reduce-scatter.10.cloned.1.call-done = bf16[1024,1024]{1,0:T(8,128)(2,1)} async-done(((bf16[2048,1024]{1,0:T(8,128)(2,1)}), bf16[1024,1024]{1,0:T(8,128)(2,1)}) %reduce-scatter.10.cloned.1.call-update) | async-done | bytes 2097168 | tf_op jit(solution)/shard_map/reduce_scatter | solution.py:180
  797.5 15.0 convolution_convert_fusion.3
  814.1 13.9 convolution_convert_fusion.4
  828.1 26.2 %all-gather.24.cloned.1.call-done = bf16[2048,1024]{1,0:T(8,128)(2,1)} async-done(((bf16[1024,1024]{1,0:T(8,128)(2,1)}), bf16[2048,1024]{1,0:T(8,128)(2,1)}) %all-gather.24.cloned.1.call-update) | async-done | bytes 4194320 | tf_op jit(solution)/shard_map/all_gather | solution.py:214
  862.6 471.3 %while.36 = (s32[]{:T(128)}, f32[2048,512]{0,1:T(8,128)}, f32[2048,512]{0,1:T(8,128)}, bf16[4,512,512]{2,1,0:T(8,128)(2,1)}, s32[4]{0:T(128)S(1)}, /*index=5*/bf...) while((s32[]{:T(128)}, f32[2048,512]{0,1:T(8,128)}, ...), condition=%wide.region_27.28_spmd.clone.clone, body=%wide.region_25.27_spmd.clone.sunk.clone | while | flops 5451042816 | bytes 379162976 | solution.py:114
  870.0 13.8 fusion.164
  883.8 25.4 %multiply_reduce_fusion.9 = (f32[8,512]{1,0:T(8,128)S(1)}, f32[8,512,2048]{2,1,0:T(8,128)}) fusion(f32[8,512,2048]{2,1,0:T(8,128)} %fusion.164, f32[8,512]{1,0:T(8,128)S(1)} %dynamic-slice_bitcast_fusion.3, bf16[512,8,64]{0,2,1:T(8,128)(2,1)S(1)} %bitcast.151, bf16[2048,8,64]{0,2,1:T(8,128)(2,1)S(1)} %get-tuple-element.727, ...), kind=kOutput, calls=%fused_computation.29.clone.1.clone | convolution fusion | flops 1115680768 | bytes 70811648 | tf_op jit(solution)/shard_map/while/body/eval_jaxpr/qhd,khd->hqk/dot_general | solution.py:39
  909.2 27.8 %multiply_convert_fusion.8 = bf16[8,512,2048]{2,1,0:T(8,128)(2,1)} fusion(f32[8,512,2048]{2,1,0:T(8,128)} %get-tuple-element.651, f32[8,512,2048]{2,1,0:T(8,128)} %fusion.164, f32[8,512]{1,0:T(8,128)S(1)} %get-tuple-element.652), kind=kLoop, calls=%fused_computation.28.clone.1.clone | loop fusion | flops 25165824 | bytes 83902464 | tf_op jit(solution)/shard_map/while/body/eval_jaxpr/convert_element_type | solution.py:98
  937.1 17.1 %fusion.165 = f32[8,64,2048]{2,1,0:T(8,128)} fusion(bf16[512,8,64]{0,2,1:T(8,128)(2,1)S(1)} %bitcast.149, f32[8,512,2048]{2,1,0:T(8,128)} %get-tuple-element.651), kind=kOutput, calls=%fused_computation.31.clone.1.clone | convolution fusion | flops 1082130432 | bytes 38273024 | tf_op jit(solution)/shard_map/while/body/eval_jaxpr/hqk,qhd->khd/dot_general | solution.py:88
  954.1 9.7 convolution_multiply_fusion.7
  970.3 9.8 bitcast_add_fusion.4
  988.3 13.3 fusion.164
  1001.6 25.5 %multiply_reduce_fusion.9 = (f32[8,512]{1,0:T(8,128)S(1)}, f32[8,512,2048]{2,1,0:T(8,128)}) fusion(f32[8,512,2048]{2,1,0:T(8,128)} %fusion.164, f32[8,512]{1,0:T(8,128)S(1)} %dynamic-slice_bitcast_fusion.3, bf16[512,8,64]{0,2,1:T(8,128)(2,1)S(1)} %bitcast.151, bf16[2048,8,64]{0,2,1:T(8,128)(2,1)S(1)} %get-tuple-element.727, ...), kind=kOutput, calls=%fused_computation.29.clone.1.clone | convolution fusion | flops 1115680768 | bytes 70811648 | tf_op jit(solution)/shard_map/while/body/eval_jaxpr/qhd,khd->hqk/dot_general | solution.py:39
  1027.1 27.4 %multiply_convert_fusion.8 = bf16[8,512,2048]{2,1,0:T(8,128)(2,1)} fusion(f32[8,512,2048]{2,1,0:T(8,128)} %get-tuple-element.651, f32[8,512,2048]{2,1,0:T(8,128)} %fusion.164, f32[8,512]{1,0:T(8,128)S(1)} %get-tuple-element.652), kind=kLoop, calls=%fused_computation.28.clone.1.clone | loop fusion | flops 25165824 | bytes 83902464 | tf_op jit(solution)/shard_map/while/body/eval_jaxpr/convert_element_type | solution.py:98
  1054.5 15.6 fusion.165
  1070.1 9.7 convolution_multiply_fusion.7
  1085.8 12.0 bitcast_add_fusion.4
  1106.0 13.1 fusion.164
  1119.1 25.4 %multiply_reduce_fusion.9 = (f32[8,512]{1,0:T(8,128)S(1)}, f32[8,512,2048]{2,1,0:T(8,128)}) fusion(f32[8,512,2048]{2,1,0:T(8,128)} %fusion.164, f32[8,512]{1,0:T(8,128)S(1)} %dynamic-slice_bitcast_fusion.3, bf16[512,8,64]{0,2,1:T(8,128)(2,1)S(1)} %bitcast.151, bf16[2048,8,64]{0,2,1:T(8,128)(2,1)S(1)} %get-tuple-element.727, ...), kind=kOutput, calls=%fused_computation.29.clone.1.clone | convolution fusion | flops 1115680768 | bytes 70811648 | tf_op jit(solution)/shard_map/while/body/eval_jaxpr/qhd,khd->hqk/dot_general | solution.py:39
  1144.5 27.4 %multiply_convert_fusion.8 = bf16[8,512,2048]{2,1,0:T(8,128)(2,1)} fusion(f32[8,512,2048]{2,1,0:T(8,128)} %get-tuple-element.651, f32[8,512,2048]{2,1,0:T(8,128)} %fusion.164, f32[8,512]{1,0:T(8,128)S(1)} %get-tuple-element.652), kind=kLoop, calls=%fused_computation.28.clone.1.clone | loop fusion | flops 25165824 | bytes 83902464 | tf_op jit(solution)/shard_map/while/body/eval_jaxpr/convert_element_type | solution.py:98
  1171.9 15.6 fusion.165
  1187.5 9.7 convolution_multiply_fusion.7
  1203.2 12.0 bitcast_add_fusion.4
  1223.4 13.1 fusion.164
  1236.5 25.4 %multiply_reduce_fusion.9 = (f32[8,512]{1,0:T(8,128)S(1)}, f32[8,512,2048]{2,1,0:T(8,128)}) fusion(f32[8,512,2048]{2,1,0:T(8,128)} %fusion.164, f32[8,512]{1,0:T(8,128)S(1)} %dynamic-slice_bitcast_fusion.3, bf16[512,8,64]{0,2,1:T(8,128)(2,1)S(1)} %bitcast.151, bf16[2048,8,64]{0,2,1:T(8,128)(2,1)S(1)} %get-tuple-element.727, ...), kind=kOutput, calls=%fused_computation.29.clone.1.clone | convolution fusion | flops 1115680768 | bytes 70811648 | tf_op jit(solution)/shard_map/while/body/eval_jaxpr/qhd,khd->hqk/dot_general | solution.py:39
  1261.9 27.4 %multiply_convert_fusion.8 = bf16[8,512,2048]{2,1,0:T(8,128)(2,1)} fusion(f32[8,512,2048]{2,1,0:T(8,128)} %get-tuple-element.651, f32[8,512,2048]{2,1,0:T(8,128)} %fusion.164, f32[8,512]{1,0:T(8,128)S(1)} %get-tuple-element.652), kind=kLoop, calls=%fused_computation.28.clone.1.clone | loop fusion | flops 25165824 | bytes 83902464 | tf_op jit(solution)/shard_map/while/body/eval_jaxpr/convert_element_type | solution.py:98
  1289.3 15.6 fusion.165
  1304.9 9.7 convolution_multiply_fusion.7
  1320.6 12.0 bitcast_add_fusion.4
  1342.6 11.8 convolution_convert_fusion.1
  1369.8 10.0 convolution_convert_fusion.2
  1381.3 33.7 %all-reduce.7 = bf16[2048]{0:T(1024)(128)(2,1)S(1)} all-reduce(bf16[2048]{0:T(1024)(128)(2,1)S(1)} %copy-done.38), channel_id=13, replica_groups=mesh['dp'=16,'mp'=2] {'dp'}, use_global_device_ids=true, to_apply=%region_42.43.clone | all-reduce | flops 2048 | bytes 8192
  1419.4 30.4 %psum.39 = f32[8]{0:T(128)} all-reduce(f32[8]{0:T(128)S(1)} %reduce_sum.244), channel_id=1, replica_groups=mesh['dp'=16,'mp'=2] {'dp'}, use_global_device_ids=true, to_apply=%region_45.46 | all-reduce | flops 8 | bytes 64 | tf_op jit(solution)/shard_map/psum | solution.py:264
  1449.8 25.0 %all-reduce.14.cloned.1.call-done = bf16[1024,3,512]{2,1,0:T(4,128)(2,1)} async-done(((bf16[1024,3,512]{2,1,0:T(4,128)(2,1)}), bf16[1024,3,512]{2,1,0:T(4,128)(2,1)}) %all-reduce.14.cloned.1.call-update) | async-done | bytes 3145744
  1476.6 58.4 %reduce-scatter.16.cloned.1.call-done = bf16[32,1024]{1,0:T(8,128)(2,1)} async-done(((bf16[512,1024]{1,0:T(8,128)(2,1)}), bf16[32,1024]{1,0:T(8,128)(2,1)}) %reduce-scatter.16.cloned.1.call-update) | async-done | bytes 65552 | tf_op jit(solution)/shard_map/reduce_scatter | solution.py:246
  1536.5 54.1 %reduce-scatter.14.cloned.1.call-done = bf16[1024,1024]{1,0:T(8,128)(2,1)} async-done(((bf16[2048,1024]{1,0:T(8,128)(2,1)}), bf16[1024,1024]{1,0:T(8,128)(2,1)}) %reduce-scatter.14.cloned.1.call-update) | async-done | bytes 2097168 | tf_op jit(solution)/shard_map/reduce_scatter | solution.py:234
  1594.2 39.5 %all-reduce.8 = (f32[1024]{0:T(1024)S(1)}, f32[1024]{0:T(1024)S(1)}, f32[1024]{0:T(1024)S(1)}) all-reduce(f32[1024]{0:T(1024)S(1)} %get-tuple-element.421, f32[1024]{0:T(1024)S(1)} %copy-done.34, f32[1024]{0:T(1024)S(1)} %copy-done.35), channel_id=10, replica_groups=mesh['dp'=16,'mp'=2] {'dp','mp'}, use_global_device_ids=true, to_apply=%region_36.37.clone | all-reduce | flops 3072 | bytes 24576
  (290 shorter events, 203.6 us)
Async XLA Ops:
  7.2 47.1 %copy-start.3 = (bf16[1024,1024]{1,0:T(8,128)(2,1)S(1)}, bf16[1024,1024]{1,0:T(8,128)(2,1)}, u32[]{:S(2)}) copy-start(bf16[1024,1024]{1,0:T(8,128)(2,1)} %param.15) | copy-start | bytes 6291460
  7.2 51.1 %all-gather.12.cloned.1.call-start = ((), (), s32[]{:S(2)}) async-start(), calls=%async_computation.8 | async-start | bytes 3342336 | tf_op jit(solution)/shard_map/all_gather | solution.py:137
  7.9 107.8 %all-gather.10.cloned.1.call-start = ((), (), s32[]{:S(2)}) async-start(), calls=%async_computation.7 | async-start | bytes 6291456 | tf_op jit(solution)/shard_map/all_gather | solution.py:153
  49.3 4.3 copy-start.26
  51.3 2.4 copy-start.22
  51.3 5.9 copy-start.42
  56.3 279.8 %all-gather.14.cloned.1.call-start = ((), (), s32[]{:S(2)}) async-start(), calls=%async_computation.9 | async-start | bytes 1114112 | tf_op jit(solution)/shard_map/all_gather | solution.py:138
  57.0 339.7 %reduce-scatter.8.cloned.1.call-start = ((), (), s32[]{:S(2)}) async-start(), calls=%async_computation.10 | async-start | bytes 6291456 | tf_op jit(solution)/shard_map/reduce_scatter | solution.py:162
  61.5 54.2 %copy-start.13 = (bf16[1024,3,512]{0,2,1:T(8,128)(2,1)}, bf16[1024,3,512]{0,2,1:T(8,128)(2,1)S(1)}, u32[]{:S(2)}) copy-start(bf16[1024,3,512]{0,2,1:T(8,128)(2,1)S(1)} %copy.42) | copy-start | bytes 9437188
  128.0 203.3 %copy-start.36 = (f32[512]{0:T(512)S(1)}, f32[512]{0:T(512)}, u32[]{:S(2)}) copy-start(f32[512]{0:T(512)} %mul.312) | copy-start | bytes 6148
  331.2 11.0 copy-start.1
  342.2 58.9 %copy-start.4 = (bf16[1024,1024]{1,0:T(8,128)(2,1)S(1)}, bf16[1024,1024]{1,0:T(8,128)(2,1)}, u32[]{:S(2)}) copy-start(bf16[1024,1024]{1,0:T(8,128)(2,1)} %param.15) | copy-start | bytes 6291460
  342.3 106.9 %all-gather.18.cloned.1.call-start = ((), (), s32[]{:S(2)}) async-start(), calls=%async_computation.12 | async-start | bytes 4456448 | tf_op jit(solution)/shard_map/all_gather | solution.py:139
  342.8 163.6 %all-gather.16.cloned.1.call-start = ((), (), s32[]{:S(2)}) async-start(), calls=%async_computation.11 | async-start | bytes 6291456 | tf_op jit(solution)/shard_map/all_gather | solution.py:172
  342.9 61.3 %copy-start.30 = (f32[1024]{0:T(1024)}, f32[1024]{0:T(1024)S(1)}, u32[]{:S(2)}) copy-start(f32[1024]{0:T(1024)S(1)} %convert_element_type.154) | copy-start | bytes 12292
  342.9 61.3 %copy-start.18 = (f32[1024]{0:T(1024)}, f32[1024]{0:T(1024)S(1)}, u32[]{:S(2)}) copy-start(f32[1024]{0:T(1024)S(1)} %convert_element_type.153) | copy-start | bytes 12292
  396.8 4.4 copy-start.8
  398.9 5.4 copy-start.16
  401.2 3.1 copy-start.20
  404.9 5.3 copy-start.43
  408.7 156.4 %all-gather.22.cloned.1.call-start = ((), (), s32[]{:S(2)}) async-start(), calls=%async_computation.15 | async-start | bytes 6291456 | tf_op jit(solution)/shard_map/all_gather | solution.py:189
  409.4 208.3 %all-gather.20.cloned.1.call-start = ((), (), s32[]{:S(2)}) async-start(), calls=%async_computation.13 | async-start | bytes 4456448 | tf_op jit(solution)/shard_map/all_gather | solution.py:140
  410.2 318.2 %reduce-scatter.12.cloned.1.call-start = ((), (), s32[]{:S(2)}) async-start(), calls=%async_computation.16 | async-start | bytes 6291456 | tf_op jit(solution)/shard_map/reduce_scatter | solution.py:204
  645.0 20.7 %copy-start.44 = (bf16[1024,2048]{1,0:T(8,128)(2,1)S(1)}, bf16[1024,2048]{1,0:T(8,128)(2,1)}, u32[]{:S(2)}) copy-start(bf16[1024,2048]{1,0:T(8,128)(2,1)} %all-gather.18.cloned.1.call-done) | copy-start | bytes 12582916
  662.5 3.2 copy-start.12
  676.2 108.7 %reduce-scatter.10.cloned.1.call-start = ((), (), s32[]{:S(2)}) async-start(), calls=%async_computation.14 | async-start | bytes 6291456 | tf_op jit(solution)/shard_map/reduce_scatter | solution.py:180
  692.9 35.5 %copy-start.5 = (bf16[1024,1024]{1,0:T(8,128)(2,1)S(1)}, bf16[1024,1024]{1,0:T(8,128)(2,1)}, u32[]{:S(2)}) copy-start(bf16[1024,1024]{1,0:T(8,128)(2,1)} %param.15) | copy-start | bytes 6291460
  692.9 35.5 %copy-start.17 = (f32[1024]{0:T(1024)S(1)}, f32[1024]{0:T(1024)}, u32[]{:S(2)}) copy-start(f32[1024]{0:T(1024)} %copy-done.16) | copy-start | bytes 12292
  692.9 35.5 %copy-start.19 = (f32[1024]{0:T(1024)S(1)}, f32[1024]{0:T(1024)}, u32[]{:S(2)}) copy-start(f32[1024]{0:T(1024)} %copy-done.18) | copy-start | bytes 12292
  692.9 35.5 %copy-start.21 = (f32[1024]{0:T(1024)S(1)}, f32[1024]{0:T(1024)}, u32[]{:S(2)}) copy-start(f32[1024]{0:T(1024)} %copy-done.20) | copy-start | bytes 12292
  692.9 35.5 %copy-start.25 = (f32[1024]{0:T(1024)S(1)}, f32[1024]{0:T(1024)}, u32[]{:S(2)}) copy-start(f32[1024]{0:T(1024)} %copy-done.24) | copy-start | bytes 12292
  693.0 35.5 %copy-start.31 = (f32[1024]{0:T(1024)S(1)}, f32[1024]{0:T(1024)}, u32[]{:S(2)}) copy-start(f32[1024]{0:T(1024)} %copy-done.30) | copy-start | bytes 12292
  693.0 35.5 %copy-start.33 = (f32[1024]{0:T(1024)S(1)}, f32[1024]{0:T(1024)}, u32[]{:S(2)}) copy-start(f32[1024]{0:T(1024)} %copy-done.32) | copy-start | bytes 12292
  693.0 161.3 %all-gather.24.cloned.1.call-start = ((), (), s32[]{:S(2)}) async-start(), calls=%async_computation.17 | async-start | bytes 6291456 | tf_op jit(solution)/shard_map/all_gather | solution.py:214
  785.0 10.1 copy-start.9
  793.1 1.9 copy-start.10
  797.5 618.1 %reduce-scatter.20.cloned.1.call-start = ((), (), s32[]{:S(2)}) async-start(), calls=%async_computation.21 | async-start | bytes 4456448 | tf_op jit(solution)/shard_map/reduce_scatter | solution.py:252
  812.6 605.0 %reduce-scatter.18.cloned.1.call-start = ((), (), s32[]{:S(2)}) async-start(), calls=%async_computation.20 | async-start | bytes 4456448 | tf_op jit(solution)/shard_map/reduce_scatter | solution.py:249
  828.0 26.3 %copy-start.37 = (f32[512]{0:T(512)S(1)}, f32[512]{0:T(512)}, u32[]{:S(2)}) copy-start(f32[512]{0:T(512)} %mul.312) | copy-start | bytes 6148
  828.0 34.5 %copy-start.2 = (bf16[2048,512]{0,1:T(8,128)(2,1)S(1)}, bf16[2048,512]{0,1:T(8,128)(2,1)}, u32[]{:S(2)}) copy-start(bf16[2048,512]{0,1:T(8,128)(2,1)} %copy-done.1) | copy-start | bytes 6291460
  828.1 646.7 %all-reduce.14.cloned.1.call-start = ((), (), s32[]{:S(2)}) async-start(), calls=%async_computation.22 | async-start | bytes 8388608
  868.0 1.9 copy-start.7
  954.1 11.3 copy-start
  970.3 9.8 copy-start.11
  986.4 1.9 copy-start.7
  1070.1 10.7 copy-start
  1085.8 12.0 copy-start.11
  1104.1 1.9 copy-start.7
  1187.5 10.7 copy-start
  1203.2 12.0 copy-start.11
  1221.5 1.9 copy-start.7
  1304.9 10.7 copy-start
  1320.6 12.0 copy-start.11
  1337.2 5.4 copy-start.15
  1363.4 6.4 copy-start.14
  1363.4 171.7 %reduce-scatter.16.cloned.1.call-start = ((), (), s32[]{:S(2)}) async-start(), calls=%async_computation.19 | async-start | bytes 1114112 | tf_op jit(solution)/shard_map/reduce_scatter | solution.py:246
  1369.7 220.9 %reduce-scatter.14.cloned.1.call-start = ((), (), s32[]{:S(2)}) async-start(), calls=%async_computation.18 | async-start | bytes 6291456 | tf_op jit(solution)/shard_map/reduce_scatter | solution.py:234
  1379.8 37.6 %copy-start.39 = (f32[512]{0:T(512)S(1)}, f32[512]{0:T(512)}, u32[]{:S(2)}) copy-start(f32[512]{0:T(512)} %get-tuple-element.484) | copy-start | bytes 6148
  1379.8 210.8 %copy-start.6 = (bf16[1024,1024]{1,0:T(8,128)(2,1)S(1)}, bf16[1024,1024]{1,0:T(8,128)(2,1)}, u32[]{:S(2)}) copy-start(bf16[1024,1024]{1,0:T(8,128)(2,1)} %param.15) | copy-start | bytes 6291460
  1379.8 210.8 %copy-start.23 = (f32[1024]{0:T(1024)S(1)}, f32[1024]{0:T(1024)}, u32[]{:S(2)}) copy-start(f32[1024]{0:T(1024)} %copy-done.22) | copy-start | bytes 12292
  1379.8 210.8 %copy-start.27 = (f32[1024]{0:T(1024)S(1)}, f32[1024]{0:T(1024)}, u32[]{:S(2)}) copy-start(f32[1024]{0:T(1024)} %copy-done.26) | copy-start | bytes 12292
  1379.8 210.8 %copy-start.29 = (f32[1024]{0:T(1024)S(1)}, f32[1024]{0:T(1024)}, u32[]{:S(2)}) copy-start(f32[1024]{0:T(1024)} %copy-done.28) | copy-start | bytes 12292
  1379.9 214.3 %copy-start.34 = (f32[1024]{0:T(1024)S(1)}, f32[1024]{0:T(1024)}, u32[]{:S(2)}) copy-start(f32[1024]{0:T(1024)} %get-tuple-element.419) | copy-start | bytes 12292
  1379.9 214.3 %copy-start.35 = (f32[1024]{0:T(1024)S(1)}, f32[1024]{0:T(1024)}, u32[]{:S(2)}) copy-start(f32[1024]{0:T(1024)} %get-tuple-element.417) | copy-start | bytes 12292
  (6 other events, 6.0 us)
Sparse Core Ops, SparseCore 0:
  10.2 48.0 all-gather.11
  60.4 55.2 all-gather.9
  117.8 37.8 all-gather.13
  342.4 54.3 reduce-scatter.7
  398.8 50.3 all-gather.17
  451.2 55.2 all-gather.15
  508.0 57.0 all-gather.21
  567.3 50.3 all-gather.19
  676.4 51.9 reduce-scatter.11
  730.5 54.3 reduce-scatter.9
  797.6 56.6 all-gather.23
  858.0 72.7 reduce-scatter.19
  934.7 71.9 reduce-scatter.17
  1363.5 111.2 all-reduce.13
  1478.3 56.7 reduce-scatter.15
  1537.2 53.4 reduce-scatter.13
where the time goes:
time: 1650 us
  matrix products  572 us (35%)
  waiting for transfers between devices  490 us (30%)
  other arithmetic  296 us (18%)
  blocking collectives  177 us (11%)
  local copies, waits for them, and re-layouts  78.8 us (5%)
  between operations  16.9 us (1%)
    dot_general x8, matrix products, block_scores(): jnp.einsum('qhd,khd->hqk', query_heads, key_heads, preferred_element_type...  157 us
    unnamed x3, blocking collectives  110 us
    convert_element_type x4, other arithmetic, one_block(): (probabilities * (grad_probs - inner_sum)).astype(jnp.bfloat16)  110 us
    dot_general x4, matrix products, one_block(): jnp.einsum('hqk,qhd->khd', probabilities.astype(jnp.bfloat16), grad_rows,...  63.9 us
    dot_general x4, matrix products, one_block(): jnp.einsum('hqk,khd->qhd', probabilities, value_heads, preferred_element_...  62.6 us
    reduce_sum x4, other arithmetic, one_block(): row_total = jnp.sum(exp_scores, axis=-1, keepdims=True)  60 us
    reduce_scatter x1, waiting for transfers between devices, body(): lax.psum_scatter(grad_mix.astype(jnp.bfloat16), 'dp', scatter_dimension=0...  58.4 us
    all_gather x1, waiting for transfers between devices, body(): gathered_ffn = lax.all_gather(entry_ffn, 'mp', axis=0, tiled=True)  57.3 us
  transfers between devices with their start and end apart: 16, of which 13 were waited for; matrix products, arithmetic and copies ran while one was open for 52% of the time, Pallas kernels for 0%

commit v1 on v0

v1 whole, which is shorter than its diff:
```python
import functools

import jax
import jax.numpy as jnp
from jax import lax
from jax.experimental import pallas as pl
from jax.experimental.pallas import tpu as pltpu
from jax.sharding import Mesh, PartitionSpec as P

HD = 64
BLOCK = 256
LANES = 128
NORM_EPS = 1e-05
F32 = jnp.float32
BF16 = jnp.bfloat16
WEIGHT_AXES = ("p", "h")
PART_AXES = ("c", "l")
ALL_AXES = ("p", "c", "h", "l")


def dot(a, b, dims=((1,), (0,))):
    return lax.dot_general(a, b, (dims, ((), ())), preferred_element_type=F32)


def attn_forward_kernel(chunks, blocks, offs, *refs):
    q_in, k_in, v_in = (refs[t * chunks : (t + 1) * chunks] for t in range(3))
    scale_ref = refs[3 * chunks]
    rest = refs[3 * chunks + 1 :]
    att_out, scaled_out = rest[:chunks], rest[chunks : 2 * chunks]
    lse_ref, qb, kb, vb, ob = rest[2 * chunks :]
    parity = pl.program_id(1)
    rows = q_in[0].shape[0]

    @pl.when(parity == 0)
    def _():
        for t in range(chunks):
            place = pl.ds(pl.multiple_of(offs[t], BLOCK), rows)
            qb[place, :] = q_in[t][...]
            kb[place, :] = k_in[t][...]
            vb[place, :] = v_in[t][...]

    lane_head = lax.broadcasted_iota(jnp.int32, (BLOCK, LANES), 1) // HD
    mine = lane_head == parity
    for i in range(blocks):
        here = slice(i * BLOCK, (i + 1) * BLOCK)
        keys = slice(0, (i + 1) * BLOCK)
        q = jnp.where(mine, qb[here, :] * BF16(HD**-0.5), BF16(0))
        scores = dot(q, kb[keys, :], ((1,), (1,)))
        top = jnp.max(scores, axis=1, keepdims=True)
        weights = jnp.exp(scores - top)
        total = jnp.sum(weights, axis=1, keepdims=True)
        out = dot(weights.astype(BF16), vb[keys, :]) / total
        lse = jnp.broadcast_to(top + jnp.log(total), (BLOCK, LANES))
        lse_ref[0, :, here] = lse.T[:8, :]
        ob[here, :] = jnp.where(mine, out, ob[here, :])

    @pl.when(parity == 1)
    def _():
        for t in range(chunks):
            place = pl.ds(pl.multiple_of(offs[t], BLOCK), rows)
            out = ob[place, :]
            att_out[t][...] = out.astype(BF16)
            scaled_out[t][...] = (out * scale_ref[...]).astype(BF16)


def attn_forward(offs, projected, columns):
    chunks = len(projected)
    rows, width = projected[0].shape[0], projected[0].shape[1] // 3
    total, pairs = rows * chunks, width // LANES

    def column(t):
        return pl.BlockSpec((rows, LANES), lambda j, k, o: (0, t * pairs + j))

    row_specs = [column(t) for t in range(3) for _ in range(chunks)]
    out_specs = [column(0)] * (2 * chunks) + [
        pl.BlockSpec((1, 8, total), lambda j, k, o: (2 * j + k, 0, 0))
    ]
    outs = pl.pallas_call(
        functools.partial(attn_forward_kernel, chunks, total // BLOCK),
        grid_spec=pltpu.PrefetchScalarGridSpec(
            num_scalar_prefetch=1,
            grid=(pairs, 2),
            in_specs=row_specs + [pl.BlockSpec((1, LANES), lambda j, k, o: (0, j))],
            out_specs=out_specs,
            scratch_shapes=[pltpu.VMEM((total, LANES), BF16)] * 3
            + [pltpu.VMEM((total, LANES), F32)],
        ),
        out_shape=[jax.ShapeDtypeStruct((rows, width), BF16)] * (2 * chunks)
        + [jax.ShapeDtypeStruct((2 * pairs, 8, total), F32)],
        compiler_params=pltpu.CompilerParams(
            dimension_semantics=("arbitrary", "arbitrary"), vmem_limit_bytes=48 << 20
        ),
        name="attn_forward",
    )(offs, *[part for _ in range(3) for part in projected], columns)
    return outs[:chunks], outs[chunks : 2 * chunks], outs[-1]


def attn_backward_kernel(chunks, blocks, offs, *refs):
    groups = [refs[t * chunks : (t + 1) * chunks] for t in range(5)]
    lse_ref = refs[5 * chunks]
    rest = refs[5 * chunks + 1 :]
    grad_out = rest[:chunks]
    qb, kb, vb, gb, delta, dq, dk, dv = rest[chunks:]
    pair, parity = pl.program_id(0), pl.program_id(1)
    rows = groups[0][0].shape[0]
    width = pl.num_programs(0) * LANES
    lane_head = lax.broadcasted_iota(jnp.int32, (BLOCK, LANES), 1) // HD
    mine = lane_head == parity

    @pl.when(parity == 0)
    def _():
        for t in range(chunks):
            start = pl.multiple_of(offs[t], BLOCK)
            place = pl.ds(start, rows)
            for buf, group in zip((qb, kb, vb, gb), groups):
                buf[place, :] = group[t][...]
            for i in range(rows // BLOCK):
                here = slice(i * BLOCK, (i + 1) * BLOCK)
                product = groups[3][t][here, :].astype(F32) * groups[4][t][here, :].astype(F32)
                turned = product.T
                there = pl.ds(pl.multiple_of(start + i * BLOCK, BLOCK), BLOCK)
                for head in range(2):
                    part = turned[head * HD : (head + 1) * HD, :]
                    delta[head, :, there] = jnp.broadcast_to(
                        jnp.sum(part, axis=0, keepdims=True), (8, BLOCK)
                    )
        dk[...] = jnp.zeros_like(dk)
        dv[...] = jnp.zeros_like(dv)

    for i in range(blocks):
        here = slice(i * BLOCK, (i + 1) * BLOCK)
        keys = slice(0, (i + 1) * BLOCK)
        q = jnp.where(mine, qb[here, :] * BF16(HD**-0.5), BF16(0))
        grad = jnp.where(mine, gb[here, :], BF16(0))
        scores = dot(kb[keys, :], q, ((1,), (1,)))
        probs = jnp.exp(scores - lse_ref[0, 0:1, here])
        grad_probs = dot(vb[keys, :], grad, ((1,), (1,)))
        grad_scores = (probs * (grad_probs - delta[parity, 0:1, here])).astype(BF16)
        dv[keys, :] += dot(probs.astype(BF16), grad)
        dk[keys, :] += dot(grad_scores, q)
        grad_q = dot(grad_scores, kb[keys, :], ((0,), (0,))) * HD**-0.5
        dq[here, :] = jnp.where(mine, grad_q, dq[here, :])

    @pl.when(parity == 1)
    def _():
        for t in range(chunks):
            place = pl.ds(pl.multiple_of(offs[t], BLOCK), rows)
            for n, buf in enumerate((dq, dk, dv)):
                where = pl.ds(pl.multiple_of(n * width + pair * LANES, LANES), LANES)
                grad_out[t][:, where] = buf[place, :].astype(BF16)


def attn_backward(offs, projected, grad_attended, attended, lse):
    chunks = len(projected)
    rows, width = projected[0].shape[0], projected[0].shape[1] // 3
    total, pairs = rows * chunks, width // LANES

    def column(t):
        return pl.BlockSpec((rows, LANES), lambda j, k, o: (0, t * pairs + j))

    in_specs = [column(t) for t in (0, 1, 2, 0, 0) for _ in range(chunks)]
    return pl.pallas_call(
        functools.partial(attn_backward_kernel, chunks, total // BLOCK),
        grid_spec=pltpu.PrefetchScalarGridSpec(
            num_scalar_prefetch=1,
            grid=(pairs, 2),
            in_specs=in_specs
            + [pl.BlockSpec((1, 8, total), lambda j, k, o: (2 * j + k, 0, 0))],
            out_specs=[pl.BlockSpec((rows, 3 * width), lambda j, k, o: (0, 0))] * chunks,
            scratch_shapes=[pltpu.VMEM((total, LANES), BF16)] * 4
            + [pltpu.VMEM((2, 8, total), F32)]
            + [pltpu.VMEM((total, LANES), F32)] * 3,
        ),
        out_shape=[jax.ShapeDtypeStruct((rows, 3 * width), BF16)] * chunks,
        compiler_params=pltpu.CompilerParams(
            dimension_semantics=("arbitrary", "arbitrary"), vmem_limit_bytes=56 << 20
        ),
        name="attn_backward",
    )(
        offs,
        *[part for _ in range(3) for part in projected],
        *grad_attended,
        *attended,
        lse,
    )


def exchange(a):
    return lax.ppermute(a, ("c", "h"), [(0, 0), (1, 2), (2, 1), (3, 3)])


def other_core(a):
    return lax.ppermute(a, "c", [(0, 1), (1, 0)])


def normalize(row_values):
    row_mean = jnp.mean(row_values, axis=-1, keepdims=True)
    centred = row_values - row_mean
    spread = jnp.mean(centred * centred, axis=-1, keepdims=True)
    inverse = lax.rsqrt(spread + NORM_EPS)
    return (centred * inverse, inverse)


def norm_back(gradient, normed, inverse):
    return inverse * (
        gradient
        - jnp.mean(gradient, axis=-1, keepdims=True)
        - normed * jnp.mean(gradient * normed, axis=-1, keepdims=True)
    )


def body(
    paired,
    tokens,
    w_qkv,
    w_out,
    w_in,
    w_back,
    gain_attn,
    gain_post,
    gain_ffn,
    gain_mid,
    head_scale,
    cotangent,
):
    def spread_tokens(a):
        if paired:
            return [a, other_core(a)]
        return [lax.all_gather(a, PART_AXES, axis=0, tiled=True)]

    def collect_tokens(make):
        if paired:
            sent = other_core(make(1).astype(BF16))
            return make(0) + sent.astype(F32)
        return lax.psum_scatter(
            make(0).astype(BF16), PART_AXES, scatter_dimension=0, tiled=True
        ).astype(F32)

    def sum_parts(values):
        if paired:
            theirs = other_core(jnp.stack(values))
            return [values[0] + theirs[1], values[1] + theirs[0]]
        return [lax.psum(values[0], PART_AXES)]

    def weight_grad(left, right):
        total = sum(dot(a, b, ((0,), (0,))) for a, b in zip(left, right))
        return lax.psum_scatter(
            total.astype(BF16), WEIGHT_AXES, scatter_dimension=0, tiled=True
        )

    core = lax.axis_index("c")
    ranks = lax.axis_size("p") * lax.axis_size("h")
    depth, _, feat_width = w_qkv.shape
    model = depth * ranks
    parts = 2 if paired else 1

    small = jnp.concatenate([gain_attn, gain_post, gain_ffn, gain_mid])
    columns = -(-small.shape[0] // depth)
    small = jnp.pad(small, (0, columns * depth - small.shape[0])).reshape(depth, columns)
    small = jnp.pad(small, ((0, 0), (0, LANES - columns)))
    first = jnp.concatenate([w_qkv.reshape(depth, 3 * feat_width), small], axis=1)
    first, tokens, scale, w_out_own, w_in_own, w_back_own = (
        exchange(first),
        exchange(tokens),
        exchange(head_scale),
        exchange(w_out),
        exchange(w_in),
        exchange(w_back),
    )

    def gather(a):
        return lax.all_gather(a, WEIGHT_AXES, axis=0, tiled=True)

    first = gather(first)
    w_mix, w_up, w_down = gather(w_out_own), gather(w_in_own), gather(w_back_own)
    w_proj = first[:, : 3 * feat_width]
    small = first[:, 3 * feat_width : 3 * feat_width + columns].astype(F32)
    small = small.reshape(ranks, depth * columns)
    mid_rows = gain_mid.shape[0]
    g_attn, g_post, g_ffn = (
        small[:, n * depth : (n + 1) * depth].reshape(1, model) for n in range(3)
    )
    g_mid = small[:, 3 * depth : 3 * depth + mid_rows].reshape(1, ranks * mid_rows)
    hidden = ranks * mid_rows * lax.axis_size(PART_AXES)

    inputs = tokens.astype(F32)
    rows = inputs.shape[0]
    if paired:
        offs = jnp.stack([core * rows, (1 - core) * rows]).astype(jnp.int32)
    else:
        offs = jnp.zeros((1,), jnp.int32)
    column_scale = jnp.repeat(scale.astype(F32), HD)[None, :]

    norm_attn, inv_attn = normalize(inputs)
    gathered = spread_tokens((norm_attn * g_attn).astype(BF16))
    projected = [dot(part, w_proj).astype(BF16) for part in gathered]
    attended, scaled, lse = attn_forward(offs, projected, column_scale)
    mixed_sum = collect_tokens(lambda t: dot(scaled[t], w_mix))
    norm_post, inv_post = normalize(mixed_sum)
    middle = inputs + norm_post * g_post
    norm_ffn, inv_ffn = normalize(middle)
    gathered_ffn = spread_tokens((norm_ffn * g_ffn).astype(BF16))
    upper = [dot(part, w_up) for part in gathered_ffn]
    active = [jax.nn.gelu(u, approximate=False) for u in upper]
    sums = sum_parts(
        [jnp.stack([jnp.sum(a, axis=-1), jnp.sum(a * a, axis=-1)]) for a in active]
    )
    mean_mid = [s[0][:, None] / hidden for s in sums]
    inv_mid = [
        lax.rsqrt(s[1][:, None] / hidden - m * m + NORM_EPS) for s, m in zip(sums, mean_mid)
    ]
    norm_mid = [(a - m) * r for a, m, r in zip(active, mean_mid, inv_mid)]
    fed_down = [(n * g_mid).astype(BF16) for n in norm_mid]
    output = middle + collect_tokens(lambda t: dot(fed_down[t], w_down))
    output = exchange(output.astype(BF16))

    cotangent = exchange(cotangent)
    grad_top = cotangent.astype(F32)
    grad_full = spread_tokens(cotangent)
    grad_down = weight_grad(fed_down, grad_full)
    grad_fed = [dot(g, w_down, ((1,), (1,))) for g in grad_full]
    grad_gmid = sum(jnp.sum(g * n, axis=0) for g, n in zip(grad_fed, norm_mid))
    scaled_mid = [g * g_mid for g in grad_fed]
    moments = sum_parts(
        [
            jnp.stack([jnp.sum(g, axis=-1), jnp.sum(g * n, axis=-1)])
            for g, n in zip(scaled_mid, norm_mid)
        ]
    )
    grad_upper = []
    for t in range(parts):
        grad_active = inv_mid[t] * (
            scaled_mid[t]
            - moments[t][0][:, None] / hidden
            - norm_mid[t] * (moments[t][1][:, None] / hidden)
        )
        u = upper[t]
        normal_cdf = 0.5 * (1.0 + lax.erf(u * 0.7071067811865476))
        density = jnp.exp(-0.5 * u * u) * 0.3989422804014327
        grad_upper.append((grad_active * (normal_cdf + u * density)).astype(BF16))
    grad_up = weight_grad(gathered_ffn, grad_upper)
    grad_entry_ffn = collect_tokens(lambda t: dot(grad_upper[t], w_up, ((1,), (1,))))
    grad_gffn = jnp.sum(grad_entry_ffn * norm_ffn, axis=0)
    grad_middle = grad_top + norm_back(grad_entry_ffn * g_ffn, norm_ffn, inv_ffn)
    grad_gpost = jnp.sum(grad_middle * norm_post, axis=0)
    grad_mixed = norm_back(grad_middle * g_post, norm_post, inv_post).astype(BF16)
    grad_mfull = spread_tokens(grad_mixed)
    grad_mix = weight_grad(scaled, grad_mfull)
    grad_scaled = [dot(g, w_mix, ((1,), (1,))) for g in grad_mfull]
    grad_heads = sum(
        jnp.sum(jnp.sum(g * a.astype(F32), axis=0).reshape(-1, HD), axis=1)
        for g, a in zip(grad_scaled, attended)
    )
    grad_attended = [(g * column_scale).astype(BF16) for g in grad_scaled]
    grad_proj = attn_backward(offs, projected, grad_attended, attended, lse)
    grad_wproj = weight_grad(gathered, grad_proj)
    grad_entry_attn = collect_tokens(lambda t: dot(grad_proj[t], w_proj, ((1,), (1,))))
    grad_gattn = jnp.sum(grad_entry_attn * norm_attn, axis=0)
    grad_inputs = grad_middle + norm_back(grad_entry_attn * g_attn, norm_attn, inv_attn)
    grad_inputs = exchange(grad_inputs.astype(BF16))

    slot = lax.axis_index(PART_AXES)
    slots = lax.axis_size(PART_AXES)
    own = jnp.concatenate([grad_gmid, grad_heads])
    placed = jnp.where(jnp.arange(slots)[:, None] == slot, own[None, :], 0.0).reshape(-1)
    sums = lax.psum(jnp.concatenate([grad_gattn, grad_gpost, grad_gffn, placed]), ALL_AXES)
    device_dp = lax.axis_index(("p", "c"))
    device_mp = lax.axis_index(("h", "l"))
    short = depth // slots
    starts = device_dp * depth + device_mp * short
    gains = [
        lax.dynamic_slice_in_dim(sums, n * model + starts, short) for n in range(3)
    ]
    base = 3 * model + device_mp * own.shape[0]
    grad_mid = lax.dynamic_slice_in_dim(sums, base + device_dp * mid_rows, mid_rows)
    grad_scale = lax.dynamic_slice_in_dim(
        sums, base + grad_gmid.shape[0], grad_heads.shape[0]
    )
    return (
        output,
        grad_inputs,
        exchange(grad_wproj).astype(F32).reshape(depth, 3, feat_width),
        exchange(grad_mix).astype(F32),
        exchange(grad_up).astype(F32),
        exchange(grad_down).astype(F32),
        *gains,
        grad_mid,
        grad_scale,
    )


def solution(mesh):
    data, split = mesh.shape["dp"], mesh.shape["mp"]
    named = Mesh(mesh.devices.reshape(data // 2, 2, 2, split // 2), ALL_AXES)
    dp, mp = ("p", "c"), ("h", "l")
    specs = (
        P(dp + mp, None),
        P(dp, None, mp),
        P(mp + dp, None),
        P(dp, mp),
        P(mp + dp, None),
    )
    return jax.shard_map(
        functools.partial(body, split == 2),
        mesh=named,
        in_specs=specs + (P(dp), P(dp), P(dp), P(mp + dp), P(mp), P(dp + mp, None)),
        out_specs=specs[:1]
        + specs
        + (P(dp + mp), P(dp + mp), P(dp + mp), P(mp + dp), P(mp)),
        check_vma=False,
    )
```

time: 1650 us -> 826 us (0.50)
  matrix products: 572 us -> 211 us
  other arithmetic: 296 us -> 44.2 us
  waiting for transfers between devices: 490 us -> 317 us
  blocking collectives: 177 us -> 41.4 us
  Pallas kernels: 0 us -> 102 us
  starting transfers between devices: 0.82 us -> 61.6 us
  local copies, waits for them, and re-layouts: 78.8 us -> 26.8 us
    dot_general x40 -> x24, matrix products: 572 us -> 211 us  [dot(): return lax.dot_general(a, b, (dims, ((), ())), preferred_element_type=F32)]
    convert_element_type x19 -> x8, other arithmetic: 152 us -> 34.1 us  [the longest x1 22.6 us: body(): grad_upper.append((grad_active * (normal_cdf + u * density)).astype(BF16))]
    unnamed x3 -> x0, blocking collectives: 110 us -> none
    pallas_call x0 -> x2, Pallas kernels: none -> 102 us  [the longest x1 60.6 us: attn_backward(): pl.pallas_call(functools.partial(attn_backward_kernel, chunks, total // B...]
    all_gather x8 -> x4, waiting for transfers between devices: 209 us -> 120 us  [gather(): return lax.all_gather(a, WEIGHT_AXES, axis=0, tiled=True)]
    reduce_sum x7 -> x2, other arithmetic: 69.3 us -> 0.24 us  [body(): jnp.sum(jnp.sum(g * a.astype(F32), axis=0).reshape(-1, HD), axis=1)]
    ppermute x0 -> x23, starting transfers between devices: none -> 60.7 us  [the longest x13 50.2 us: exchange(): return lax.ppermute(a, ('c', 'h'), [(0, 0), (1, 2), (2, 1), (3, 3)])]
    reduce_scatter x7 -> x4, waiting for transfers between devices: 252 us -> 196 us  [weight_grad(): lax.psum_scatter(total.astype(BF16), WEIGHT_AXES, scatter_dimension=0, ti...]
  transfers between devices with their start and end apart: 16 -> 31, of which waited for: 13 -> 8; matrix products, arithmetic and copies ran while one was open for 52% -> 26% of each run, Pallas kernels for 0% -> 12%
where the time goes in v1:
time: 826 us; the launch traced here: 819 us
  waiting for transfers between devices  317 us (38%)
  matrix products  211 us (26%)
  Pallas kernels  102 us (12%)
  starting transfers between devices  61.6 us (7%)
  other arithmetic  44.2 us (5%)
  blocking collectives  41.4 us (5%)
  local copies, waits for them, and re-layouts  26.8 us (3%)
  between operations  15.4 us (2%)
    dot_general x24, matrix products, dot(): return lax.dot_general(a, b, (dims, ((), ())), preferred_element_type=F32)  211 us
    reduce_scatter x4, waiting for transfers between devices, weight_grad(): lax.psum_scatter(total.astype(BF16), WEIGHT_AXES, scatter_dimension=0, ti...  196 us
    all_gather x4, waiting for transfers between devices, gather(): return lax.all_gather(a, WEIGHT_AXES, axis=0, tiled=True)  120 us
    pallas_call x1, Pallas kernels, attn_backward(): pl.pallas_call(functools.partial(attn_backward_kernel, chunks, total // B...  60.6 us
    ppermute x13, starting transfers between devices, exchange(): return lax.ppermute(a, ('c', 'h'), [(0, 0), (1, 2), (2, 1), (3, 3)])  50.2 us
    pallas_call x1, Pallas kernels, attn_forward(): pl.pallas_call(functools.partial(attn_forward_kernel, chunks, total // BL...  41.4 us
    psum x1, blocking collectives, body(): lax.psum(jnp.concatenate([grad_gattn, grad_gpost, grad_gffn, placed]), AL...  41.4 us
    convert_element_type x1, other arithmetic, body(): grad_upper.append((grad_active * (normal_cdf + u * density)).astype(BF16))  22.6 us
  transfers between devices with their start and end apart: 31, of which 8 were waited for; matrix products, arithmetic and copies ran while one was open for 26% of the time, Pallas kernels for 12%

profile of v1, /device:TPU:0, one launch (start us, length us, event | category | flops | bytes accessed | tf_op | source)
XLA Modules:
  0.0 819.1 jit_solution(9706470551421171625)
XLA Ops:
  7.2 0.8 pad_maximum_fusion.8
  8.2 0.9 copy.60
  10.6 1.5 collective-permute-start.4
  12.8 3.9 copy.43
  16.8 2.2 collective-permute-start
  21.5 70.2 %all-gather.5.cloned.1.call-done = bf16[1024,1664]{1,0:T(8,128)(2,1)} async-done(((bf16[64,1664]{1,0:T(8,128)(2,1)}), bf16[1024,1664]{1,0:T(8,128)(2,1)}) %all-gather.5.cloned.1.call-update) | async-done | bytes 3407888 | tf_op jit(solution)/shard_map/all_gather | solution.py:272
  91.7 1.0 slice_convert_fusion
  93.1 2.0 fusion.36
  95.8 3.9 copy.48
  99.7 17.7 %collective-permute-start.12 = (bf16[1024,1024]{0,1:T(8,128)(2,1)}, bf16[1024,1024]{0,1:T(8,128)(2,1)}, u32[]{:S(2)}, u32[]{:S(2)}) collective-permute-start(bf16[1024,1024]{0,1:T(8,128)(2,1)} %copy.48), channel_id=1, source_target_pairs={{0,0},{1,2},{2,1},{3,3},{4,4},{5,6},{6,5},{7,7},{8,8},{9,10},{10,9... | collective-permute-start | bytes 6291464 | tf_op jit(solution)/shard_map/ppermute | solution.py:189
  117.7 7.9 convolution_convert_fusion.1.refs_0_.refs_2_.refs_4_
  125.6 6.6 convolution_convert_fusion.refs_1_.refs_3_.refs_5_
  132.2 41.4 %attn_forward.1 = (bf16[1024,512]{1,0:T(8,128)(2,1)S(1)}, bf16[1024,512]{1,0:T(8,128)(2,1)S(1)}, bf16[1024,512]{1,0:T(8,128)(2,1)S(1)}, bf16[1024,512]{1,0:T(8,128)(2,1)S(1)}, f32[8,8,2048]{2,1,0:T(8,128)S(1)}) custom-call(s32[2]{0:T(128)S(1)} %pad_add_fusion.offs, bf16[1024,1536]{1,0:T(8,128)(2,1)} %convolution_convert_fusion.1.refs_0_.refs_2_.refs_4_, ...), custom_call_target="tpu_custom_call" | custom-call | tf_op jit(solution)/shard_map/attn_forward/pallas_call | solution.py:78
  173.7 0.8 copy-done.4
  174.5 1.0 copy-done.6
  175.5 5.3 convolution_convert_fusion.4
  182.5 9.3 %collective-permute-start.13 = (bf16[1024,1024]{0,1:T(8,128)(2,1)}, bf16[1024,1024]{0,1:T(8,128)(2,1)}, u32[]{:S(2)}, u32[]{:S(2)}) collective-permute-start(bf16[1024,1024]{0,1:T(8,128)(2,1)} %collective-permute-done.12), channel_id=1, source_target_pairs={{0,2},{2,0},{1,3},{3,1},{4,6},{6,4},{5,7},{7,5},{8,10},{10,8},{9,1... | collective-permute-start | bytes 6291464 | tf_op jit(solution)/shard_map/ppermute | solution.py:193
  192.0 3.3 fusion.72
  195.8 2.6 copy-done.14
  198.4 0.9 fusion.69
  199.9 2.2 multiply_convert_fusion.3
  202.1 26.1 %all-gather.9.cloned.1.call-done = bf16[1024,2048]{1,0:T(8,128)(2,1)} async-done(((bf16[64,2048]{1,0:T(8,128)(2,1)}), bf16[1024,2048]{1,0:T(8,128)(2,1)}) %all-gather.9.cloned.1.call-update) | async-done | bytes 4194320 | tf_op jit(solution)/shard_map/all_gather | solution.py:272
  228.2 26.7 %fusion.65 = (f32[1024]{0:T(1024)S(1)}, f32[1024]{0:T(1024)S(1)}, f32[1024,2048]{1,0:T(8,128)}, f32[1024,2048]{1,0:T(8,128)}) fusion(bf16[1024,1024]{0,1:T(8,128)(2,1)} %multiply_convert_fusion.3, bf16[1024,2048]{1,0:T(8,128)(2,1)} %all-gather.9.cloned.1.call-done), kind=kOutput, calls=%fused_computation.169 | convolution fusion | flops 4435474432 | bytes 23076864 | tf_op jit(solution)/shard_map/dot_general | solution.py:22
  254.9 26.8 %fusion.66 = (f32[1024]{0:T(1024)S(1)}, f32[1024]{0:T(1024)S(1)}, f32[1024,2048]{1,0:T(8,128)}, f32[1024,2048]{1,0:T(8,128)}) fusion(bf16[1024,1024]{0,1:T(8,128)(2,1)} %collective-permute-done.7, bf16[1024,2048]{1,0:T(8,128)(2,1)S(1)} %copy-done.52), kind=kOutput, calls=%fused_computation.170 | convolution fusion | flops 4435474432 | bytes 23076864 | tf_op jit(solution)/shard_map/dot_general | solution.py:22
  281.8 23.8 %all-gather.11.cloned.1.call-done = bf16[2048,1024]{1,0:T(8,128)(2,1)} async-done(((bf16[128,1024]{1,0:T(8,128)(2,1)}), bf16[2048,1024]{1,0:T(8,128)(2,1)}) %all-gather.11.cloned.1.call-update) | async-done | bytes 4194320 | tf_op jit(solution)/shard_map/all_gather | solution.py:272
  305.6 10.6 %fusion.73 = f32[1024,2048]{1,0:T(8,128)} fusion(bf16[1024,1024]{0,1:T(8,128)(2,1)} %collective-permute-done.13, bf16[2048,1024]{1,0:T(8,128)(2,1)} %all-gather.11.cloned.1.call-done), kind=kOutput, calls=%fused_computation.175 | convolution fusion | flops 4294967296 | bytes 14680064 | tf_op jit(solution)/shard_map/dot_general | solution.py:22
  316.3 19.7 %multiply_reduce_fusion.1 = (f32[2048]{0:T(1024)}, f32[1024]{0:T(1024)S(1)}, f32[1024]{0:T(1024)S(1)}, f32[1024]{0:T(1024)S(1)}, f32[1024]{0:T(1024)S(1)}, /*index=5*/f32[2048]{0:T(1024)}, f32[1024,2048]{1,0:T(8,128)}) fusion(f32[1024,2048]{1,0:T(8,128)} %get-tuple-element.78, f32[1024]{0:T(1024)S(1)} %add_rsqrt_fusion.1, f32[1024]{0:T(1024)S(1)} %bitcast.99, ...), kind=kOutput, calls=%fused_computation.21 | convolution fusion | flops 4328513536 | bytes 39903232 | tf_op jit(solution)/shard_map/dot_general | solution.py:22
  336.2 1.2 collective-permute-done.14
  337.4 22.6 %fusion.9 = (bf16[1024,2048]{1,0:T(8,128)(2,1)S(1)}, bf16[1024,2048]{1,0:T(8,128)(2,1)}, bf16[1024,2048]{1,0:T(8,128)(2,1)}, bf16[1024,2048]{1,0:T(8,128)(2,1)S(1)}) fusion(f32[1024,2048]{1,0:T(8,128)} %get-tuple-element.115, f32[1024,2048]{1,0:T(8,128)} %get-tuple-element.117, f32[1024,2048]{1,0:T(8,128)} %get-tuple-element.78, f32[1024]{0:T(1024)S(1)} %bitcast.105, ...), kind=kLoop, calls=%fused_computation.13 | loop fusion | flops 79691776 | bytes 67149824 | tf_op jit(solution)/shard_map/convert_element_type | solution.py:340
  360.0 7.7 fusion.76
  367.7 7.7 add_convert_fusion.1
  375.4 9.4 %convolution_convert_fusion.2 = bf16[1024,1024]{0,1:T(8,128)(2,1)} fusion(bf16[1024,2048]{1,0:T(8,128)(2,1)} %copy-done.22, bf16[1024,2048]{1,0:T(8,128)(2,1)} %all-gather.9.cloned.1.call-done), kind=kOutput, calls=%fused_computation.114 | convolution fusion | flops 4296015872 | bytes 10485760 | tf_op jit(solution)/shard_map/dot_general | solution.py:22
  385.0 6.4 fusion.77
  391.4 7.9 add_convert_fusion
  400.0 10.6 %multiply_reduce_fusion.8 = (f32[1024]{0:T(1024)S(1)}, f32[1024]{0:T(1024)S(1)}, f32[1024]{0:T(1024)S(1)}, f32[1024,1024]{0,1:T(8,128)S(1)}) fusion(f32[1024,1024]{0,1:T(8,128)} %copy-done.10, f32[1024]{0:T(1024)S(1)} %copy-done.47, f32[1024]{0:T(1024)S(1)} %copy-done.37, f32[1024]{0:T(1024)S(1)} %copy-done.45, ...), kind=kOutput, calls=%fused_computation.82 | convolution fusion | flops 4305449984 | bytes 18898944 | tf_op jit(solution)/shard_map/dot_general | solution.py:22
  410.7 4.8 multiply_reduce_fusion.9
  415.5 2.4 multiply_convert_fusion.2
  418.5 4.0 multiply_reduce_fusion.18
  422.6 3.9 multiply_reduce_fusion.17
  426.5 60.6 %attn_backward.1 = (bf16[1024,1536]{1,0:T(8,128)(2,1)}, bf16[1024,1536]{1,0:T(8,128)(2,1)}) custom-call(s32[2]{0:T(128)} %copy-done.5, bf16[1024,1536]{1,0:T(8,128)(2,1)} %convolution_convert_fusion.1.refs_0_.refs_2_.refs_4_, bf16[1024,1536]{1,0:T(8,128)(2,1)} %convolution_convert_fusion.refs_1_.refs_3_.refs_5_, ...), custom_call_target="tpu_custom_call" | custom-call | tf_op jit(solution)/shard_map/attn_backward/pallas_call | solution.py:162
  487.1 6.1 fusion.74
  493.2 6.5 add_convert_fusion.2
  500.0 8.2 %convolution_convert_fusion.3 = bf16[1024,1024]{0,1:T(8,128)(2,1)S(1)} fusion(bf16[1024,2048]{1,0:T(8,128)(2,1)} %get-tuple-element.100, bf16[2048,1024]{1,0:T(8,128)(2,1)} %all-gather.11.cloned.1.call-done), kind=kOutput, calls=%fused_computation.115 | convolution fusion | flops 4296015872 | bytes 10485760 | tf_op jit(solution)/shard_map/dot_general | solution.py:22
  508.7 4.6 fusion.52
  513.5 5.9 add_convert_fusion.3
  519.4 17.5 %collective-permute-start.11 = (bf16[1024,1024]{0,1:T(8,128)(2,1)}, bf16[1024,1024]{0,1:T(8,128)(2,1)}, u32[]{:S(2)}, u32[]{:S(2)}) collective-permute-start(bf16[1024,1024]{0,1:T(8,128)(2,1)} %add_convert_fusion.3), channel_id=1, source_target_pairs={{0,0},{1,2},{2,1},{3,3},{4,4},{5,6},{6,5},{7,7},{8,8},{9,10},{10,9... | collective-permute-start | bytes 6291464 | tf_op jit(solution)/shard_map/ppermute | solution.py:189
  536.9 2.9 fusion.75
  539.9 4.1 add_convert_fusion.4
  544.1 7.7 fusion.42
  551.8 2.7 fusion.41
  554.5 2.2 collective-permute-start.18
  557.2 1.6 collective-permute-start.21
  558.8 25.4 %reduce-scatter.11.cloned.1.call-done = bf16[128,1024]{1,0:T(8,128)(2,1)} async-done(((bf16[2048,1024]{1,0:T(8,128)(2,1)}), bf16[128,1024]{1,0:T(8,128)(2,1)}) %reduce-scatter.11.cloned.1.call-update) | async-done | bytes 262160 | tf_op jit(solution)/shard_map/reduce_scatter | solution.py:247
  584.2 1.6 collective-permute-start.22
  585.9 3.9 copy.51
  589.9 134.3 %reduce-scatter.5.cloned.1.call-done = bf16[64,1536]{1,0:T(8,128)(2,1)} async-done(((bf16[1024,1536]{1,0:T(8,128)(2,1)}), bf16[64,1536]{1,0:T(8,128)(2,1)}) %reduce-scatter.5.cloned.1.call-update) | async-done | bytes 196624 | tf_op jit(solution)/shard_map/reduce_scatter | solution.py:247
  724.1 1.6 collective-permute-start.19
  725.7 41.4 %psum.7 = f32[7184]{0:T(1024)S(1)} all-reduce(f32[7184]{0:T(1024)S(1)} %pad_maximum_fusion), channel_id=1, replica_groups=mesh['p'=8,'c'=2,'h'=2,'l'=1] {'p','c','h','l'}, use_global_device_ids=true, to_apply=%region_33.34 | all-reduce | flops 7184 | bytes 57472 | tf_op jit(solution)/shard_map/psum | solution.py:366
  768.3 36.0 %reduce-scatter.7.cloned.1.call-done = bf16[32,1024]{1,0:T(8,128)(2,1)} async-done(((bf16[512,1024]{1,0:T(8,128)(2,1)}), bf16[32,1024]{1,0:T(8,128)(2,1)}) %reduce-scatter.7.cloned.1.call-update) | async-done | bytes 65552 | tf_op jit(solution)/shard_map/reduce_scatter | solution.py:247
  804.3 1.5 collective-permute-start.20
  807.0 2.5 copy.52
  809.6 0.8 convert_element_type.131
  810.4 0.8 convert_element_type.133
  811.3 0.8 copy.62
  (225 shorter events, 14.7 us)
Async XLA Ops:
  7.2 11.8 %copy-start.56 = (bf16[64,2048]{1,0:T(8,128)(2,1)S(1)}, bf16[64,2048]{1,0:T(8,128)(2,1)}, u32[]{:S(2)}) copy-start(bf16[64,2048]{1,0:T(8,128)(2,1)} %param.14) | copy-start | bytes 786436
  7.2 84.6 %all-gather.5.cloned.1.call-start = ((), (), s32[]{:S(2)}) async-start(), calls=%async_computation.4 | async-start | bytes 3620864 | tf_op jit(solution)/shard_map/all_gather | solution.py:272
  9.2 0.7 collective-permute-start.1
  10.6 164.9 %all-gather.7.cloned.1.call-start = ((), (), s32[]{:S(2)}) async-start(), calls=%async_computation.5 | async-start | bytes 1114112 | tf_op jit(solution)/shard_map/all_gather | solution.py:272
  10.6 1.5 collective-permute-start.4
  12.8 215.4 %all-gather.9.cloned.1.call-start = ((), (), s32[]{:S(2)}) async-start(), calls=%async_computation.6 | async-start | bytes 4456448 | tf_op jit(solution)/shard_map/all_gather | solution.py:272
  16.8 3.7 collective-permute-start
  19.0 0.7 collective-permute-start.6
  20.4 285.2 %all-gather.11.cloned.1.call-start = ((), (), s32[]{:S(2)}) async-start(), calls=%async_computation.7 | async-start | bytes 4456448 | tf_op jit(solution)/shard_map/all_gather | solution.py:272
  20.5 74.6 %copy-start.13 = (bf16[1024,1024]{0,1:T(8,128)(2,1)}, bf16[1024,1024]{0,1:T(8,128)(2,1)S(1)}, u32[]{:S(2)}) copy-start(bf16[1024,1024]{0,1:T(8,128)(2,1)S(1)} %collective-permute-done) | copy-start | bytes 6291460
  20.9 74.2 %copy-start.58 = (bf16[8]{0:T(256)(128)(2,1)S(1)}, bf16[8]{0:T(256)(128)(2,1)}, u32[]{:S(2)}) copy-start(bf16[8]{0:T(256)(128)(2,1)} %param.20) | copy-start | bytes 52
  20.9 78.8 %copy-start.33 = (f32[1024]{0:T(1024)}, f32[1024]{0:T(1024)S(1)}, u32[]{:S(2)}) copy-start(f32[1024]{0:T(1024)S(1)} %broadcast_multiply_fusion.8) | copy-start | bytes 12292
  21.5 78.2 %copy-start.40 = (f32[1024]{0:T(1024)}, f32[1024]{0:T(1024)S(1)}, u32[]{:S(2)}) copy-start(f32[1024]{0:T(1024)S(1)} %add_rsqrt_fusion.4) | copy-start | bytes 12292
  93.1 6.6 copy-start.38
  95.1 30.5 %collective-permute-start.2 = (bf16[1024,1024]{0,1:T(8,128)(2,1)}, bf16[1024,1024]{0,1:T(8,128)(2,1)}, u32[]{:S(2)}, u32[]{:S(2)}) collective-permute-start(bf16[1024,1024]{0,1:T(8,128)(2,1)} %fusion.36), channel_id=1, source_target_pairs={{0,2},{2,0},{1,3},{3,1},{4,6},{6,4},{5,7},{7,5},{8,10},{10,8},{9,1... | collective-permute-start | bytes 6291464 | tf_op jit(solution)/shard_map/ppermute | solution.py:193
  95.1 22.4 %collective-permute-start.3 = (bf16[8]{0:T(256)(128)(2,1)S(1)}, bf16[8]{0:T(256)(128)(2,1)S(1)}, u32[]{:S(2)}, u32[]{:S(2)}) collective-permute-start(bf16[8]{0:T(256)(128)(2,1)S(1)} %copy-done.58), channel_id=1, source_target_pairs={{0,0},{1,2},{2,1},{3,3},{4,4},{5,6},{6,5},{7,7},{8,8},{9,10},{10,9... | collective-permute-start | bytes 56 | tf_op jit(solution)/shard_map/ppermute | solution.py:189
  99.7 82.7 %collective-permute-start.12 = (bf16[1024,1024]{0,1:T(8,128)(2,1)}, bf16[1024,1024]{0,1:T(8,128)(2,1)}, u32[]{:S(2)}, u32[]{:S(2)}) collective-permute-start(bf16[1024,1024]{0,1:T(8,128)(2,1)} %copy.48), channel_id=1, source_target_pairs={{0,0},{1,2},{2,1},{3,3},{4,4},{5,6},{6,5},{7,7},{8,8},{9,10},{10,9... | collective-permute-start | bytes 6291464 | tf_op jit(solution)/shard_map/ppermute | solution.py:189
  117.5 14.7 %copy-start.5 = (s32[2]{0:T(128)}, s32[2]{0:T(128)S(1)}, u32[]{:S(2)}) copy-start(s32[2]{0:T(128)S(1)} %pad_add_fusion.offs) | copy-start | bytes 28
  117.6 8.0 copy-start.42
  117.7 7.9 copy-start.48
  175.5 16.5 %copy-start = (bf16[1024,512]{1,0:T(8,128)(2,1)}, bf16[1024,512]{1,0:T(8,128)(2,1)S(1)}, u32[]{:S(2)}) copy-start(bf16[1024,512]{1,0:T(8,128)(2,1)S(1)} %get-tuple-element.18) | copy-start | bytes 3145732
  175.5 243.0 %copy-start.2 = (bf16[1024,512]{1,0:T(8,128)(2,1)}, bf16[1024,512]{1,0:T(8,128)(2,1)S(1)}, u32[]{:S(2)}) copy-start(bf16[1024,512]{1,0:T(8,128)(2,1)S(1)} %get-tuple-element.20.refs_8_) | copy-start | bytes 3145732
  175.5 247.1 %copy-start.3 = (bf16[1024,512]{1,0:T(8,128)(2,1)}, bf16[1024,512]{1,0:T(8,128)(2,1)S(1)}, u32[]{:S(2)}) copy-start(bf16[1024,512]{1,0:T(8,128)(2,1)S(1)} %get-tuple-element.21.refs_9_) | copy-start | bytes 3145732
  175.5 5.3 copy-start.57
  180.8 11.2 %collective-permute-start.5 = (bf16[1024,1024]{0,1:T(8,128)(2,1)}, bf16[1024,1024]{0,1:T(8,128)(2,1)}, u32[]{:S(2)}, u32[]{:S(2)}) collective-permute-start(bf16[1024,1024]{0,1:T(8,128)(2,1)} %convolution_convert_fusion.4), channel_id=1, source_target_pairs={{0,2},{2,0},{1,3},{3,1},{4,6},{6,4},{5,7},{7,5},{8,10},{10,8},{9,1... | collective-permute-start | bytes 6291464 | tf_op jit(solution)/shard_map/ppermute | solution.py:193
  180.8 0.7 collective-permute-start.9
  182.2 374.9 %reduce-scatter.9.cloned.1.call-start = ((), (), s32[]{:S(2)}) async-start(), calls=%async_computation.10 | async-start | bytes 4456448 | tf_op jit(solution)/shard_map/reduce_scatter | solution.py:247
  182.5 99.4 %collective-permute-start.13 = (bf16[1024,1024]{0,1:T(8,128)(2,1)}, bf16[1024,1024]{0,1:T(8,128)(2,1)}, u32[]{:S(2)}, u32[]{:S(2)}) collective-permute-start(bf16[1024,1024]{0,1:T(8,128)(2,1)} %collective-permute-done.12), channel_id=1, source_target_pairs={{0,2},{2,0},{1,3},{3,1},{4,6},{6,4},{5,7},{7,5},{8,10},{10,8},{9,1... | collective-permute-start | bytes 6291464 | tf_op jit(solution)/shard_map/ppermute | solution.py:193
  191.8 8.1 copy-start.44
  199.9 55.0 %copy-start.46 = (f32[1024]{0:T(1024)}, f32[1024]{0:T(1024)S(1)}, u32[]{:S(2)}) copy-start(f32[1024]{0:T(1024)S(1)} %add_rsqrt_fusion.2) | copy-start | bytes 12292
  202.0 52.9 %collective-permute-start.7 = (bf16[1024,1024]{0,1:T(8,128)(2,1)}, bf16[1024,1024]{0,1:T(8,128)(2,1)}, u32[]{:S(2)}, u32[]{:S(2)}) collective-permute-start(bf16[1024,1024]{0,1:T(8,128)(2,1)} %multiply_convert_fusion.3), channel_id=1, source_target_pairs={{0,2},{2,0},{1,3},{3,1},{4,6},{6,4},{5,7},{7,5},{8,10},{10,8},{9,1... | collective-permute-start | bytes 6291464 | tf_op jit(solution)/shard_map/ppermute | solution.py:193
  228.2 26.7 %copy-start.52 = (bf16[1024,2048]{1,0:T(8,128)(2,1)S(1)}, bf16[1024,2048]{1,0:T(8,128)(2,1)}, u32[]{:S(2)}) copy-start(bf16[1024,2048]{1,0:T(8,128)(2,1)} %all-gather.9.cloned.1.call-done) | copy-start | bytes 12582916
  281.7 34.5 %collective-permute-start.8 = (f32[2,2,1024]{2,1,0:T(2,128)S(1)}, f32[2,2,1024]{2,1,0:T(2,128)S(1)}, u32[]{:S(2)}, u32[]{:S(2)}) collective-permute-start(f32[2,2,1024]{2,1,0:T(2,128)S(1)} %pad_maximum_fusion.1), channel_id=1, source_target_pairs={{0,2},{2,0},{1,3},{3,1},{4,6},{6,4},{5,7},{7,5},{8,10},{10,8},{9,1... | collective-permute-start | bytes 49160 | tf_op jit(solution)/shard_map/ppermute | solution.py:193
  336.1 1.2 collective-permute-start.14
  360.0 7.7 copy-start.22
  360.0 7.7 copy-start.21
  375.3 208.8 %reduce-scatter.11.cloned.1.call-start = ((), (), s32[]{:S(2)}) async-start(), calls=%async_computation.11 | async-start | bytes 4456448 | tf_op jit(solution)/shard_map/reduce_scatter | solution.py:247
  375.4 9.6 %copy-start.18 = (bf16[1024,2048]{1,0:T(8,128)(2,1)S(1)}, bf16[1024,2048]{1,0:T(8,128)(2,1)}, u32[]{:S(2)}) copy-start(bf16[1024,2048]{1,0:T(8,128)(2,1)} %get-tuple-element.83) | copy-start | bytes 12582916
  384.9 14.8 %collective-permute-start.15 = (bf16[1024,1024]{0,1:T(8,128)(2,1)}, bf16[1024,1024]{0,1:T(8,128)(2,1)}, u32[]{:S(2)}, u32[]{:S(2)}) collective-permute-start(bf16[1024,1024]{0,1:T(8,128)(2,1)} %convolution_convert_fusion.2), channel_id=1, source_target_pairs={{0,2},{2,0},{1,3},{3,1},{4,6},{6,4},{5,7},{7,5},{8,10},{10,8},{9,1... | collective-permute-start | bytes 6291464 | tf_op jit(solution)/shard_map/ppermute | solution.py:193
  385.0 6.4 copy-start.20
  399.4 11.3 %copy-start.28 = (f32[1024]{0:T(1024)S(1)}, f32[1024]{0:T(1024)}, u32[]{:S(2)}) copy-start(f32[1024]{0:T(1024)} %copy-done.27) | copy-start | bytes 12292
  399.4 11.3 %copy-start.30 = (f32[1024]{0:T(1024)S(1)}, f32[1024]{0:T(1024)}, u32[]{:S(2)}) copy-start(f32[1024]{0:T(1024)} %copy-done.29) | copy-start | bytes 12292
  399.4 11.3 %copy-start.32 = (f32[1024]{0:T(1024)S(1)}, f32[1024]{0:T(1024)}, u32[]{:S(2)}) copy-start(f32[1024]{0:T(1024)} %copy-done.31) | copy-start | bytes 12292
  399.4 324.7 %reduce-scatter.5.cloned.1.call-start = ((), (), s32[]{:S(2)}) async-start(), calls=%async_computation.8 | async-start | bytes 3342336 | tf_op jit(solution)/shard_map/reduce_scatter | solution.py:247
  399.7 11.0 %copy-start.9 = (f32[1024,1024]{0,1:T(8,128)S(1)}, f32[1024,1024]{0,1:T(8,128)}, u32[]{:S(2)}) copy-start(f32[1024,1024]{0,1:T(8,128)} %copy-done.8) | copy-start | bytes 12582916
  399.7 11.0 %copy-start.11 = (f32[1024,1024]{0,1:T(8,128)S(1)}, f32[1024,1024]{0,1:T(8,128)}, u32[]{:S(2)}) copy-start(f32[1024,1024]{0,1:T(8,128)} %copy-done.10) | copy-start | bytes 12582916
  418.1 4.5 collective-permute-start.16
  487.1 6.1 copy-start.54
  499.7 8.9 %copy-start.49 = (bf16[1024,1664]{1,0:T(8,128)(2,1)S(1)}, bf16[1024,1664]{1,0:T(8,128)(2,1)}, u32[]{:S(2)}) copy-start(bf16[1024,1664]{1,0:T(8,128)(2,1)} %all-gather.5.cloned.1.call-done) | copy-start | bytes 10223620
  499.8 304.5 %reduce-scatter.7.cloned.1.call-start = ((), (), s32[]{:S(2)}) async-start(), calls=%async_computation.9 | async-start | bytes 1114112 | tf_op jit(solution)/shard_map/reduce_scatter | solution.py:247
  500.0 8.7 %copy-start.55 = (bf16[1024,1536]{1,0:T(8,128)(2,1)S(1)}, bf16[1024,1536]{1,0:T(8,128)(2,1)}, u32[]{:S(2)}) copy-start(bf16[1024,1536]{1,0:T(8,128)(2,1)} %get-tuple-element.24) | copy-start | bytes 9437188
  508.2 5.3 copy-start.12
  508.2 5.3 copy-start.19
  508.2 5.2 collective-permute-start.10
  513.3 23.6 %copy-start.7 = (bf16[1024,512]{1,0:T(8,128)(2,1)S(1)}, bf16[1024,512]{1,0:T(8,128)(2,1)}, u32[]{:S(2)}) copy-start(bf16[1024,512]{1,0:T(8,128)(2,1)} %copy-done.6) | copy-start | bytes 3145732
  513.3 30.7 %collective-permute-start.17 = (bf16[1024,1024]{0,1:T(8,128)(2,1)}, bf16[1024,1024]{0,1:T(8,128)(2,1)}, u32[]{:S(2)}, u32[]{:S(2)}) collective-permute-start(bf16[1024,1024]{0,1:T(8,128)(2,1)} %fusion.52), channel_id=1, source_target_pairs={{0,2},{2,0},{1,3},{3,1},{4,6},{6,4},{5,7},{7,5},{8,10},{10,8},{9,1... | collective-permute-start | bytes 6291464 | tf_op jit(solution)/shard_map/ppermute | solution.py:193
  519.4 20.5 %copy-start.1 = (bf16[1024,512]{1,0:T(8,128)(2,1)S(1)}, bf16[1024,512]{1,0:T(8,128)(2,1)}, u32[]{:S(2)}) copy-start(bf16[1024,512]{1,0:T(8,128)(2,1)} %copy-done) | copy-start | bytes 3145732
  519.4 66.6 %collective-permute-start.11 = (bf16[1024,1024]{0,1:T(8,128)(2,1)}, bf16[1024,1024]{0,1:T(8,128)(2,1)}, u32[]{:S(2)}, u32[]{:S(2)}) collective-permute-start(bf16[1024,1024]{0,1:T(8,128)(2,1)} %add_convert_fusion.3), channel_id=1, source_target_pairs={{0,0},{1,2},{2,1},{3,3},{4,4},{5,6},{6,5},{7,7},{8,8},{9,10},{10,9... | collective-permute-start | bytes 6291464 | tf_op jit(solution)/shard_map/ppermute | solution.py:189
  544.0 7.8 copy-start.17
  554.5 252.6 %collective-permute-start.18 = (bf16[1024,1024]{0,1:T(8,128)(2,1)}, bf16[1024,1024]{0,1:T(8,128)(2,1)S(1)}, u32[]{:S(2)}, u32[]{:S(2)}) collective-permute-start(bf16[1024,1024]{0,1:T(8,128)(2,1)} %fusion.41), channel_id=1, source_target_pairs={{0,0},{1,2},{2,1},{3,3},{4,4},{5,6},{6,5},{7,7},{8,8},{9,10},{10,9... | collective-permute-start | bytes 6291464 | tf_op jit(solution)/shard_map/ppermute | solution.py:189
  557.2 252.4 %collective-permute-start.21 = (bf16[64,2048]{1,0:T(8,128)(2,1)}, bf16[64,2048]{1,0:T(8,128)(2,1)S(1)}, u32[]{:S(2)}, u32[]{:S(2)}) collective-permute-start(bf16[64,2048]{1,0:T(8,128)(2,1)} %reduce-scatter.9.cloned.1.call-done), channel_id=1, source_target_pairs={{0,0},{1,2},{2,1},{3,3},{4,4},{5,6},{6,5},{7,7},{8,8},{9,10},{10,9... | collective-permute-start | bytes 786440 | tf_op jit(solution)/shard_map/ppermute | solution.py:189
  584.2 226.2 %collective-permute-start.22 = (bf16[128,1024]{1,0:T(8,128)(2,1)}, bf16[128,1024]{1,0:T(8,128)(2,1)S(1)}, u32[]{:S(2)}, u32[]{:S(2)}) collective-permute-start(bf16[128,1024]{1,0:T(8,128)(2,1)} %reduce-scatter.11.cloned.1.call-done), channel_id=1, source_target_pairs={{0,0},{1,2},{2,1},{3,3},{4,4},{5,6},{6,5},{7,7},{8,8},{9,10},{10,9... | collective-permute-start | bytes 786440 | tf_op jit(solution)/shard_map/ppermute | solution.py:189
  724.1 87.1 %collective-permute-start.19 = (bf16[64,1536]{1,0:T(8,128)(2,1)}, bf16[64,1536]{1,0:T(8,128)(2,1)S(1)}, u32[]{:S(2)}, u32[]{:S(2)}) collective-permute-start(bf16[64,1536]{1,0:T(8,128)(2,1)} %reduce-scatter.5.cloned.1.call-done), channel_id=1, source_target_pairs={{0,0},{1,2},{2,1},{3,3},{4,4},{5,6},{6,5},{7,7},{8,8},{9,10},{10,9... | collective-permute-start | bytes 589832 | tf_op jit(solution)/shard_map/ppermute | solution.py:189
  804.3 2.1 collective-permute-start.20
  (26 other events, 68.2 us)
Sparse Core Ops, SparseCore 0:
  11.3 80.4 all-gather.4
  95.1 54.5 all-gather.6
  153.0 75.1 all-gather.8
  231.4 74.1 all-gather.10
  375.5 93.8 reduce-scatter.8
  471.5 112.6 reduce-scatter.10
  589.1 134.9 reduce-scatter.4
  726.4 77.8 reduce-scatter.6

commit v2 on v1

--- a/solution.py
+++ b/solution.py
@@ -193,6 +193,35 @@
     return lax.ppermute(a, "c", [(0, 1), (1, 0)])
 
 
+def rank_pairs(ranks, bit):
+    return [(r, r ^ (1 << bit)) for r in range(ranks)]
+
+
+def halving_sum(total, ranks, order):
+    rank = lax.axis_index(WEIGHT_AXES)
+    rows, columns = total.shape[0] // ranks, total.shape[1]
+    left = list(range(ranks.bit_length() - 1))
+    for bit in order:
+        low = 1 << left.index(bit)
+        left.remove(bit)
+        view = total.reshape(-1, 2, low * rows, columns)
+        mine = (rank >> bit) & 1
+        sent = lax.dynamic_index_in_dim(view, 1 - mine, 1, keepdims=False)
+        kept = lax.dynamic_index_in_dim(view, mine, 1, keepdims=False)
+        theirs = lax.ppermute(sent.astype(BF16), WEIGHT_AXES, rank_pairs(ranks, bit))
+        total = kept.astype(F32) + theirs.astype(F32)
+        if left:
+            total = total.astype(BF16)
+        total = total.reshape(-1, columns)
+    return total
+
+
+def doubling_sum(values, ranks):
+    for bit in range(ranks.bit_length() - 1):
+        values = values + lax.ppermute(values, WEIGHT_AXES, rank_pairs(ranks, bit))
+    return values
+
+
 def normalize(row_values):
     row_mean = jnp.mean(row_values, axis=-1, keepdims=True)
     centred = row_values - row_mean
@@ -242,11 +271,21 @@
             return [values[0] + theirs[1], values[1] + theirs[0]]
         return [lax.psum(values[0], PART_AXES)]
 
-    def weight_grad(left, right):
-        total = sum(dot(a, b, ((0,), (0,))) for a, b in zip(left, right))
-        return lax.psum_scatter(
-            total.astype(BF16), WEIGHT_AXES, scatter_dimension=0, tiled=True
-        )
+    def product(left, right):
+        return sum(dot(a, b, ((0,), (0,))) for a, b in zip(left, right)).astype(BF16)
+
+    def scatter(total):
+        return lax.psum_scatter(total, WEIGHT_AXES, scatter_dimension=0, tiled=True)
+
+    def scatter_fast(total, splits):
+        bits = list(range(ranks.bit_length() - 1))
+        orders = [bits, [bits[1], bits[0]] + bits[2:]]
+        width = total.shape[1] // splits
+        pieces = [
+            halving_sum(total[:, n * width : (n + 1) * width], ranks, orders[n % 2])
+            for n in range(splits)
+        ]
+        return pieces[0] if splits == 1 else jnp.concatenate(pieces, axis=1)
 
     core = lax.axis_index("c")
     ranks = lax.axis_size("p") * lax.axis_size("h")
@@ -317,7 +356,9 @@
     cotangent = exchange(cotangent)
     grad_top = cotangent.astype(F32)
     grad_full = spread_tokens(cotangent)
-    grad_down = weight_grad(fed_down, grad_full)
+    grad_down = product(fed_down, grad_full)
+    grad_down, grad_full = lax.optimization_barrier((grad_down, grad_full))
+    grad_down = scatter(grad_down)
     grad_fed = [dot(g, w_down, ((1,), (1,))) for g in grad_full]
     grad_gmid = sum(jnp.sum(g * n, axis=0) for g, n in zip(grad_fed, norm_mid))
     scaled_mid = [g * g_mid for g in grad_fed]
@@ -338,14 +379,14 @@
         normal_cdf = 0.5 * (1.0 + lax.erf(u * 0.7071067811865476))
         density = jnp.exp(-0.5 * u * u) * 0.3989422804014327
         grad_upper.append((grad_active * (normal_cdf + u * density)).astype(BF16))
-    grad_up = weight_grad(gathered_ffn, grad_upper)
+    grad_up = scatter(product(gathered_ffn, grad_upper))
     grad_entry_ffn = collect_tokens(lambda t: dot(grad_upper[t], w_up, ((1,), (1,))))
     grad_gffn = jnp.sum(grad_entry_ffn * norm_ffn, axis=0)
     grad_middle = grad_top + norm_back(grad_entry_ffn * g_ffn, norm_ffn, inv_ffn)
     grad_gpost = jnp.sum(grad_middle * norm_post, axis=0)
     grad_mixed = norm_back(grad_middle * g_post, norm_post, inv_post).astype(BF16)
     grad_mfull = spread_tokens(grad_mixed)
-    grad_mix = weight_grad(scaled, grad_mfull)
+    grad_mix = scatter_fast(product(scaled, grad_mfull), 1)
     grad_scaled = [dot(g, w_mix, ((1,), (1,))) for g in grad_mfull]
     grad_heads = sum(
         jnp.sum(jnp.sum(g * a.astype(F32), axis=0).reshape(-1, HD), axis=1)
@@ -353,34 +394,35 @@
     )
     grad_attended = [(g * column_scale).astype(BF16) for g in grad_scaled]
     grad_proj = attn_backward(offs, projected, grad_attended, attended, lse)
-    grad_wproj = weight_grad(gathered, grad_proj)
+    grad_wproj = scatter_fast(product(gathered, grad_proj), 2)
     grad_entry_attn = collect_tokens(lambda t: dot(grad_proj[t], w_proj, ((1,), (1,))))
     grad_gattn = jnp.sum(grad_entry_attn * norm_attn, axis=0)
     grad_inputs = grad_middle + norm_back(grad_entry_attn * g_attn, norm_attn, inv_attn)
     grad_inputs = exchange(grad_inputs.astype(BF16))
 
-    slot = lax.axis_index(PART_AXES)
-    slots = lax.axis_size(PART_AXES)
-    own = jnp.concatenate([grad_gmid, grad_heads])
-    placed = jnp.where(jnp.arange(slots)[:, None] == slot, own[None, :], 0.0).reshape(-1)
-    sums = lax.psum(jnp.concatenate([grad_gattn, grad_gpost, grad_gffn, placed]), ALL_AXES)
+    gains = jnp.concatenate([grad_gattn, grad_gpost, grad_gffn])
+    own = doubling_sum(jnp.concatenate([gains, grad_gmid, grad_heads]), ranks)
     device_dp = lax.axis_index(("p", "c"))
     device_mp = lax.axis_index(("h", "l"))
-    short = depth // slots
+    if paired:
+        theirs = other_core(own)
+        gains = own[: 3 * model] + theirs[: 3 * model]
+        own = jnp.where(core == lax.axis_index("h"), own, theirs)[3 * model :]
+    else:
+        gains = lax.psum(own[: 3 * model], PART_AXES)
+        own = exchange(own[3 * model :])
+    short = depth // lax.axis_size(PART_AXES)
     starts = device_dp * depth + device_mp * short
     gains = [
-        lax.dynamic_slice_in_dim(sums, n * model + starts, short) for n in range(3)
+        lax.dynamic_slice_in_dim(gains, n * model + starts, short) for n in range(3)
     ]
-    base = 3 * model + device_mp * own.shape[0]
-    grad_mid = lax.dynamic_slice_in_dim(sums, base + device_dp * mid_rows, mid_rows)
-    grad_scale = lax.dynamic_slice_in_dim(
-        sums, base + grad_gmid.shape[0], grad_heads.shape[0]
-    )
+    grad_mid = lax.dynamic_slice_in_dim(own, device_dp * mid_rows, mid_rows)
+    grad_scale = own[grad_gmid.shape[0] :]
     return (
         output,
         grad_inputs,
-        exchange(grad_wproj).astype(F32).reshape(depth, 3, feat_width),
-        exchange(grad_mix).astype(F32),
+        exchange(grad_wproj.astype(BF16)).astype(F32).reshape(depth, 3, feat_width),
+        exchange(grad_mix.astype(BF16)).astype(F32),
         exchange(grad_up).astype(F32),
         exchange(grad_down).astype(F32),
         *gains,

time: 826 us -> 669 us (0.81)
  waiting for transfers between devices: 317 us -> 173 us
  blocking collectives: 41.4 us -> 0 us
  starting transfers between devices: 61.6 us -> 80.2 us
    reduce_scatter x4 -> x2, waiting for transfers between devices: 196 us -> 0.01 us  [scatter(): return lax.psum_scatter(total, WEIGHT_AXES, scatter_dimension=0, tiled=True)]
    ppermute x0 -> x16, waiting for transfers between devices: none -> 69.9 us  [the longest x12 36.6 us: halving_sum(): lax.ppermute(sent.astype(BF16), WEIGHT_AXES, rank_pairs(ranks, bit))]
    psum x1 -> x0, blocking collectives: 41.4 us -> none  [body(): lax.psum(jnp.concatenate([grad_gattn, grad_gpost, grad_gffn, placed]), AL...]
    ppermute x0 -> x16, starting transfers between devices: none -> 21.9 us  [the longest x12 18.3 us: halving_sum(): lax.ppermute(sent.astype(BF16), WEIGHT_AXES, rank_pairs(ranks, bit))]
    all_gather x4, waiting for transfers between devices: 120 us -> 101 us  [gather(): return lax.all_gather(a, WEIGHT_AXES, axis=0, tiled=True)]
    convert_element_type x1 -> x12, other arithmetic: 0.67 us -> 9.32 us  [the longest x9 4.5 us: halving_sum(): total = total.astype(BF16)]
    unnamed x122 -> x133, local copies, waits for them, and re-layouts: 22.1 us -> 22.5 us
  transfers between devices with their start and end apart: 31 -> 46, of which waited for: 8 -> 15; matrix products, arithmetic and copies ran while one was open for 26% -> 38% of each run, Pallas kernels for 12% -> 15%
where the time goes in v2:
time: 669 us; the launch traced here: 659 us
  matrix products  207 us (31%)
  waiting for transfers between devices  173 us (26%)
  Pallas kernels  102 us (15%)
  starting transfers between devices  80.2 us (12%)
  other arithmetic  52 us (8%)
  local copies, waits for them, and re-layouts  29.4 us (4%)
  between operations  15.7 us (2%)
    dot_general x24, matrix products, dot(): return lax.dot_general(a, b, (dims, ((), ())), preferred_element_type=F32)  207 us
    all_gather x4, waiting for transfers between devices, gather(): return lax.all_gather(a, WEIGHT_AXES, axis=0, tiled=True)  101 us
    pallas_call x1, Pallas kernels, attn_backward(): pl.pallas_call(functools.partial(attn_backward_kernel, chunks, total // B...  60.3 us
    ppermute x13, starting transfers between devices, exchange(): return lax.ppermute(a, ('c', 'h'), [(0, 0), (1, 2), (2, 1), (3, 3)])  47.7 us
    pallas_call x1, Pallas kernels, attn_forward(): pl.pallas_call(functools.partial(attn_forward_kernel, chunks, total // BL...  41.6 us
    ppermute x12, waiting for transfers between devices, halving_sum(): lax.ppermute(sent.astype(BF16), WEIGHT_AXES, rank_pairs(ranks, bit))  36.6 us
    ppermute x4, waiting for transfers between devices, doubling_sum(): values = values + lax.ppermute(values, WEIGHT_AXES, rank_pairs(ranks, bit))  33.3 us
    unnamed x133, local copies, waits for them, and re-layouts  22.5 us
  transfers between devices with their start and end apart: 46, of which 15 were waited for; matrix products, arithmetic and copies ran while one was open for 38% of the time, Pallas kernels for 15%

profile of v2, /device:TPU:0, one launch (start us, length us, event | category | flops | bytes accessed | tf_op | source)
XLA Modules:
  0.0 659.2 jit_solution(7036719556482134223)
XLA Ops:
  12.8 3.9 copy.71
  16.8 2.2 collective-permute-start
  21.5 70.2 %all-gather.5.cloned.1.call-done = bf16[1024,1664]{1,0:T(8,128)(2,1)} async-done(((bf16[64,1664]{1,0:T(8,128)(2,1)}), bf16[1024,1664]{1,0:T(8,128)(2,1)}) %all-gather.5.cloned.1.call-update) | async-done | bytes 3407888 | tf_op jit(solution)/shard_map/all_gather | solution.py:311
  93.1 2.0 fusion.36
  95.8 3.9 copy.76
  99.7 17.3 %collective-permute-start.12 = (bf16[1024,1024]{0,1:T(8,128)(2,1)}, bf16[1024,1024]{0,1:T(8,128)(2,1)}, u32[]{:S(2)}, u32[]{:S(2)}) collective-permute-start(bf16[1024,1024]{0,1:T(8,128)(2,1)} %copy.76), channel_id=1, source_target_pairs={{0,0},{1,2},{2,1},{3,3},{4,4},{5,6},{6,5},{7,7},{8,8},{9,10},{10,9... | collective-permute-start | bytes 6291464 | tf_op jit(solution)/shard_map/ppermute | solution.py:189
  117.3 7.8 %convolution_convert_fusion.1.refs_0_.refs_2_.refs_4_ = bf16[1024,1536]{1,0:T(8,128)(2,1)} fusion(bf16[1024,1024]{0,1:T(8,128)(2,1)} %fusion.36, bf16[1024,1664]{1,0:T(8,128)(2,1)} %all-gather.5.cloned.1.call-done), kind=kOutput, calls=%fused_computation.98 | convolution fusion | flops 3222798336 | bytes 8388608 | tf_op jit(solution)/shard_map/dot_general | solution.py:22
  125.2 6.6 %convolution_convert_fusion.refs_1_.refs_3_.refs_5_ = bf16[1024,1536]{1,0:T(8,128)(2,1)} fusion(bf16[1024,1024]{0,1:T(8,128)(2,1)} %collective-permute-done.2, bf16[1024,1664]{1,0:T(8,128)(2,1)S(1)} %copy-done.51), kind=kOutput, calls=%fused_computation.97 | convolution fusion | flops 3222798336 | bytes 8388608 | tf_op jit(solution)/shard_map/dot_general | solution.py:22
  131.8 41.6 %attn_forward.1 = (bf16[1024,512]{1,0:T(8,128)(2,1)S(1)}, bf16[1024,512]{1,0:T(8,128)(2,1)S(1)}, bf16[1024,512]{1,0:T(8,128)(2,1)S(1)}, bf16[1024,512]{1,0:T(8,128)(2,1)S(1)}, f32[8,8,2048]{2,1,0:T(8,128)S(1)}) custom-call(s32[2]{0:T(128)S(1)} %pad_add_fusion.offs, bf16[1024,1536]{1,0:T(8,128)(2,1)} %convolution_convert_fusion.1.refs_0_.refs_2_.refs_4_, ...), custom_call_target="tpu_custom_call" | custom-call | tf_op jit(solution)/shard_map/attn_forward/pallas_call | solution.py:78
  175.2 5.3 convolution_convert_fusion.4
  182.2 9.1 %collective-permute-start.13 = (bf16[1024,1024]{0,1:T(8,128)(2,1)}, bf16[1024,1024]{0,1:T(8,128)(2,1)}, u32[]{:S(2)}, u32[]{:S(2)}) collective-permute-start(bf16[1024,1024]{0,1:T(8,128)(2,1)} %collective-permute-done.12), channel_id=1, source_target_pairs={{0,2},{2,0},{1,3},{3,1},{4,6},{6,4},{5,7},{7,5},{8,10},{10,8},{9,1... | collective-permute-start | bytes 6291464 | tf_op jit(solution)/shard_map/ppermute | solution.py:193
  191.5 3.4 fusion.85
  195.4 2.6 copy-done.13
  199.4 2.2 multiply_convert_fusion.3
  201.6 26.8 %all-gather.9.cloned.1.call-done = bf16[1024,2048]{1,0:T(8,128)(2,1)} async-done(((bf16[64,2048]{1,0:T(8,128)(2,1)}), bf16[1024,2048]{1,0:T(8,128)(2,1)}) %all-gather.9.cloned.1.call-update) | async-done | bytes 4194320 | tf_op jit(solution)/shard_map/all_gather | solution.py:311
  228.4 26.1 %fusion.77 = (f32[1024]{0:T(1024)S(1)}, f32[1024]{0:T(1024)S(1)}, f32[1024,2048]{1,0:T(8,128)S(1)}, f32[1024,2048]{1,0:T(8,128)}) fusion(bf16[1024,1024]{0,1:T(8,128)(2,1)} %multiply_convert_fusion.3, bf16[1024,2048]{1,0:T(8,128)(2,1)} %all-gather.9.cloned.1.call-done), kind=kOutput, calls=%fused_computation.209 | convolution fusion | flops 4435474432 | bytes 23076864 | tf_op jit(solution)/shard_map/dot_general | solution.py:22
  254.5 26.2 %fusion.78 = (f32[1024]{0:T(1024)S(1)}, f32[1024]{0:T(1024)S(1)}, f32[1024,2048]{1,0:T(8,128)S(1)}, f32[1024,2048]{1,0:T(8,128)}) fusion(bf16[1024,1024]{0,1:T(8,128)(2,1)} %collective-permute-done.7, bf16[1024,2048]{1,0:T(8,128)(2,1)S(1)} %copy-done.54), kind=kOutput, calls=%fused_computation.210 | convolution fusion | flops 4435474432 | bytes 23076864 | tf_op jit(solution)/shard_map/dot_general | solution.py:22
  282.1 4.1 multiply_convert_fusion.1
  286.3 7.9 %fusion.86 = f32[2048,1024]{1,0:T(8,128)S(1)} fusion(bf16[1024,2048]{1,0:T(8,128)(2,1)S(1)} %get-tuple-element.135, bf16[1024,1024]{0,1:T(8,128)(2,1)} %collective-permute-done.12), kind=kOutput, calls=%fused_computation.216 | convolution fusion | flops 4294967296 | bytes 14680064 | tf_op jit(solution)/shard_map/dot_general | solution.py:22
  294.2 8.0 %add_convert_fusion.1 = bf16[2048,1024]{1,0:T(8,128)(2,1)} fusion(f32[2048,1024]{1,0:T(8,128)S(1)} %fusion.86, bf16[1024,2048]{1,0:T(8,128)(2,1)S(1)} %copy-done.20, bf16[1024,1024]{0,1:T(8,128)(2,1)} %collective-permute-done.13), kind=kOutput, calls=%fused_computation.25 | convolution fusion | flops 4299161600 | bytes 18874368 | tf_op jit(solution)/shard_map/dot_general | solution.py:22
  302.2 3.6 all-gather.11.cloned.1.call-done
  305.8 10.6 %fusion.87 = f32[1024,2048]{1,0:T(8,128)} fusion(bf16[1024,1024]{0,1:T(8,128)(2,1)} %collective-permute-done.13, bf16[2048,1024]{1,0:T(8,128)(2,1)} %all-gather.11.cloned.1.call-done), kind=kOutput, calls=%fused_computation.217 | convolution fusion | flops 4294967296 | bytes 14680064 | tf_op jit(solution)/shard_map/dot_general | solution.py:22
  316.4 19.1 %multiply_reduce_fusion.1 = (f32[2048]{0:T(1024)S(1)}, f32[1024]{0:T(1024)S(1)}, f32[1024]{0:T(1024)S(1)}, f32[1024]{0:T(1024)S(1)}, f32[1024]{0:T(1024)S(1)}, /*index=5*/f32[2048]{0:T(1024)S(1)}, f32[1024,2048]{1,0:T(8,128)}) fusion(f32[1024,2048]{1,0:T(8,128)} %copy-done.17, f32[1024]{0:T(1024)S(1)} %add_rsqrt_fusion.1, f32[1024]{0:T(1024)S(1)} %bitcast.186, ...), kind=kOutput, calls=%fused_computation.21 | convolution fusion | flops 4328513536 | bytes 39903232 | tf_op jit(solution)/shard_map/dot_general | solution.py:22
  336.9 21.5 %fusion.9 = (bf16[1024,2048]{1,0:T(8,128)(2,1)}, bf16[1024,2048]{1,0:T(8,128)(2,1)S(1)}) fusion(f32[1024,2048]{1,0:T(8,128)} %get-tuple-element.143, f32[1024,2048]{1,0:T(8,128)} %get-tuple-element.145, f32[1024,2048]{1,0:T(8,128)} %copy-done.17, f32[1024]{0:T(1024)S(1)} %bitcast.193, f32[1024]{0:T(1024)S(1)} %bitcast.192, f32[2048]{0:T(1024)S(1)} %slice_bitcast_fusion.3, ...), kind=kLoop, calls=%fused_computation.13 | loop fusion | flops 71303168 | bytes 58761216 | tf_op jit(solution)/shard_map/convert_element_type | solution.py:381
  358.4 5.8 convolution_convert_fusion.2
  364.5 9.5 %convolution_convert_fusion.3 = bf16[1024,1024]{0,1:T(8,128)(2,1)} fusion(bf16[1024,2048]{1,0:T(8,128)(2,1)} %get-tuple-element.136, bf16[2048,1024]{1,0:T(8,128)(2,1)} %all-gather.11.cloned.1.call-done), kind=kOutput, calls=%fused_computation.115 | convolution fusion | flops 4296015872 | bytes 10485760 | tf_op jit(solution)/shard_map/dot_general | solution.py:22
  374.4 9.0 %fusion.90 = f32[1024,2048]{1,0:T(8,128)} fusion(bf16[1024,1024]{0,1:T(8,128)(2,1)} %collective-permute-done.7, bf16[1024,2048]{1,0:T(8,128)(2,1)S(1)} %copy-done.23), kind=kOutput, calls=%fused_computation.220 | convolution fusion | flops 4294967296 | bytes 14680064 | tf_op jit(solution)/shard_map/dot_general | solution.py:22
  383.5 7.0 %multiply_reduce_fusion.8 = (f32[1024]{0:T(1024)S(1)}, f32[1024]{0:T(1024)S(1)}, f32[1024]{0:T(1024)S(1)}, f32[1024,1024]{0,1:T(8,128)S(1)}) fusion(f32[1024,1024]{0,1:T(8,128)S(1)} %copy-done.11, f32[1024]{0:T(1024)S(1)} %copy-done.50, f32[1024]{0:T(1024)S(1)} %copy-done.40, f32[1024]{0:T(1024)S(1)} %copy-done.48, ...), kind=kOutput, calls=%fused_computation.82 | convolution fusion | flops 4305449984 | bytes 18898944 | tf_op jit(solution)/shard_map/dot_general | solution.py:22
  390.6 4.8 multiply_reduce_fusion.9
  395.4 2.6 multiply_convert_fusion.2
  398.2 9.2 %add_convert_fusion = bf16[1024,2048]{1,0:T(8,128)(2,1)} fusion(f32[1024,2048]{1,0:T(8,128)} %fusion.90, bf16[1024,1024]{0,1:T(8,128)(2,1)} %multiply_convert_fusion.3, bf16[1024,2048]{1,0:T(8,128)(2,1)S(1)} %copy-done.21), kind=kOutput, calls=%fused_computation.22 | convolution fusion | flops 4299161600 | bytes 18874368 | tf_op jit(solution)/shard_map/dot_general | solution.py:22
  407.4 11.4 %add_convert_fusion.3 = bf16[1024,1024]{0,1:T(8,128)(2,1)} fusion(f32[1024,1024]{0,1:T(8,128)} %copy-done.10, bf16[1024,1024]{0,1:T(8,128)(2,1)} %collective-permute-done.10, bf16[1024,2048]{1,0:T(8,128)(2,1)} %copy-done.19, bf16[2048,1024]{1,0:T(8,128)(2,1)} %all-gather.11.cloned.1.call-done), kind=kOutput, calls=%fused_computation.90 | convolution fusion | flops 4299161600 | bytes 16777216 | tf_op jit(solution)/shard_map/dot_general | solution.py:22
  418.9 17.2 %collective-permute-start.11 = (bf16[1024,1024]{0,1:T(8,128)(2,1)}, bf16[1024,1024]{0,1:T(8,128)(2,1)}, u32[]{:S(2)}, u32[]{:S(2)}) collective-permute-start(bf16[1024,1024]{0,1:T(8,128)(2,1)} %add_convert_fusion.3), channel_id=1, source_target_pairs={{0,0},{1,2},{2,1},{3,3},{4,4},{5,6},{6,5},{7,7},{8,8},{9,10},{10,9... | collective-permute-start | bytes 6291464 | tf_op jit(solution)/shard_map/ppermute | solution.py:189
  436.1 4.0 multiply_reduce_fusion.18
  440.4 3.0 fusion.89
  443.4 3.0 add_convert_fusion.4
  446.5 3.9 multiply_reduce_fusion.17
  450.4 60.3 %attn_backward.1 = (bf16[1024,1536]{1,0:T(8,128)(2,1)}, bf16[1024,1536]{1,0:T(8,128)(2,1)}) custom-call(s32[2]{0:T(128)} %copy-done.5, bf16[1024,1536]{1,0:T(8,128)(2,1)} %convolution_convert_fusion.1.refs_0_.refs_2_.refs_4_, bf16[1024,1536]{1,0:T(8,128)(2,1)} %convolution_convert_fusion.refs_1_.refs_3_.refs_5_, ...), custom_call_target="tpu_custom_call" | custom-call | tf_op jit(solution)/shard_map/attn_backward/pallas_call | solution.py:162
  510.8 6.1 fusion.88
  516.9 5.3 add_convert_fusion.2
  523.3 2.0 collective-permute-start.19
  529.4 4.9 fusion.52
  534.6 25.2 %collective-permute-done.29 = bf16[4,32,1024]{2,1,0:T(8,128)(2,1)} collective-permute-done((bf16[4,32,1024]{2,1,0:T(8,128)(2,1)S(1)}, bf16[4,32,1024]{2,1,0:T(8,128)(2,1)}, u32[]{:S(2)}, u32[]{:S(2)}) %collective-permute-start.29) | collective-permute-done | bytes 262176 | tf_op jit(solution)/shard_map/ppermute | solution.py:211
  562.4 2.3 collective-permute-start.20
  564.7 1.5 fusion.55
  567.5 2.1 collective-permute-start.31
  569.6 4.5 collective-permute-done.20
  575.7 1.7 collective-permute-done.24
  577.6 1.7 collective-permute-start.25
  579.3 2.4 collective-permute-done.21
  581.7 2.8 collective-permute-start.22
  585.9 2.5 collective-permute-start.26
  588.4 1.6 collective-permute-done.22
  590.1 4.1 fusion.42
  594.3 2.7 fusion.41
  596.9 2.2 collective-permute-start.18
  601.0 23.9 %collective-permute-done.35 = f32[5128]{0:T(1024)S(1)} collective-permute-done((f32[5128]{0:T(1024)S(1)}, f32[5128]{0:T(1024)S(1)}, u32[]{:S(2)}, u32[]{:S(2)}) %collective-permute-start.35) | collective-permute-done | bytes 20544 | tf_op jit(solution)/shard_map/ppermute | solution.py:221
  624.9 2.3 collective-permute-start.36
  629.0 3.8 collective-permute-done.37
  633.0 4.5 collective-permute-done.38
  637.6 3.9 copy.83
  644.1 1.6 collective-permute-start.34
  645.7 1.6 collective-permute-start.33
  647.9 2.5 copy.84
  (292 shorter events, 41.0 us)
Async XLA Ops:
  7.2 84.6 %all-gather.5.cloned.1.call-start = ((), (), s32[]{:S(2)}) async-start(), calls=%async_computation.2 | async-start | bytes 3620864 | tf_op jit(solution)/shard_map/all_gather | solution.py:311
  9.2 0.7 collective-permute-start.1
  10.6 164.6 %all-gather.7.cloned.1.call-start = ((), (), s32[]{:S(2)}) async-start(), calls=%async_computation.3 | async-start | bytes 1114112 | tf_op jit(solution)/shard_map/all_gather | solution.py:311
  10.6 1.5 collective-permute-start.4
  12.8 215.6 %all-gather.9.cloned.1.call-start = ((), (), s32[]{:S(2)}) async-start(), calls=%async_computation.4 | async-start | bytes 4456448 | tf_op jit(solution)/shard_map/all_gather | solution.py:311
  16.8 3.7 collective-permute-start
  19.0 0.7 collective-permute-start.6
  20.4 285.4 %all-gather.11.cloned.1.call-start = ((), (), s32[]{:S(2)}) async-start(), calls=%async_computation.5 | async-start | bytes 4456448 | tf_op jit(solution)/shard_map/all_gather | solution.py:311
  20.5 74.6 %copy-start.12 = (bf16[1024,1024]{0,1:T(8,128)(2,1)}, bf16[1024,1024]{0,1:T(8,128)(2,1)S(1)}, u32[]{:S(2)}) copy-start(bf16[1024,1024]{0,1:T(8,128)(2,1)S(1)} %collective-permute-done) | copy-start | bytes 6291460
  20.9 74.2 %copy-start.62 = (bf16[8]{0:T(256)(128)(2,1)S(1)}, bf16[8]{0:T(256)(128)(2,1)}, u32[]{:S(2)}) copy-start(bf16[8]{0:T(256)(128)(2,1)} %param.20) | copy-start | bytes 52
  20.9 78.8 %copy-start.36 = (f32[1024]{0:T(1024)}, f32[1024]{0:T(1024)S(1)}, u32[]{:S(2)}) copy-start(f32[1024]{0:T(1024)S(1)} %broadcast_multiply_fusion.8) | copy-start | bytes 12292
  21.5 78.2 %copy-start.43 = (f32[1024]{0:T(1024)}, f32[1024]{0:T(1024)S(1)}, u32[]{:S(2)}) copy-start(f32[1024]{0:T(1024)S(1)} %add_rsqrt_fusion.4) | copy-start | bytes 12292
  95.1 30.1 %collective-permute-start.2 = (bf16[1024,1024]{0,1:T(8,128)(2,1)}, bf16[1024,1024]{0,1:T(8,128)(2,1)}, u32[]{:S(2)}, u32[]{:S(2)}) collective-permute-start(bf16[1024,1024]{0,1:T(8,128)(2,1)} %fusion.36), channel_id=1, source_target_pairs={{0,2},{2,0},{1,3},{3,1},{4,6},{6,4},{5,7},{7,5},{8,10},{10,8},{9,1... | collective-permute-start | bytes 6291464 | tf_op jit(solution)/shard_map/ppermute | solution.py:193
  95.1 22.1 %collective-permute-start.3 = (bf16[8]{0:T(256)(128)(2,1)S(1)}, bf16[8]{0:T(256)(128)(2,1)S(1)}, u32[]{:S(2)}, u32[]{:S(2)}) collective-permute-start(bf16[8]{0:T(256)(128)(2,1)S(1)} %copy-done.62), channel_id=1, source_target_pairs={{0,0},{1,2},{2,1},{3,3},{4,4},{5,6},{6,5},{7,7},{8,8},{9,10},{10,9... | collective-permute-start | bytes 56 | tf_op jit(solution)/shard_map/ppermute | solution.py:189
  99.7 82.5 %collective-permute-start.12 = (bf16[1024,1024]{0,1:T(8,128)(2,1)}, bf16[1024,1024]{0,1:T(8,128)(2,1)}, u32[]{:S(2)}, u32[]{:S(2)}) collective-permute-start(bf16[1024,1024]{0,1:T(8,128)(2,1)} %copy.76), channel_id=1, source_target_pairs={{0,0},{1,2},{2,1},{3,3},{4,4},{5,6},{6,5},{7,7},{8,8},{9,10},{10,9... | collective-permute-start | bytes 6291464 | tf_op jit(solution)/shard_map/ppermute | solution.py:189
  175.2 16.3 %copy-start = (bf16[1024,512]{1,0:T(8,128)(2,1)}, bf16[1024,512]{1,0:T(8,128)(2,1)S(1)}, u32[]{:S(2)}) copy-start(bf16[1024,512]{1,0:T(8,128)(2,1)S(1)} %get-tuple-element.21) | copy-start | bytes 3145732
  175.2 260.9 %copy-start.2 = (bf16[1024,512]{1,0:T(8,128)(2,1)}, bf16[1024,512]{1,0:T(8,128)(2,1)S(1)}, u32[]{:S(2)}) copy-start(bf16[1024,512]{1,0:T(8,128)(2,1)S(1)} %get-tuple-element.25.refs_8_) | copy-start | bytes 3145732
  175.2 271.3 %copy-start.3 = (bf16[1024,512]{1,0:T(8,128)(2,1)}, bf16[1024,512]{1,0:T(8,128)(2,1)S(1)}, u32[]{:S(2)}) copy-start(bf16[1024,512]{1,0:T(8,128)(2,1)S(1)} %get-tuple-element.26.refs_9_) | copy-start | bytes 3145732
  180.5 11.0 %collective-permute-start.5 = (bf16[1024,1024]{0,1:T(8,128)(2,1)}, bf16[1024,1024]{0,1:T(8,128)(2,1)}, u32[]{:S(2)}, u32[]{:S(2)}) collective-permute-start(bf16[1024,1024]{0,1:T(8,128)(2,1)} %convolution_convert_fusion.4), channel_id=1, source_target_pairs={{0,2},{2,0},{1,3},{3,1},{4,6},{6,4},{5,7},{7,5},{8,10},{10,8},{9,1... | collective-permute-start | bytes 6291464 | tf_op jit(solution)/shard_map/ppermute | solution.py:193
  180.5 0.7 collective-permute-start.9
  181.9 462.2 %reduce-scatter.5.cloned.1.call-start = ((), (), s32[]{:S(2)}) async-start(), calls=%async_computation.7 | async-start | bytes 4456448 | tf_op jit(solution)/shard_map/reduce_scatter | solution.py:278
  182.2 112.0 %collective-permute-start.13 = (bf16[1024,1024]{0,1:T(8,128)(2,1)}, bf16[1024,1024]{0,1:T(8,128)(2,1)}, u32[]{:S(2)}, u32[]{:S(2)}) collective-permute-start(bf16[1024,1024]{0,1:T(8,128)(2,1)} %collective-permute-done.12), channel_id=1, source_target_pairs={{0,2},{2,0},{1,3},{3,1},{4,6},{6,4},{5,7},{7,5},{8,10},{10,8},{9,1... | collective-permute-start | bytes 6291464 | tf_op jit(solution)/shard_map/ppermute | solution.py:193
  199.4 55.1 %copy-start.49 = (f32[1024]{0:T(1024)}, f32[1024]{0:T(1024)S(1)}, u32[]{:S(2)}) copy-start(f32[1024]{0:T(1024)S(1)} %add_rsqrt_fusion.2) | copy-start | bytes 12292
  201.6 52.9 %collective-permute-start.7 = (bf16[1024,1024]{0,1:T(8,128)(2,1)}, bf16[1024,1024]{0,1:T(8,128)(2,1)}, u32[]{:S(2)}, u32[]{:S(2)}) collective-permute-start(bf16[1024,1024]{0,1:T(8,128)(2,1)} %multiply_convert_fusion.3), channel_id=1, source_target_pairs={{0,2},{2,0},{1,3},{3,1},{4,6},{6,4},{5,7},{7,5},{8,10},{10,8},{9,1... | collective-permute-start | bytes 6291464 | tf_op jit(solution)/shard_map/ppermute | solution.py:193
  228.4 26.1 %copy-start.54 = (bf16[1024,2048]{1,0:T(8,128)(2,1)S(1)}, bf16[1024,2048]{1,0:T(8,128)(2,1)}, u32[]{:S(2)}) copy-start(bf16[1024,2048]{1,0:T(8,128)(2,1)} %all-gather.9.cloned.1.call-done) | copy-start | bytes 12582916
  254.5 27.6 %copy-start.17 = (f32[1024,2048]{1,0:T(8,128)}, f32[1024,2048]{1,0:T(8,128)S(1)}, u32[]{:S(2)}) copy-start(f32[1024,2048]{1,0:T(8,128)S(1)} %get-tuple-element.106) | copy-start | bytes 25165828
  280.8 1.2 collective-permute-start.8
  335.6 1.2 collective-permute-start.14
  335.7 310.0 %reduce-scatter.3.cloned.1.call-start = ((), (), s32[]{:S(2)}) async-start(), calls=%async_computation.6 | async-start | bytes 4456448 | tf_op jit(solution)/shard_map/reduce_scatter | solution.py:278
  336.9 21.5 %copy-start.55 = (bf16[1024,2048]{1,0:T(8,128)(2,1)S(1)}, bf16[1024,2048]{1,0:T(8,128)(2,1)}, u32[]{:S(2)}) copy-start(bf16[1024,2048]{1,0:T(8,128)(2,1)} %all-gather.9.cloned.1.call-done) | copy-start | bytes 12582916
  364.2 19.2 %collective-permute-start.15 = (bf16[1024,1024]{0,1:T(8,128)(2,1)}, bf16[1024,1024]{0,1:T(8,128)(2,1)}, u32[]{:S(2)}, u32[]{:S(2)}) collective-permute-start(bf16[1024,1024]{0,1:T(8,128)(2,1)} %convolution_convert_fusion.2), channel_id=1, source_target_pairs={{0,2},{2,0},{1,3},{3,1},{4,6},{6,4},{5,7},{7,5},{8,10},{10,8},{9,1... | collective-permute-start | bytes 6291464 | tf_op jit(solution)/shard_map/ppermute | solution.py:193
  374.1 33.4 %collective-permute-start.10 = (bf16[1024,1024]{0,1:T(8,128)(2,1)}, bf16[1024,1024]{0,1:T(8,128)(2,1)}, u32[]{:S(2)}, u32[]{:S(2)}) collective-permute-start(bf16[1024,1024]{0,1:T(8,128)(2,1)} %convolution_convert_fusion.3), channel_id=1, source_target_pairs={{0,2},{2,0},{1,3},{3,1},{4,6},{6,4},{5,7},{7,5},{8,10},{10,8},{9,1... | collective-permute-start | bytes 6291464 | tf_op jit(solution)/shard_map/ppermute | solution.py:193
  398.0 42.4 %collective-permute-start.16 = (bf16[1024,1024]{0,1:T(8,128)(2,1)}, bf16[1024,1024]{0,1:T(8,128)(2,1)}, u32[]{:S(2)}, u32[]{:S(2)}) collective-permute-start(bf16[1024,1024]{0,1:T(8,128)(2,1)} %multiply_convert_fusion.2), channel_id=1, source_target_pairs={{0,2},{2,0},{1,3},{3,1},{4,6},{6,4},{5,7},{7,5},{8,10},{10,8},{9,1... | collective-permute-start | bytes 6291464 | tf_op jit(solution)/shard_map/ppermute | solution.py:193
  407.4 28.7 %copy-start.25 = (bf16[512,1024]{1,0:T(8,128)(2,1)S(1)}, bf16[512,1024]{1,0:T(8,128)(2,1)}, u32[]{:S(2)}) copy-start(bf16[512,1024]{1,0:T(8,128)(2,1)} %all-gather.7.cloned.1.call-done) | copy-start | bytes 3145732
  418.9 218.7 %collective-permute-start.11 = (bf16[1024,1024]{0,1:T(8,128)(2,1)}, bf16[1024,1024]{0,1:T(8,128)(2,1)}, u32[]{:S(2)}, u32[]{:S(2)}) collective-permute-start(bf16[1024,1024]{0,1:T(8,128)(2,1)} %add_convert_fusion.3), channel_id=1, source_target_pairs={{0,0},{1,2},{2,1},{3,3},{4,4},{5,6},{6,5},{7,7},{8,8},{9,10},{10,9... | collective-permute-start | bytes 6291464 | tf_op jit(solution)/shard_map/ppermute | solution.py:189
  446.4 81.4 %collective-permute-start.28 = (bf16[8,32,1024]{2,1,0:T(8,128)(2,1)S(1)}, bf16[8,32,1024]{2,1,0:T(8,128)(2,1)S(1)}, u32[]{:S(2)}, u32[]{:S(2)}) collective-permute-start(bf16[8,32,1024]{2,1,0:T(8,128)(2,1)S(1)} %dynamic-slice_bitcast_fusion.2), channel_id=1, source_target_pairs={{0,1},{1,0},{4,5},{5,4},{8,9},{9,8},{12,13},{13,12},{16,17},{17,16... | collective-permute-start | bytes 1572872 | tf_op jit(solution)/shard_map/ppermute | solution.py:211
  523.3 37.6 %collective-permute-start.19 = (bf16[8,64,768]{2,1,0:T(8,128)(2,1)}, bf16[8,64,768]{2,1,0:T(8,128)(2,1)}, u32[]{:S(2)}, u32[]{:S(2)}) collective-permute-start(bf16[8,64,768]{2,1,0:T(8,128)(2,1)} %dynamic-slice_bitcast_fusion.1), channel_id=1, source_target_pairs={{0,1},{1,0},{4,5},{5,4},{8,9},{9,8},{12,13},{13,12},{16,17},{17,16... | collective-permute-start | bytes 2359304 | tf_op jit(solution)/shard_map/ppermute | solution.py:211
  526.3 38.4 %collective-permute-start.23 = (bf16[4,128,768]{2,1,0:T(8,128)(2,1)}, bf16[4,128,768]{2,1,0:T(8,128)(2,1)}, u32[]{:S(2)}, u32[]{:S(2)}) collective-permute-start(bf16[4,128,768]{2,1,0:T(8,128)(2,1)} %dynamic-slice_bitcast_fusion), channel_id=1, source_target_pairs={{0,4},{1,5},{4,0},{5,1},{8,12},{9,13},{12,8},{13,9},{16,20},{17,21... | collective-permute-start | bytes 2359304 | tf_op jit(solution)/shard_map/ppermute | solution.py:211
  528.8 30.9 %collective-permute-start.29 = (bf16[4,32,1024]{2,1,0:T(8,128)(2,1)S(1)}, bf16[4,32,1024]{2,1,0:T(8,128)(2,1)}, u32[]{:S(2)}, u32[]{:S(2)}) collective-permute-start(bf16[4,32,1024]{2,1,0:T(8,128)(2,1)S(1)} %dynamic-slice_bitcast_fusion.5), channel_id=1, source_target_pairs={{0,4},{1,5},{4,0},{5,1},{8,12},{9,13},{12,8},{13,9},{16,20},{17,21... | collective-permute-start | bytes 786440 | tf_op jit(solution)/shard_map/ppermute | solution.py:211
  534.5 55.5 %collective-permute-start.17 = (bf16[1024,1024]{0,1:T(8,128)(2,1)}, bf16[1024,1024]{0,1:T(8,128)(2,1)S(1)}, u32[]{:S(2)}, u32[]{:S(2)}) collective-permute-start(bf16[1024,1024]{0,1:T(8,128)(2,1)} %fusion.52), channel_id=1, source_target_pairs={{0,2},{2,0},{1,3},{3,1},{4,6},{6,4},{5,7},{7,5},{8,10},{10,8},{9,1... | collective-permute-start | bytes 6291464 | tf_op jit(solution)/shard_map/ppermute | solution.py:193
  560.9 6.5 collective-permute-start.30
  562.4 27.7 %copy-start.14 = (bf16[1024,1024]{0,1:T(8,128)(2,1)S(1)}, bf16[1024,1024]{0,1:T(8,128)(2,1)}, u32[]{:S(2)}) copy-start(bf16[1024,1024]{0,1:T(8,128)(2,1)} %copy-done.12) | copy-start | bytes 6291460
  562.4 27.7 %copy-start.37 = (f32[1024]{0:T(1024)S(1)}, f32[1024]{0:T(1024)}, u32[]{:S(2)}) copy-start(f32[1024]{0:T(1024)} %copy-done.36) | copy-start | bytes 12292
  562.4 27.7 %copy-start.42 = (f32[1024]{0:T(1024)S(1)}, f32[1024]{0:T(1024)}, u32[]{:S(2)}) copy-start(f32[1024]{0:T(1024)} %copy-done.41) | copy-start | bytes 12292
  562.4 27.7 %copy-start.44 = (f32[1024]{0:T(1024)S(1)}, f32[1024]{0:T(1024)}, u32[]{:S(2)}) copy-start(f32[1024]{0:T(1024)} %copy-done.43) | copy-start | bytes 12292
  562.4 27.7 %copy-start.53 = (bf16[1024,1664]{1,0:T(8,128)(2,1)S(1)}, bf16[1024,1664]{1,0:T(8,128)(2,1)}, u32[]{:S(2)}) copy-start(bf16[1024,1664]{1,0:T(8,128)(2,1)} %all-gather.5.cloned.1.call-done) | copy-start | bytes 10223620
  562.4 27.7 %copy-start.58 = (bf16[1024,1536]{1,0:T(8,128)(2,1)S(1)}, bf16[1024,1536]{1,0:T(8,128)(2,1)}, u32[]{:S(2)}) copy-start(bf16[1024,1536]{1,0:T(8,128)(2,1)} %get-tuple-element.28) | copy-start | bytes 9437188
  562.4 11.6 %collective-permute-start.20 = (bf16[4,64,768]{2,1,0:T(8,128)(2,1)S(1)}, bf16[4,64,768]{2,1,0:T(8,128)(2,1)S(1)}, u32[]{:S(2)}, u32[]{:S(2)}) collective-permute-start(bf16[4,64,768]{2,1,0:T(8,128)(2,1)S(1)} %dynamic-slice_bitcast_fusion.4), channel_id=1, source_target_pairs={{0,4},{1,5},{4,0},{5,1},{8,12},{9,13},{12,8},{13,9},{16,20},{17,21... | collective-permute-start | bytes 1179656 | tf_op jit(solution)/shard_map/ppermute | solution.py:211
  566.3 11.2 %collective-permute-start.24 = (bf16[4,64,768]{2,1,0:T(8,128)(2,1)S(1)}, bf16[4,64,768]{2,1,0:T(8,128)(2,1)S(1)}, u32[]{:S(2)}, u32[]{:S(2)}) collective-permute-start(bf16[4,64,768]{2,1,0:T(8,128)(2,1)S(1)} %dynamic-slice_bitcast_fusion.3), channel_id=1, source_target_pairs={{0,1},{1,0},{4,5},{5,4},{8,9},{9,8},{12,13},{13,12},{16,17},{17,16... | collective-permute-start | bytes 1179656 | tf_op jit(solution)/shard_map/ppermute | solution.py:211
  567.5 59.7 %collective-permute-start.31 = (bf16[1,32,1024]{2,1,0:T(8,128)(2,1)S(1)}, bf16[1,32,1024]{2,1,0:T(8,128)(2,1)S(1)}, u32[]{:S(2)}, u32[]{:S(2)}) collective-permute-start(bf16[1,32,1024]{2,1,0:T(8,128)(2,1)S(1)} %constant_dynamic-slice_fusion), channel_id=1, source_target_pairs={{0,16},{1,17},{4,20},{5,21},{8,24},{9,25},{12,28},{13,29},{16,0},{... | collective-permute-start | bytes 196616 | tf_op jit(solution)/shard_map/ppermute | solution.py:211
  574.2 7.4 %collective-permute-start.21 = (bf16[2,64,768]{2,1,0:T(8,128)(2,1)S(1)}, bf16[2,64,768]{2,1,0:T(8,128)(2,1)S(1)}, u32[]{:S(2)}, u32[]{:S(2)}) collective-permute-start(bf16[2,64,768]{2,1,0:T(8,128)(2,1)S(1)} %dynamic-slice_bitcast_fusion.7), channel_id=1, source_target_pairs={{0,8},{1,9},{4,12},{5,13},{8,0},{9,1},{12,4},{13,5},{16,24},{17,25... | collective-permute-start | bytes 589832 | tf_op jit(solution)/shard_map/ppermute | solution.py:211
  577.6 8.2 %collective-permute-start.25 = (bf16[2,64,768]{2,1,0:T(8,128)(2,1)S(1)}, bf16[2,64,768]{2,1,0:T(8,128)(2,1)S(1)}, u32[]{:S(2)}, u32[]{:S(2)}) collective-permute-start(bf16[2,64,768]{2,1,0:T(8,128)(2,1)S(1)} %dynamic-slice_bitcast_fusion.6), channel_id=1, source_target_pairs={{0,8},{1,9},{4,12},{5,13},{8,0},{9,1},{12,4},{13,5},{16,24},{17,25... | collective-permute-start | bytes 589832 | tf_op jit(solution)/shard_map/ppermute | solution.py:211
  581.7 8.3 %collective-permute-start.22 = (bf16[1,64,768]{2,1,0:T(8,128)(2,1)S(1)}, bf16[1,64,768]{2,1,0:T(8,128)(2,1)S(1)}, u32[]{:S(2)}, u32[]{:S(2)}) collective-permute-start(bf16[1,64,768]{2,1,0:T(8,128)(2,1)S(1)} %constant_dynamic-slice_fusion.2), channel_id=1, source_target_pairs={{0,16},{1,17},{4,20},{5,21},{8,24},{9,25},{12,28},{13,29},{16,0},{... | collective-permute-start | bytes 294920 | tf_op jit(solution)/shard_map/ppermute | solution.py:211
  585.9 13.2 %collective-permute-start.26 = (bf16[1,64,768]{2,1,0:T(8,128)(2,1)S(1)}, bf16[1,64,768]{2,1,0:T(8,128)(2,1)S(1)}, u32[]{:S(2)}, u32[]{:S(2)}) collective-permute-start(bf16[1,64,768]{2,1,0:T(8,128)(2,1)S(1)} %constant_dynamic-slice_fusion.1), channel_id=1, source_target_pairs={{0,16},{1,17},{4,20},{5,21},{8,24},{9,25},{12,28},{13,29},{16,0},{... | collective-permute-start | bytes 294920 | tf_op jit(solution)/shard_map/ppermute | solution.py:211
  596.9 51.0 %collective-permute-start.18 = (bf16[1024,1024]{0,1:T(8,128)(2,1)}, bf16[1024,1024]{0,1:T(8,128)(2,1)S(1)}, u32[]{:S(2)}, u32[]{:S(2)}) collective-permute-start(bf16[1024,1024]{0,1:T(8,128)(2,1)} %fusion.41), channel_id=1, source_target_pairs={{0,0},{1,2},{2,1},{3,3},{4,4},{5,6},{6,5},{7,7},{8,8},{9,10},{10,9... | collective-permute-start | bytes 6291464 | tf_op jit(solution)/shard_map/ppermute | solution.py:189
  599.2 25.6 %collective-permute-start.35 = (f32[5128]{0:T(1024)S(1)}, f32[5128]{0:T(1024)S(1)}, u32[]{:S(2)}, u32[]{:S(2)}) collective-permute-start(f32[5128]{0:T(1024)S(1)} %constant_dynamic-update-slice_fusion), channel_id=1, source_target_pairs={{0,1},{1,0},{4,5},{5,4},{8,9},{9,8},{12,13},{13,12},{16,17},{17,16... | collective-permute-start | bytes 61544 | tf_op jit(solution)/shard_map/ppermute | solution.py:221
  600.3 41.8 %collective-permute-start.27 = (bf16[64,1536]{1,0:T(8,128)(2,1)S(1)}, bf16[64,1536]{1,0:T(8,128)(2,1)S(1)}, u32[]{:S(2)}, u32[]{:S(2)}) collective-permute-start(bf16[64,1536]{1,0:T(8,128)(2,1)S(1)} %pad_maximum_fusion), channel_id=1, source_target_pairs={{0,0},{1,2},{2,1},{3,3},{4,4},{5,6},{6,5},{7,7},{8,8},{9,10},{10,9... | collective-permute-start | bytes 589832 | tf_op jit(solution)/shard_map/ppermute | solution.py:189
  624.9 4.1 collective-permute-start.36
  627.2 14.3 %collective-permute-start.32 = (bf16[32,1024]{1,0:T(8,128)(2,1)S(1)}, bf16[32,1024]{1,0:T(8,128)(2,1)S(1)}, u32[]{:S(2)}, u32[]{:S(2)}) collective-permute-start(bf16[32,1024]{1,0:T(8,128)(2,1)S(1)} %fusion.68), channel_id=1, source_target_pairs={{0,0},{1,2},{2,1},{3,3},{4,4},{5,6},{6,5},{7,7},{8,8},{9,10},{10,9... | collective-permute-start | bytes 196616 | tf_op jit(solution)/shard_map/ppermute | solution.py:189
  629.0 3.8 collective-permute-start.37
  632.8 4.7 collective-permute-start.38
  637.5 5.5 collective-permute-start.39
  644.1 6.3 collective-permute-start.34
  645.7 5.6 collective-permute-start.33
  (45 other events, 254.2 us)
Sparse Core Ops, SparseCore 0:
  11.3 80.4 all-gather.4
  95.1 54.4 all-gather.6
  152.9 75.4 all-gather.8
  231.6 74.1 all-gather.10
  335.8 94.0 reduce-scatter.4
  432.0 130.5 reduce-scatter.2

commit v3 on v2

--- a/solution.py
+++ b/solution.py
@@ -185,6 +185,135 @@
     )
 
 
+def gelu_parts(u):
+    size = jnp.abs(u) * 0.7071067811865476
+    t = 1.0 / (1.0 + 0.3275911 * size)
+    series = t * (
+        0.254829592
+        + t * (-0.284496736 + t * (1.421413741 + t * (-1.453152027 + t * 1.061405429)))
+    )
+    bell = jnp.exp(-size * size)
+    tail = 0.5 * series * bell
+    cdf = jnp.where(u >= 0, 1.0 - tail, tail)
+    return u * cdf, cdf + u * (bell * 0.3989422804014327)
+
+
+def lane_sum(v):
+    return functools.reduce(
+        jnp.add, [v[:, n : n + LANES] for n in range(0, v.shape[1], LANES)]
+    )
+
+
+def pack_rows(first, second):
+    first = jnp.sum(first, axis=1, keepdims=True)
+    second = jnp.sum(second, axis=1, keepdims=True)
+    lane = lax.broadcasted_iota(jnp.int32, (first.shape[0], LANES), 1)
+    return jnp.where(lane == 0, first, second).T[:8, :]
+
+
+def unpack_rows(block):
+    turned = jnp.concatenate([block] * (LANES // 8), axis=0).T
+    return turned[:, 0:1], turned[:, 1:2]
+
+
+def mid_stats(sums_ref, hidden):
+    first, second = unpack_rows(sums_ref[...])
+    mean = first / hidden
+    return mean, lax.rsqrt(second / hidden - mean * mean + NORM_EPS)
+
+
+def spans(width, step):
+    step = min(step, width)
+    return [slice(n, n + step) for n in range(0, width, step)]
+
+
+def up_kernel(x_ref, w_ref, active_ref, slope_ref, sums_ref):
+    x = x_ref[...]
+    first = second = 0.0
+    for cols in spans(w_ref.shape[1], 512):
+        active, slope = gelu_parts(dot(x, w_ref[:, cols]))
+        active_ref[:, cols] = active.astype(BF16)
+        slope_ref[:, cols] = slope.astype(BF16)
+        first += lane_sum(active)
+        second += lane_sum(active * active)
+    sums_ref[...] = pack_rows(first, second)
+
+
+def down_kernel(hidden, active_ref, sums_ref, gain_ref, w_ref, fed_ref, out_ref):
+    mean, inverse = mid_stats(sums_ref, hidden)
+    for cols in spans(active_ref.shape[1], 512):
+        normed = (active_ref[:, cols].astype(F32) - mean) * inverse
+        fed_ref[:, cols] = (normed * gain_ref[:, cols]).astype(BF16)
+    out_ref[...] = dot(fed_ref[...], w_ref[...]).astype(out_ref.dtype)
+
+
+def down_back_kernel(
+    hidden, grad_ref, w_ref, active_ref, sums_ref, gain_ref, back_ref, moments_ref, mid_ref
+):
+    @pl.when(pl.program_id(0) == 0)
+    def _():
+        mid_ref[...] = jnp.zeros_like(mid_ref)
+
+    mean, inverse = mid_stats(sums_ref, hidden)
+    grad = grad_ref[...]
+    first = second = 0.0
+    for cols in spans(active_ref.shape[1], 512):
+        fed = dot(grad, w_ref[cols, :], ((1,), (1,)))
+        normed = (active_ref[:, cols].astype(F32) - mean) * inverse
+        along = fed * normed
+        mid_ref[:, cols] += jnp.sum(along.reshape(-1, 8, along.shape[1]), axis=0)
+        back = fed * gain_ref[:, cols]
+        back_ref[:, cols] = back.astype(BF16)
+        first += lane_sum(back)
+        second += lane_sum(along * gain_ref[:, cols])
+    moments_ref[...] = pack_rows(first, second)
+
+
+def up_back_kernel(
+    hidden,
+    back_ref,
+    active_ref,
+    slope_ref,
+    sums_ref,
+    moments_ref,
+    w_ref,
+    grad_ref,
+    out_ref,
+):
+    mean, inverse = mid_stats(sums_ref, hidden)
+    first, second = unpack_rows(moments_ref[...])
+    first, second = first / hidden, second / hidden
+    for cols in spans(active_ref.shape[1], 512):
+        normed = (active_ref[:, cols].astype(F32) - mean) * inverse
+        grad = inverse * (back_ref[:, cols].astype(F32) - first - normed * second)
+        grad_ref[:, cols] = (grad * slope_ref[:, cols].astype(F32)).astype(BF16)
+    out_ref[...] = dot(grad_ref[...], w_ref[...], ((1,), (1,))).astype(out_ref.dtype)
+
+
+def row_call(kernel, name, inputs, outputs):
+    rows = inputs[0][0].shape[0]
+    block = min(BLOCK, rows)
+
+    def spec(shape, how):
+        if how == "rows":
+            return pl.BlockSpec((block, shape[1]), lambda i: (i, 0))
+        if how == "columns":
+            return pl.BlockSpec((shape[0], block), lambda i: (0, i))
+        return pl.BlockSpec(shape, lambda i: (0, 0))
+
+    return pl.pallas_call(
+        kernel,
+        grid=(rows // block,),
+        in_specs=[spec(a.shape, how) for a, how in inputs],
+        out_specs=[spec(shape, how) for shape, _, how in outputs],
+        out_shape=[jax.ShapeDtypeStruct(shape, dtype) for shape, dtype, _ in outputs],
+        compiler_params=pltpu.CompilerParams(
+            dimension_semantics=("arbitrary",), vmem_limit_bytes=48 << 20
+        ),
+        name=name,
+    )(*[a for a, _ in inputs])
+
+
 def exchange(a):
     return lax.ppermute(a, ("c", "h"), [(0, 0), (1, 2), (2, 1), (3, 3)])
 
@@ -259,10 +388,10 @@
 
     def collect_tokens(make):
         if paired:
-            sent = other_core(make(1).astype(BF16))
-            return make(0) + sent.astype(F32)
+            sent = other_core(make(1, BF16))
+            return make(0, F32) + sent.astype(F32)
         return lax.psum_scatter(
-            make(0).astype(BF16), PART_AXES, scatter_dimension=0, tiled=True
+            make(0, BF16), PART_AXES, scatter_dimension=0, tiled=True
         ).astype(F32)
 
     def sum_parts(values):
@@ -334,23 +463,35 @@
     gathered = spread_tokens((norm_attn * g_attn).astype(BF16))
     projected = [dot(part, w_proj).astype(BF16) for part in gathered]
     attended, scaled, lse = attn_forward(offs, projected, column_scale)
-    mixed_sum = collect_tokens(lambda t: dot(scaled[t], w_mix))
+    mixed_sum = collect_tokens(lambda t, kind: dot(scaled[t], w_mix).astype(kind))
     norm_post, inv_post = normalize(mixed_sum)
     middle = inputs + norm_post * g_post
     norm_ffn, inv_ffn = normalize(middle)
     gathered_ffn = spread_tokens((norm_ffn * g_ffn).astype(BF16))
-    upper = [dot(part, w_up) for part in gathered_ffn]
-    active = [jax.nn.gelu(u, approximate=False) for u in upper]
-    sums = sum_parts(
-        [jnp.stack([jnp.sum(a, axis=-1), jnp.sum(a * a, axis=-1)]) for a in active]
-    )
-    mean_mid = [s[0][:, None] / hidden for s in sums]
-    inv_mid = [
-        lax.rsqrt(s[1][:, None] / hidden - m * m + NORM_EPS) for s, m in zip(sums, mean_mid)
+    units = w_up.shape[1]
+    part_rows = gathered_ffn[0].shape[0]
+    wide = ((part_rows, units), BF16, "rows")
+    narrow = ((8, part_rows), F32, "columns")
+    raised = [
+        row_call(
+            up_kernel, "ffn_up", [(part, "rows"), (w_up, "whole")], [wide, wide, narrow]
+        )
+        for part in gathered_ffn
     ]
-    norm_mid = [(a - m) * r for a, m, r in zip(active, mean_mid, inv_mid)]
-    fed_down = [(n * g_mid).astype(BF16) for n in norm_mid]
-    output = middle + collect_tokens(lambda t: dot(fed_down[t], w_down))
+    active, slope = [r[0] for r in raised], [r[1] for r in raised]
+    sums_mid = sum_parts([r[2] for r in raised])
+    fed_down = [None] * parts
+
+    def lower(t, kind):
+        fed_down[t], out = row_call(
+            functools.partial(down_kernel, hidden),
+            "ffn_down",
+            [(active[t], "rows"), (sums_mid[t], "columns"), (g_mid, "whole"), (w_down, "whole")],
+            [wide, ((part_rows, model), kind, "rows")],
+        )
+        return out
+
+    output = middle + collect_tokens(lower)
     output = exchange(output.astype(BF16))
 
     cotangent = exchange(cotangent)
@@ -359,28 +500,43 @@
     grad_down = product(fed_down, grad_full)
     grad_down, grad_full = lax.optimization_barrier((grad_down, grad_full))
     grad_down = scatter(grad_down)
-    grad_fed = [dot(g, w_down, ((1,), (1,))) for g in grad_full]
-    grad_gmid = sum(jnp.sum(g * n, axis=0) for g, n in zip(grad_fed, norm_mid))
-    scaled_mid = [g * g_mid for g in grad_fed]
-    moments = sum_parts(
-        [
-            jnp.stack([jnp.sum(g, axis=-1), jnp.sum(g * n, axis=-1)])
-            for g, n in zip(scaled_mid, norm_mid)
-        ]
-    )
-    grad_upper = []
-    for t in range(parts):
-        grad_active = inv_mid[t] * (
-            scaled_mid[t]
-            - moments[t][0][:, None] / hidden
-            - norm_mid[t] * (moments[t][1][:, None] / hidden)
+    lowered_back = [
+        row_call(
+            functools.partial(down_back_kernel, hidden),
+            "ffn_down_back",
+            [
+                (grad_full[t], "rows"),
+                (w_down, "whole"),
+                (active[t], "rows"),
+                (sums_mid[t], "columns"),
+                (g_mid, "whole"),
+            ],
+            [wide, narrow, ((8, units), F32, "whole")],
         )
-        u = upper[t]
-        normal_cdf = 0.5 * (1.0 + lax.erf(u * 0.7071067811865476))
-        density = jnp.exp(-0.5 * u * u) * 0.3989422804014327
-        grad_upper.append((grad_active * (normal_cdf + u * density)).astype(BF16))
+        for t in range(parts)
+    ]
+    grad_gmid = sum(jnp.sum(r[2], axis=0) for r in lowered_back)
+    moments = sum_parts([r[1] for r in lowered_back])
+    grad_upper = [None] * parts
+
+    def raise_back(t, kind):
+        grad_upper[t], out = row_call(
+            functools.partial(up_back_kernel, hidden),
+            "ffn_up_back",
+            [
+                (lowered_back[t][0], "rows"),
+                (active[t], "rows"),
+                (slope[t], "rows"),
+                (sums_mid[t], "columns"),
+                (moments[t], "columns"),
+                (w_up, "whole"),
+            ],
+            [wide, ((part_rows, model), kind, "rows")],
+        )
+        return out
+
+    grad_entry_ffn = collect_tokens(raise_back)
     grad_up = scatter(product(gathered_ffn, grad_upper))
-    grad_entry_ffn = collect_tokens(lambda t: dot(grad_upper[t], w_up, ((1,), (1,))))
     grad_gffn = jnp.sum(grad_entry_ffn * norm_ffn, axis=0)
     grad_middle = grad_top + norm_back(grad_entry_ffn * g_ffn, norm_ffn, inv_ffn)
     grad_gpost = jnp.sum(grad_middle * norm_post, axis=0)
@@ -395,7 +551,9 @@
     grad_attended = [(g * column_scale).astype(BF16) for g in grad_scaled]
     grad_proj = attn_backward(offs, projected, grad_attended, attended, lse)
     grad_wproj = scatter_fast(product(gathered, grad_proj), 2)
-    grad_entry_attn = collect_tokens(lambda t: dot(grad_proj[t], w_proj, ((1,), (1,))))
+    grad_entry_attn = collect_tokens(
+        lambda t, kind: dot(grad_proj[t], w_proj, ((1,), (1,))).astype(kind)
+    )
     grad_gattn = jnp.sum(grad_entry_attn * norm_attn, axis=0)
     grad_inputs = grad_middle + norm_back(grad_entry_attn * g_attn, norm_attn, inv_attn)
     grad_inputs = exchange(grad_inputs.astype(BF16))

time: 669 us -> 674 us (level)
  matrix products: 207 us -> 84.7 us
  Pallas kernels: 102 us -> 201 us
  waiting for transfers between devices: 173 us -> 216 us
  other arithmetic: 52 us -> 32.8 us
  starting transfers between devices: 80.2 us -> 87.1 us
    dot_general x24 -> x16, matrix products: 207 us -> 84.7 us  [dot(): return lax.dot_general(a, b, (dims, ((), ())), preferred_element_type=F32)]
    pallas_call x0 -> x8, Pallas kernels: none -> 99.3 us  [row_call(): pl.pallas_call(kernel, grid=(rows // block,), in_specs=[spec(a.shape, how...]
    all_gather x4, waiting for transfers between devices: 101 us -> 145 us  [gather(): return lax.all_gather(a, WEIGHT_AXES, axis=0, tiled=True)]
    convert_element_type x2 -> x0, other arithmetic: 25.6 us -> none  [the longest x1 21.5 us: body(): grad_upper.append((grad_active * (normal_cdf + u * density)).astype(BF16))]
    ppermute x11, starting transfers between devices: 10.1 us -> 28.4 us  [other_core(): return lax.ppermute(a, 'c', [(0, 1), (1, 0)])]
    ppermute x13, starting transfers between devices: 47.7 us -> 33.8 us  [exchange(): return lax.ppermute(a, ('c', 'h'), [(0, 0), (1, 2), (2, 1), (3, 3)])]
    unnamed x133 -> x73, local copies, waits for them, and re-layouts: 22.5 us -> 16.8 us
  transfers between devices with their start and end apart: 46 -> 46, of which waited for: 15 -> 16; matrix products, arithmetic and copies ran while one was open for 38% -> 17% of each run, Pallas kernels for 15% -> 30%
where the time goes in v3:
time: 674 us; the launch traced here: 661 us
  waiting for transfers between devices  216 us (32%)
  Pallas kernels  201 us (30%)
  starting transfers between devices  87.1 us (13%)
  matrix products  84.7 us (13%)
  other arithmetic  32.8 us (5%)
  local copies, waits for them, and re-layouts  23.7 us (4%)
  between operations  15.2 us (2%)
    all_gather x4, waiting for transfers between devices, gather(): return lax.all_gather(a, WEIGHT_AXES, axis=0, tiled=True)  145 us
    pallas_call x8, Pallas kernels, row_call(): pl.pallas_call(kernel, grid=(rows // block,), in_specs=[spec(a.shape, how...  99.3 us
    dot_general x16, matrix products, dot(): return lax.dot_general(a, b, (dims, ((), ())), preferred_element_type=F32)  84.7 us
    pallas_call x1, Pallas kernels, attn_backward(): pl.pallas_call(functools.partial(attn_backward_kernel, chunks, total // B...  60.5 us
    pallas_call x1, Pallas kernels, attn_forward(): pl.pallas_call(functools.partial(attn_forward_kernel, chunks, total // BL...  41.5 us
    ppermute x12, waiting for transfers between devices, halving_sum(): lax.ppermute(sent.astype(BF16), WEIGHT_AXES, rank_pairs(ranks, bit))  39.7 us
    ppermute x13, starting transfers between devices, exchange(): return lax.ppermute(a, ('c', 'h'), [(0, 0), (1, 2), (2, 1), (3, 3)])  33.8 us
    ppermute x11, starting transfers between devices, other_core(): return lax.ppermute(a, 'c', [(0, 1), (1, 0)])  28.4 us
  transfers between devices with their start and end apart: 46, of which 16 were waited for; matrix products, arithmetic and copies ran while one was open for 17% of the time, Pallas kernels for 30%

profile of v3, /device:TPU:0, one launch (start us, length us, event | category | flops | bytes accessed | tf_op | source)
XLA Modules:
  0.0 661.1 jit_solution(3972315136834983948)
XLA Ops:
  10.6 1.5 collective-permute-start.4
  12.8 1.6 collective-permute-start.6
  15.2 2.3 collective-permute-start
  18.5 73.7 %all-gather.5.cloned.1.call-done = bf16[1024,1664]{1,0:T(8,128)(2,1)} async-done(((bf16[64,1664]{1,0:T(8,128)(2,1)}), bf16[1024,1664]{1,0:T(8,128)(2,1)}) %all-gather.5.cloned.1.call-update) | async-done | bytes 3407888 | tf_op jit(solution)/shard_map/all_gather | solution.py:440
  93.7 2.0 fusion.6
  98.2 7.7 %convolution_convert_fusion.1.refs_0_.refs_2_.refs_4_ = bf16[1024,1536]{1,0:T(8,128)(2,1)} fusion(bf16[1024,1024]{1,0:T(8,128)(2,1)} %fusion.6, bf16[1024,1664]{1,0:T(8,128)(2,1)} %all-gather.5.cloned.1.call-done), kind=kOutput, calls=%fused_computation.36 | convolution fusion | flops 3222798336 | bytes 8388608 | tf_op jit(solution)/shard_map/dot_general | solution.py:22
  106.0 6.5 convolution_convert_fusion.refs_1_.refs_3_.refs_5_
  112.5 41.5 %attn_forward.1 = (bf16[1024,512]{1,0:T(8,128)(2,1)S(1)}, bf16[1024,512]{1,0:T(8,128)(2,1)S(1)}, bf16[1024,512]{1,0:T(8,128)(2,1)S(1)}, bf16[1024,512]{1,0:T(8,128)(2,1)S(1)}, f32[8,8,2048]{2,1,0:T(8,128)S(1)}) custom-call(s32[2]{0:T(128)S(1)} %pad_add_fusion.offs, bf16[1024,1536]{1,0:T(8,128)(2,1)} %convolution_convert_fusion.1.refs_0_.refs_2_.refs_4_, ...), custom_call_target="tpu_custom_call" | custom-call | tf_op jit(solution)/shard_map/attn_forward/pallas_call | solution.py:78
  156.0 4.4 convolution_convert_fusion.2
  160.4 6.9 %collective-permute-start.5 = (bf16[1024,1024]{1,0:T(8,128)(2,1)}, bf16[1024,1024]{1,0:T(8,128)(2,1)}, u32[]{:S(2)}, u32[]{:S(2)}) collective-permute-start(bf16[1024,1024]{1,0:T(8,128)(2,1)} %convolution_convert_fusion.2), channel_id=1, source_target_pairs={{0,2},{2,0},{1,3},{3,1},{4,6},{6,4},{5,7},{7,5},{8,10},{10,8},{9,1... | collective-permute-start | bytes 6291464 | tf_op jit(solution)/shard_map/ppermute | solution.py:322
  167.3 2.4 collective-permute-start.12
  169.8 1.6 collective-permute-done.5
  171.4 3.3 fusion.47
  175.3 2.5 copy-done.13
  179.5 2.1 multiply_convert_fusion.1.x_ref
  182.0 20.3 %collective-permute-start.13 = (bf16[1024,1024]{1,0:T(8,128)(2,1)S(1)}, bf16[1024,1024]{1,0:T(8,128)(2,1)}, u32[]{:S(2)}, u32[]{:S(2)}) collective-permute-start(bf16[1024,1024]{1,0:T(8,128)(2,1)S(1)} %collective-permute-done.12.grad_ref), channel_id=1, source_target_pairs={{0,2},{2,0},{1,3},{3,1},{4,6},{6,4},{5,7},{7,5},{8,10},{10,8},{9,1... | collective-permute-start | bytes 6291464 | tf_op jit(solution)/shard_map/ppermute | solution.py:322
  202.3 28.3 %all-gather.9.cloned.1.call-done.w_ref = bf16[1024,2048]{1,0:T(8,128)(2,1)} async-done(((bf16[64,2048]{1,0:T(8,128)(2,1)}), bf16[1024,2048]{1,0:T(8,128)(2,1)}) %all-gather.9.cloned.1.call-update) | async-done | bytes 4194320 | tf_op jit(solution)/shard_map/all_gather | solution.py:440
  230.6 16.6 %ffn_up.2 = (bf16[1024,2048]{1,0:T(8,128)(2,1)}, bf16[1024,2048]{1,0:T(8,128)(2,1)}, f32[8,1024]{1,0:T(8,128)S(1)}) custom-call(bf16[1024,1024]{1,0:T(8,128)(2,1)} %multiply_convert_fusion.1.x_ref, bf16[1024,2048]{1,0:T(8,128)(2,1)} %all-gather.9.cloned.1.call-done.w_ref), custom_call_target="tpu_custom_call" | custom-call | tf_op jit(solution)/shard_map/ffn_up/pallas_call | solution.py:304
  247.2 16.6 %ffn_up.3 = (bf16[1024,2048]{1,0:T(8,128)(2,1)}, bf16[1024,2048]{1,0:T(8,128)(2,1)}, f32[8,1024]{1,0:T(8,128)S(1)}) custom-call(bf16[1024,1024]{1,0:T(8,128)(2,1)} %collective-permute-done.7.x_ref, bf16[1024,2048]{1,0:T(8,128)(2,1)} %all-gather.9.cloned.1.call-done.w_ref), custom_call_target="tpu_custom_call" | custom-call | tf_op jit(solution)/shard_map/ffn_up/pallas_call | solution.py:304
  265.1 42.9 %all-gather.11.cloned.1.call-done.w_ref = bf16[2048,1024]{1,0:T(8,128)(2,1)} async-done(((bf16[128,1024]{1,0:T(8,128)(2,1)}), bf16[2048,1024]{1,0:T(8,128)(2,1)}) %all-gather.11.cloned.1.call-update) | async-done | bytes 4194320 | tf_op jit(solution)/shard_map/all_gather | solution.py:440
  308.1 9.6 %ffn_down.3 = (bf16[1024,2048]{1,0:T(8,128)(2,1)}, bf16[1024,1024]{1,0:T(8,128)(2,1)}) custom-call(bf16[1024,2048]{1,0:T(8,128)(2,1)} %get-tuple-element.47.active_ref, f32[8,1024]{1,0:T(8,128)S(1)} %get-tuple-element.136.sums_ref, f32[1,2048]{1,0:T(1,128)S(1)} %bitcast.125, bf16[2048,1024]{1,0:T(8,128)(2,1)} %all-gather.11.cloned.1.call-done.w_ref), custom_call_target="tpu_custom_call" | custom-call | tf_op jit(solution)/shard_map/ffn_down/pallas_call | solution.py:304
  317.6 10.2 %ffn_down.2 = (bf16[1024,2048]{1,0:T(8,128)(2,1)S(1)}, f32[1024,1024]{1,0:T(8,128)}) custom-call(bf16[1024,2048]{1,0:T(8,128)(2,1)} %get-tuple-element.43.active_ref, f32[8,1024]{1,0:T(8,128)S(1)} %get-tuple-element.137.sums_ref, f32[1,2048]{1,0:T(1,128)S(1)} %bitcast.126, bf16[2048,1024]{1,0:T(8,128)(2,1)} %all-gather.11.cloned.1.call-done.w_ref), custom_call_target="tpu_custom_call" | custom-call | tf_op jit(solution)/shard_map/ffn_down/pallas_call | solution.py:304
  327.8 4.6 fusion.48
  332.4 7.7 %add_convert_fusion.1 = bf16[2048,1024]{1,0:T(8,128)(2,1)} fusion(f32[2048,1024]{1,0:T(8,128)S(1)} %fusion.48, bf16[1024,2048]{1,0:T(8,128)(2,1)S(1)} %copy-done.28, bf16[1024,1024]{1,0:T(8,128)(2,1)} %collective-permute-done.13.grad_ref), kind=kOutput, calls=%fused_computation.1 | convolution fusion | flops 4299161600 | bytes 18874368 | tf_op jit(solution)/shard_map/dot_general | solution.py:22
  340.3 10.9 %ffn_down_back.3 = (bf16[1024,2048]{1,0:T(8,128)(2,1)}, f32[8,1024]{1,0:T(8,128)S(1)}, f32[8,2048]{1,0:T(8,128)S(1)}) custom-call(bf16[1024,1024]{1,0:T(8,128)(2,1)} %collective-permute-done.13.grad_ref, bf16[2048,1024]{1,0:T(8,128)(2,1)} %all-gather.11.cloned.1.call-done.w_ref, bf16[1024,2048]{1,0:T(8,128)(2,1)} %get-tuple-element.47.active_ref, ...), custom_call_target="tpu_custom_call" | custom-call | tf_op jit(solution)/shard_map/ffn_down_back/pallas_call | solution.py:304
  351.1 10.4 %ffn_down_back.2 = (bf16[1024,2048]{1,0:T(8,128)(2,1)}, f32[8,1024]{1,0:T(8,128)S(1)}, f32[8,2048]{1,0:T(8,128)S(1)}) custom-call(bf16[1024,1024]{1,0:T(8,128)(2,1)S(1)} %collective-permute-done.12.grad_ref, bf16[2048,1024]{1,0:T(8,128)(2,1)} %all-gather.11.cloned.1.call-done.w_ref, bf16[1024,2048]{1,0:T(8,128)(2,1)} %get-tuple-element.43.active_ref, ...), custom_call_target="tpu_custom_call" | custom-call | tf_op jit(solution)/shard_map/ffn_down_back/pallas_call | solution.py:304
  362.8 12.4 %ffn_up_back.3 = (bf16[1024,2048]{1,0:T(8,128)(2,1)}, bf16[1024,1024]{1,0:T(8,128)(2,1)}) custom-call(bf16[1024,2048]{1,0:T(8,128)(2,1)} %get-tuple-element.58.back_ref, bf16[1024,2048]{1,0:T(8,128)(2,1)} %get-tuple-element.47.active_ref, bf16[1024,2048]{1,0:T(8,128)(2,1)} %get-tuple-element.59.slope_ref, f32[8,1024]{1,0:T(8,128)S(1)} %get-tuple-element.136.sums_ref, ...), custom_call_target="tpu_custom_call" | custom-call | tf_op jit(solution)/shard_map/ffn_up_back/pallas_call | solution.py:304
  375.8 12.8 %ffn_up_back.2 = (bf16[1024,2048]{1,0:T(8,128)(2,1)S(1)}, f32[1024,1024]{1,0:T(8,128)}) custom-call(bf16[1024,2048]{1,0:T(8,128)(2,1)} %get-tuple-element.52.back_ref, bf16[1024,2048]{1,0:T(8,128)(2,1)} %get-tuple-element.43.active_ref, bf16[1024,2048]{1,0:T(8,128)(2,1)} %get-tuple-element.53.slope_ref, f32[8,1024]{1,0:T(8,128)S(1)} %get-tuple-element.137.sums_ref, ...), custom_call_target="tpu_custom_call" | custom-call | tf_op jit(solution)/shard_map/ffn_up_back/pallas_call | solution.py:304
  388.7 4.1 multiply_reduce_fusion
  394.1 7.3 %multiply_reduce_fusion.1 = (f32[1024]{0:T(1024)S(1)}, f32[1024]{0:T(1024)S(1)}, f32[1024]{0:T(1024)S(1)}, f32[1024,1024]{1,0:T(8,128)S(1)}, bf16[1024,1024]{1,0:T(8,128)(2,1)}) fusion(f32[1024,1024]{1,0:T(8,128)S(1)} %copy-done.9, f32[1024]{0:T(1024)S(1)} %add_rsqrt_fusion.1, f32[1024]{0:T(1024)S(1)} %broadcast_multiply_fusion.7, f32[1024]{0:T(1024)S(1)} %mul.195, ...), kind=kLoop, calls=%fused_computation.21 | loop fusion | flops 24114176 | bytes 29405184 | tf_op jit(solution)/shard_map/reduce_sum | solution.py:542
  401.4 2.5 multiply_convert_fusion
  405.8 6.2 fusion.51
  412.0 7.8 %add_convert_fusion = bf16[1024,2048]{1,0:T(8,128)(2,1)} fusion(f32[1024,2048]{1,0:T(8,128)S(1)} %fusion.51, bf16[1024,1024]{1,0:T(8,128)(2,1)} %multiply_convert_fusion.1.x_ref, bf16[1024,2048]{1,0:T(8,128)(2,1)S(1)} %get-tuple-element.66), kind=kOutput, calls=%fused_computation | convolution fusion | flops 4299161600 | bytes 18874368 | tf_op jit(solution)/shard_map/dot_general | solution.py:22
  421.0 4.3 multiply_reduce_fusion.10
  425.5 17.2 %collective-permute-start.11 = (bf16[1024,1024]{1,0:T(8,128)(2,1)}, bf16[1024,1024]{1,0:T(8,128)(2,1)}, u32[]{:S(2)}, u32[]{:S(2)}) collective-permute-start(bf16[1024,1024]{1,0:T(8,128)(2,1)} %get-tuple-element.127), channel_id=1, source_target_pairs={{0,0},{1,2},{2,1},{3,3},{4,4},{5,6},{6,5},{7,7},{8,8},{9,10},{10,9... | collective-permute-start | bytes 6291464 | tf_op jit(solution)/shard_map/ppermute | solution.py:318
  442.7 3.0 fusion.50
  445.7 3.0 add_convert_fusion.4
  448.9 4.0 multiply_reduce_fusion.9
  452.9 60.5 %attn_backward.1 = (bf16[1024,1536]{1,0:T(8,128)(2,1)}, bf16[1024,1536]{1,0:T(8,128)(2,1)}) custom-call(s32[2]{0:T(128)} %copy-done.7, bf16[1024,1536]{1,0:T(8,128)(2,1)} %convolution_convert_fusion.1.refs_0_.refs_2_.refs_4_, bf16[1024,1536]{1,0:T(8,128)(2,1)} %convolution_convert_fusion.refs_1_.refs_3_.refs_5_, ...), custom_call_target="tpu_custom_call" | custom-call | tf_op jit(solution)/shard_map/attn_backward/pallas_call | solution.py:162
  513.3 6.2 fusion.49
  519.6 5.6 add_convert_fusion.2
  526.4 2.0 collective-permute-start.19
  532.5 4.6 fusion.22
  537.3 25.0 %collective-permute-done.29 = bf16[4,32,1024]{2,1,0:T(8,128)(2,1)} collective-permute-done((bf16[4,32,1024]{2,1,0:T(8,128)(2,1)S(1)}, bf16[4,32,1024]{2,1,0:T(8,128)(2,1)}, u32[]{:S(2)}, u32[]{:S(2)}) %collective-permute-start.29) | collective-permute-done | bytes 262176 | tf_op jit(solution)/shard_map/ppermute | solution.py:340
  565.9 3.4 collective-permute-start.20
  570.9 2.1 collective-permute-start.31
  573.0 5.6 collective-permute-done.20
  580.0 1.5 collective-permute-done.24
  582.9 3.7 collective-permute-done.21
  586.7 2.2 collective-permute-start.22
  590.4 2.3 collective-permute-start.26
  592.7 2.2 collective-permute-done.22
  595.0 5.8 fusion.12
  600.8 2.6 fusion.11
  603.4 2.2 collective-permute-start.18
  606.5 21.6 %collective-permute-done.35 = f32[5128]{0:T(1024)S(1)} collective-permute-done((f32[5128]{0:T(1024)S(1)}, f32[5128]{0:T(1024)S(1)}, u32[]{:S(2)}, u32[]{:S(2)}) %collective-permute-start.35) | collective-permute-done | bytes 20544 | tf_op jit(solution)/shard_map/ppermute | solution.py:350
  629.5 2.4 collective-permute-done.36
  631.9 2.4 collective-permute-start.37
  634.3 1.8 collective-permute-done.37
  636.1 3.6 collective-permute-start.38
  639.8 1.8 collective-permute-done.38
  644.2 1.6 collective-permute-start.34
  645.8 1.6 collective-permute-start.33
  649.7 3.1 copy.67
  (223 shorter events, 45.8 us)
Async XLA Ops:
  7.2 85.1 %all-gather.5.cloned.1.call-start = ((), (), s32[]{:S(2)}) async-start(), calls=%async_computation.2 | async-start | bytes 3620864 | tf_op jit(solution)/shard_map/all_gather | solution.py:440
  9.1 0.7 collective-permute-start.1
  10.5 145.5 %all-gather.7.cloned.1.call-start = ((), (), s32[]{:S(2)}) async-start(), calls=%async_computation.3 | async-start | bytes 1114112 | tf_op jit(solution)/shard_map/all_gather | solution.py:440
  10.6 1.5 collective-permute-start.4
  12.7 217.9 %all-gather.9.cloned.1.call-start = ((), (), s32[]{:S(2)}) async-start(), calls=%async_computation.4 | async-start | bytes 4456448 | tf_op jit(solution)/shard_map/all_gather | solution.py:440
  12.8 1.6 collective-permute-start.6
  15.1 292.9 %all-gather.11.cloned.1.call-start = ((), (), s32[]{:S(2)}) async-start(), calls=%async_computation.5 | async-start | bytes 4456448 | tf_op jit(solution)/shard_map/all_gather | solution.py:440
  15.2 2.3 collective-permute-start
  17.4 78.2 %copy-start.12 = (bf16[1024,1024]{1,0:T(8,128)(2,1)}, bf16[1024,1024]{1,0:T(8,128)(2,1)S(1)}, u32[]{:S(2)}) copy-start(bf16[1024,1024]{1,0:T(8,128)(2,1)S(1)} %collective-permute-done) | copy-start | bytes 6291460
  17.8 77.9 %copy-start.32 = (bf16[128,1024]{1,0:T(8,128)(2,1)S(1)}, bf16[128,1024]{1,0:T(8,128)(2,1)}, u32[]{:S(2)}) copy-start(bf16[128,1024]{1,0:T(8,128)(2,1)} %param.15) | copy-start | bytes 786436
  17.8 78.6 %copy-start.33 = (bf16[8]{0:T(256)(128)(2,1)S(1)}, bf16[8]{0:T(256)(128)(2,1)}, u32[]{:S(2)}) copy-start(bf16[8]{0:T(256)(128)(2,1)} %param.20) | copy-start | bytes 52
  95.7 10.3 %collective-permute-start.2 = (bf16[1024,1024]{1,0:T(8,128)(2,1)}, bf16[1024,1024]{1,0:T(8,128)(2,1)}, u32[]{:S(2)}, u32[]{:S(2)}) collective-permute-start(bf16[1024,1024]{1,0:T(8,128)(2,1)} %fusion.6), channel_id=1, source_target_pairs={{0,2},{2,0},{1,3},{3,1},{4,6},{6,4},{5,7},{7,5},{8,10},{10,8},{9,1... | collective-permute-start | bytes 6291464 | tf_op jit(solution)/shard_map/ppermute | solution.py:322
  95.7 1.6 collective-permute-start.9
  96.4 0.8 collective-permute-start.3
  97.1 15.4 %copy-start.7 = (s32[2]{0:T(128)}, s32[2]{0:T(128)S(1)}, u32[]{:S(2)}) copy-start(s32[2]{0:T(128)S(1)} %pad_add_fusion.offs) | copy-start | bytes 28
  98.0 546.2 %reduce-scatter.5.cloned.1.call-start = ((), (), s32[]{:S(2)}) async-start(), calls=%async_computation.7 | async-start | bytes 4456448 | tf_op jit(solution)/shard_map/reduce_scatter | solution.py:407
  98.2 7.7 %copy-start.24 = (bf16[1024,1664]{1,0:T(8,128)(2,1)S(1)}, bf16[1024,1664]{1,0:T(8,128)(2,1)}, u32[]{:S(2)}) copy-start(bf16[1024,1664]{1,0:T(8,128)(2,1)} %all-gather.5.cloned.1.call-done) | copy-start | bytes 10223620
  156.0 4.4 copy-start.6
  160.4 11.0 %collective-permute-start.5 = (bf16[1024,1024]{1,0:T(8,128)(2,1)}, bf16[1024,1024]{1,0:T(8,128)(2,1)}, u32[]{:S(2)}, u32[]{:S(2)}) collective-permute-start(bf16[1024,1024]{1,0:T(8,128)(2,1)} %convolution_convert_fusion.2), channel_id=1, source_target_pairs={{0,2},{2,0},{1,3},{3,1},{4,6},{6,4},{5,7},{7,5},{8,10},{10,8},{9,1... | collective-permute-start | bytes 6291464 | tf_op jit(solution)/shard_map/ppermute | solution.py:322
  167.3 14.7 %collective-permute-start.12 = (bf16[1024,1024]{1,0:T(8,128)(2,1)}, bf16[1024,1024]{1,0:T(8,128)(2,1)S(1)}, u32[]{:S(2)}, u32[]{:S(2)}) collective-permute-start(bf16[1024,1024]{1,0:T(8,128)(2,1)} %param.21), channel_id=1, source_target_pairs={{0,0},{1,2},{2,1},{3,3},{4,4},{5,6},{6,5},{7,7},{8,8},{9,10},{10,9... | collective-permute-start | bytes 6291464 | tf_op jit(solution)/shard_map/ppermute | solution.py:318
  181.6 65.6 %collective-permute-start.7 = (bf16[1024,1024]{1,0:T(8,128)(2,1)}, bf16[1024,1024]{1,0:T(8,128)(2,1)}, u32[]{:S(2)}, u32[]{:S(2)}) collective-permute-start(bf16[1024,1024]{1,0:T(8,128)(2,1)} %multiply_convert_fusion.1.x_ref), channel_id=1, source_target_pairs={{0,2},{2,0},{1,3},{3,1},{4,6},{6,4},{5,7},{7,5},{8,10},{10,8},{9,1... | collective-permute-start | bytes 6291464 | tf_op jit(solution)/shard_map/ppermute | solution.py:322
  182.0 150.5 %collective-permute-start.13 = (bf16[1024,1024]{1,0:T(8,128)(2,1)S(1)}, bf16[1024,1024]{1,0:T(8,128)(2,1)}, u32[]{:S(2)}, u32[]{:S(2)}) collective-permute-start(bf16[1024,1024]{1,0:T(8,128)(2,1)S(1)} %collective-permute-done.12.grad_ref), channel_id=1, source_target_pairs={{0,2},{2,0},{1,3},{3,1},{4,6},{6,4},{5,7},{7,5},{8,10},{10,8},{9,1... | collective-permute-start | bytes 6291464 | tf_op jit(solution)/shard_map/ppermute | solution.py:322
  263.8 1.3 collective-permute-start.8
  327.8 4.6 copy-start.28
  340.2 305.6 %reduce-scatter.3.cloned.1.call-start = ((), (), s32[]{:S(2)}) async-start(), calls=%async_computation.6 | async-start | bytes 4456448 | tf_op jit(solution)/shard_map/reduce_scatter | solution.py:407
  361.5 1.3 collective-permute-start.14
  375.2 13.5 %collective-permute-start.15 = (bf16[1024,1024]{1,0:T(8,128)(2,1)}, bf16[1024,1024]{1,0:T(8,128)(2,1)}, u32[]{:S(2)}, u32[]{:S(2)}) collective-permute-start(bf16[1024,1024]{1,0:T(8,128)(2,1)} %get-tuple-element.60), channel_id=1, source_target_pairs={{0,2},{2,0},{1,3},{3,1},{4,6},{6,4},{5,7},{7,5},{8,10},{10,8},{9,1... | collective-permute-start | bytes 6291464 | tf_op jit(solution)/shard_map/ppermute | solution.py:322
  375.3 17.5 %collective-permute-start.10 = (bf16[1024,1024]{1,0:T(8,128)(2,1)}, bf16[1024,1024]{1,0:T(8,128)(2,1)}, u32[]{:S(2)}, u32[]{:S(2)}) collective-permute-start(bf16[1024,1024]{1,0:T(8,128)(2,1)} %get-tuple-element.48), channel_id=1, source_target_pairs={{0,2},{2,0},{1,3},{3,1},{4,6},{6,4},{5,7},{7,5},{8,10},{10,8},{9,1... | collective-permute-start | bytes 6291464 | tf_op jit(solution)/shard_map/ppermute | solution.py:322
  375.8 12.9 %copy-start.11 = (f32[1024,1024]{1,0:T(8,128)S(1)}, f32[1024,1024]{1,0:T(8,128)}, u32[]{:S(2)}) copy-start(f32[1024,1024]{1,0:T(8,128)} %copy-done.10) | copy-start | bytes 12582916
  388.7 5.4 copy-start.17
  401.4 4.4 copy-start.27
  404.5 38.2 %collective-permute-start.16 = (bf16[1024,1024]{1,0:T(8,128)(2,1)}, bf16[1024,1024]{1,0:T(8,128)(2,1)}, u32[]{:S(2)}, u32[]{:S(2)}) collective-permute-start(bf16[1024,1024]{1,0:T(8,128)(2,1)} %multiply_convert_fusion), channel_id=1, source_target_pairs={{0,2},{2,0},{1,3},{3,1},{4,6},{6,4},{5,7},{7,5},{8,10},{10,8},{9,1... | collective-permute-start | bytes 6291464 | tf_op jit(solution)/shard_map/ppermute | solution.py:322
  421.0 21.7 %copy-start.5 = (bf16[1024,512]{1,0:T(8,128)(2,1)S(1)}, bf16[1024,512]{1,0:T(8,128)(2,1)}, u32[]{:S(2)}) copy-start(bf16[1024,512]{1,0:T(8,128)(2,1)} %copy-done.4) | copy-start | bytes 3145732
  425.5 216.1 %collective-permute-start.11 = (bf16[1024,1024]{1,0:T(8,128)(2,1)}, bf16[1024,1024]{1,0:T(8,128)(2,1)}, u32[]{:S(2)}, u32[]{:S(2)}) collective-permute-start(bf16[1024,1024]{1,0:T(8,128)(2,1)} %get-tuple-element.127), channel_id=1, source_target_pairs={{0,0},{1,2},{2,1},{3,3},{4,4},{5,6},{6,5},{7,7},{8,8},{9,10},{10,9... | collective-permute-start | bytes 6291464 | tf_op jit(solution)/shard_map/ppermute | solution.py:318
  448.8 81.9 %collective-permute-start.28 = (bf16[8,32,1024]{2,1,0:T(8,128)(2,1)S(1)}, bf16[8,32,1024]{2,1,0:T(8,128)(2,1)S(1)}, u32[]{:S(2)}, u32[]{:S(2)}) collective-permute-start(bf16[8,32,1024]{2,1,0:T(8,128)(2,1)S(1)} %dynamic-slice_bitcast_fusion.2), channel_id=1, source_target_pairs={{0,1},{1,0},{4,5},{5,4},{8,9},{9,8},{12,13},{13,12},{16,17},{17,16... | collective-permute-start | bytes 1572872 | tf_op jit(solution)/shard_map/ppermute | solution.py:340
  513.3 6.2 copy-start.29
  525.2 7.3 %copy-start.31 = (bf16[1024,1536]{1,0:T(8,128)(2,1)S(1)}, bf16[1024,1536]{1,0:T(8,128)(2,1)}, u32[]{:S(2)}) copy-start(bf16[1024,1536]{1,0:T(8,128)(2,1)} %get-tuple-element.65) | copy-start | bytes 9437188
  525.4 7.0 %copy-start.25 = (bf16[1024,1664]{1,0:T(8,128)(2,1)S(1)}, bf16[1024,1664]{1,0:T(8,128)(2,1)}, u32[]{:S(2)}) copy-start(bf16[1024,1664]{1,0:T(8,128)(2,1)} %all-gather.5.cloned.1.call-done) | copy-start | bytes 10223620
  526.4 38.1 %collective-permute-start.19 = (bf16[8,64,768]{2,1,0:T(8,128)(2,1)}, bf16[8,64,768]{2,1,0:T(8,128)(2,1)}, u32[]{:S(2)}, u32[]{:S(2)}) collective-permute-start(bf16[8,64,768]{2,1,0:T(8,128)(2,1)} %dynamic-slice_bitcast_fusion.1), channel_id=1, source_target_pairs={{0,1},{1,0},{4,5},{5,4},{8,9},{9,8},{12,13},{13,12},{16,17},{17,16... | collective-permute-start | bytes 2359304 | tf_op jit(solution)/shard_map/ppermute | solution.py:340
  529.3 40.0 %collective-permute-start.23 = (bf16[4,128,768]{2,1,0:T(8,128)(2,1)}, bf16[4,128,768]{2,1,0:T(8,128)(2,1)}, u32[]{:S(2)}, u32[]{:S(2)}) collective-permute-start(bf16[4,128,768]{2,1,0:T(8,128)(2,1)} %dynamic-slice_bitcast_fusion), channel_id=1, source_target_pairs={{0,4},{1,5},{4,0},{5,1},{8,12},{9,13},{12,8},{13,9},{16,20},{17,21... | collective-permute-start | bytes 2359304 | tf_op jit(solution)/shard_map/ppermute | solution.py:340
  531.7 30.6 %collective-permute-start.29 = (bf16[4,32,1024]{2,1,0:T(8,128)(2,1)S(1)}, bf16[4,32,1024]{2,1,0:T(8,128)(2,1)}, u32[]{:S(2)}, u32[]{:S(2)}) collective-permute-start(bf16[4,32,1024]{2,1,0:T(8,128)(2,1)S(1)} %dynamic-slice_bitcast_fusion.5), channel_id=1, source_target_pairs={{0,4},{1,5},{4,0},{5,1},{8,12},{9,13},{12,8},{13,9},{16,20},{17,21... | collective-permute-start | bytes 786440 | tf_op jit(solution)/shard_map/ppermute | solution.py:340
  537.1 57.8 %collective-permute-start.17 = (bf16[1024,1024]{1,0:T(8,128)(2,1)}, bf16[1024,1024]{1,0:T(8,128)(2,1)}, u32[]{:S(2)}, u32[]{:S(2)}) collective-permute-start(bf16[1024,1024]{1,0:T(8,128)(2,1)} %fusion.22), channel_id=1, source_target_pairs={{0,2},{2,0},{1,3},{3,1},{4,6},{6,4},{5,7},{7,5},{8,10},{10,8},{9,1... | collective-permute-start | bytes 6291464 | tf_op jit(solution)/shard_map/ppermute | solution.py:322
  563.4 7.4 %collective-permute-start.30 = (bf16[2,32,1024]{2,1,0:T(8,128)(2,1)S(1)}, bf16[2,32,1024]{2,1,0:T(8,128)(2,1)S(1)}, u32[]{:S(2)}, u32[]{:S(2)}) collective-permute-start(bf16[2,32,1024]{2,1,0:T(8,128)(2,1)S(1)} %dynamic-slice_bitcast_fusion.8), channel_id=1, source_target_pairs={{0,8},{1,9},{4,12},{5,13},{8,0},{9,1},{12,4},{13,5},{16,24},{17,25... | collective-permute-start | bytes 393224 | tf_op jit(solution)/shard_map/ppermute | solution.py:340
  565.9 29.0 %copy-start.14 = (bf16[1024,1024]{1,0:T(8,128)(2,1)S(1)}, bf16[1024,1024]{1,0:T(8,128)(2,1)}, u32[]{:S(2)}) copy-start(bf16[1024,1024]{1,0:T(8,128)(2,1)} %copy-done.12) | copy-start | bytes 6291460
  565.9 29.0 %copy-start.26 = (bf16[1024,1664]{1,0:T(8,128)(2,1)S(1)}, bf16[1024,1664]{1,0:T(8,128)(2,1)}, u32[]{:S(2)}) copy-start(bf16[1024,1664]{1,0:T(8,128)(2,1)} %all-gather.5.cloned.1.call-done) | copy-start | bytes 10223620
  565.9 29.0 %copy-start.30 = (bf16[1024,1536]{1,0:T(8,128)(2,1)S(1)}, bf16[1024,1536]{1,0:T(8,128)(2,1)}, u32[]{:S(2)}) copy-start(bf16[1024,1536]{1,0:T(8,128)(2,1)} %get-tuple-element.64) | copy-start | bytes 9437188
  565.9 12.7 %collective-permute-start.20 = (bf16[4,64,768]{2,1,0:T(8,128)(2,1)S(1)}, bf16[4,64,768]{2,1,0:T(8,128)(2,1)S(1)}, u32[]{:S(2)}, u32[]{:S(2)}) collective-permute-start(bf16[4,64,768]{2,1,0:T(8,128)(2,1)S(1)} %dynamic-slice_bitcast_fusion.4), channel_id=1, source_target_pairs={{0,4},{1,5},{4,0},{5,1},{8,12},{9,13},{12,8},{13,9},{16,20},{17,21... | collective-permute-start | bytes 1179656 | tf_op jit(solution)/shard_map/ppermute | solution.py:340
  570.8 10.8 %collective-permute-start.24 = (bf16[4,64,768]{2,1,0:T(8,128)(2,1)S(1)}, bf16[4,64,768]{2,1,0:T(8,128)(2,1)S(1)}, u32[]{:S(2)}, u32[]{:S(2)}) collective-permute-start(bf16[4,64,768]{2,1,0:T(8,128)(2,1)S(1)} %dynamic-slice_bitcast_fusion.3), channel_id=1, source_target_pairs={{0,1},{1,0},{4,5},{5,4},{8,9},{9,8},{12,13},{13,12},{16,17},{17,16... | collective-permute-start | bytes 1179656 | tf_op jit(solution)/shard_map/ppermute | solution.py:340
  570.9 57.9 %collective-permute-start.31 = (bf16[1,32,1024]{2,1,0:T(8,128)(2,1)S(1)}, bf16[1,32,1024]{2,1,0:T(8,128)(2,1)S(1)}, u32[]{:S(2)}, u32[]{:S(2)}) collective-permute-start(bf16[1,32,1024]{2,1,0:T(8,128)(2,1)S(1)} %constant_dynamic-slice_fusion), channel_id=1, source_target_pairs={{0,16},{1,17},{4,20},{5,21},{8,24},{9,25},{12,28},{13,29},{16,0},{... | collective-permute-start | bytes 196616 | tf_op jit(solution)/shard_map/ppermute | solution.py:340
  578.8 7.8 %collective-permute-start.21 = (bf16[2,64,768]{2,1,0:T(8,128)(2,1)S(1)}, bf16[2,64,768]{2,1,0:T(8,128)(2,1)S(1)}, u32[]{:S(2)}, u32[]{:S(2)}) collective-permute-start(bf16[2,64,768]{2,1,0:T(8,128)(2,1)S(1)} %dynamic-slice_bitcast_fusion.7), channel_id=1, source_target_pairs={{0,8},{1,9},{4,12},{5,13},{8,0},{9,1},{12,4},{13,5},{16,24},{17,25... | collective-permute-start | bytes 589832 | tf_op jit(solution)/shard_map/ppermute | solution.py:340
  581.7 8.6 %collective-permute-start.25 = (bf16[2,64,768]{2,1,0:T(8,128)(2,1)S(1)}, bf16[2,64,768]{2,1,0:T(8,128)(2,1)S(1)}, u32[]{:S(2)}, u32[]{:S(2)}) collective-permute-start(bf16[2,64,768]{2,1,0:T(8,128)(2,1)S(1)} %dynamic-slice_bitcast_fusion.6), channel_id=1, source_target_pairs={{0,8},{1,9},{4,12},{5,13},{8,0},{9,1},{12,4},{13,5},{16,24},{17,25... | collective-permute-start | bytes 589832 | tf_op jit(solution)/shard_map/ppermute | solution.py:340
  586.7 8.2 %collective-permute-start.22 = (bf16[1,64,768]{2,1,0:T(8,128)(2,1)S(1)}, bf16[1,64,768]{2,1,0:T(8,128)(2,1)S(1)}, u32[]{:S(2)}, u32[]{:S(2)}) collective-permute-start(bf16[1,64,768]{2,1,0:T(8,128)(2,1)S(1)} %constant_dynamic-slice_fusion.2), channel_id=1, source_target_pairs={{0,16},{1,17},{4,20},{5,21},{8,24},{9,25},{12,28},{13,29},{16,0},{... | collective-permute-start | bytes 294920 | tf_op jit(solution)/shard_map/ppermute | solution.py:340
  590.4 15.3 %collective-permute-start.26 = (bf16[1,64,768]{2,1,0:T(8,128)(2,1)S(1)}, bf16[1,64,768]{2,1,0:T(8,128)(2,1)S(1)}, u32[]{:S(2)}, u32[]{:S(2)}) collective-permute-start(bf16[1,64,768]{2,1,0:T(8,128)(2,1)S(1)} %constant_dynamic-slice_fusion.1), channel_id=1, source_target_pairs={{0,16},{1,17},{4,20},{5,21},{8,24},{9,25},{12,28},{13,29},{16,0},{... | collective-permute-start | bytes 294920 | tf_op jit(solution)/shard_map/ppermute | solution.py:340
  594.9 5.9 copy-start.16
  603.4 44.6 %collective-permute-start.18 = (bf16[1024,1024]{1,0:T(8,128)(2,1)}, bf16[1024,1024]{1,0:T(8,128)(2,1)S(1)}, u32[]{:S(2)}, u32[]{:S(2)}) collective-permute-start(bf16[1024,1024]{1,0:T(8,128)(2,1)} %fusion.11), channel_id=1, source_target_pairs={{0,0},{1,2},{2,1},{3,3},{4,4},{5,6},{6,5},{7,7},{8,8},{9,10},{10,9... | collective-permute-start | bytes 6291464 | tf_op jit(solution)/shard_map/ppermute | solution.py:318
  605.7 22.4 %collective-permute-start.35 = (f32[5128]{0:T(1024)S(1)}, f32[5128]{0:T(1024)S(1)}, u32[]{:S(2)}, u32[]{:S(2)}) collective-permute-start(f32[5128]{0:T(1024)S(1)} %constant_dynamic-update-slice_fusion), channel_id=1, source_target_pairs={{0,1},{1,0},{4,5},{5,4},{8,9},{9,8},{12,13},{13,12},{16,17},{17,16... | collective-permute-start | bytes 61544 | tf_op jit(solution)/shard_map/ppermute | solution.py:350
  605.8 36.4 %collective-permute-start.27 = (bf16[64,1536]{1,0:T(8,128)(2,1)S(1)}, bf16[64,1536]{1,0:T(8,128)(2,1)S(1)}, u32[]{:S(2)}, u32[]{:S(2)}) collective-permute-start(bf16[64,1536]{1,0:T(8,128)(2,1)S(1)} %pad_maximum_fusion), channel_id=1, source_target_pairs={{0,0},{1,2},{2,1},{3,3},{4,4},{5,6},{6,5},{7,7},{8,8},{9,10},{10,9... | collective-permute-start | bytes 589832 | tf_op jit(solution)/shard_map/ppermute | solution.py:318
  628.1 3.8 collective-permute-start.36
  628.8 12.8 %collective-permute-start.32 = (bf16[32,1024]{1,0:T(8,128)(2,1)S(1)}, bf16[32,1024]{1,0:T(8,128)(2,1)S(1)}, u32[]{:S(2)}, u32[]{:S(2)}) collective-permute-start(bf16[32,1024]{1,0:T(8,128)(2,1)S(1)} %fusion.38), channel_id=1, source_target_pairs={{0,0},{1,2},{2,1},{3,3},{4,4},{5,6},{6,5},{7,7},{8,8},{9,10},{10,9... | collective-permute-start | bytes 196616 | tf_op jit(solution)/shard_map/ppermute | solution.py:318
  631.9 4.2 collective-permute-start.37
  636.1 5.4 collective-permute-start.38
  641.6 1.5 collective-permute-start.39
  644.2 3.8 collective-permute-start.34
  645.8 3.0 collective-permute-start.33
  (16 other events, 34.8 us)
Sparse Core Ops, SparseCore 0:
  11.2 80.9 all-gather.4
  95.6 53.5 all-gather.6
  152.6 78.0 all-gather.8
  233.8 74.1 all-gather.10
  340.3 93.9 reduce-scatter.4
  436.5 131.2 reduce-scatter.2
